TPU v7x, 128 devices: a whole 4x4x4 slice. The times are simulated.
128 devices in a mesh: gx: 4 (over y), gy: 32 (over x, z, core).
Axes of the slice: x: 4, y: 4, z: 4, core: 2. Of those that a mesh axis runs over, the one named last changes fastest.
Arguments:
- a_blocks: bfloat16 [8192, 8, 9216], P(('gx', 'gy')), may hold values from -2 to 2
- a_cols: int32 [8192, 8], P(('gx', 'gy')), may hold values from 0 to 63
- q_blocks: bfloat16 [8192, 9216], P(('gx', 'gy')), may hold values from -0.625 to 0.625
- part_of: int32 [8192, 8], P(('gx', 'gy')), may hold values from 0 to 63
- part_dest: int32 [8192, 1], P(('gx', 'gy')), may hold values from 0 to 31; in each aligned block of 64 rows (0 to 63, 64 to 127, ...) at most 4 rows name the same one
- part_pos: int32 [8192], P(('gx', 'gy')), may hold values from 0 to 15
- g_level: float32 [3, 9216], replicated, may hold values from -0.625 to 0.625
Outputs:
- coarse_first: float32 [256, 8, 9216], P(('gx', 'gy'))
- coarsest: float32 [256, 8, 9216], P(('gx', 'gy'))
Inputs may be any that keep to these rules, and one draw needn't show every extreme that they name: `part_dest`: among the partial blocks of one device at most 4 name the same gy index, and some device's blocks name one index exactly 4 times.
All inputs are finite; a program needn't handle non-finite values.
Results may differ from a plain program's by a relative error of at most 0.0029.
Values sent between devices are 32-bit elements; how exact they have to be, the bound alone decides.
No kernel may reach another device: no remote copies, remote signals or barrier semaphores. Data moves between devices by JAX's collectives and lax.ppermute only.
A program may use at most 128 MiB of HBM per device.

v0:
```python
import jax
import jax.numpy as jnp
from jax import lax
from jax.sharding import PartitionSpec as P

B = 96
KA = 8
RC = 2
SC = 8
NP = 64


def partner_2(shard, axis, stride):
    return lax.ppermute(shard, axis, [(i, i ^ 1 << stride) for i in range(lax.axis_size(axis))])


def project(blocks, gmat):
    shaped = blocks.reshape(blocks.shape[0], B, B)
    right = jnp.einsum("mab,bj->maj", shaped, gmat, precision=lax.Precision.HIGHEST)
    result = jnp.einsum("ai,maj->mij", gmat, right, precision=lax.Precision.HIGHEST)
    return result.reshape(blocks.shape[0], B * B)


def select_sum(labels, count, values):
    table = (jnp.arange(count, dtype=jnp.int32)[:, None] == labels[None, :]).astype(jnp.float32)
    return jnp.dot(table, values, precision=lax.Precision.HIGHEST)


def local(a_blocks, a_cols, q_blocks, part_of, part_dest, part_pos, g_level):
    rows = a_blocks.shape[0]
    width = B * B
    cells = RC * SC
    n_inner = lax.axis_size("gy")
    capacity = 2 * NP // n_inner
    qmats = q_blocks.reshape(rows, B, B)
    picked = q_blocks[a_cols.reshape(-1)].reshape(rows, KA, B, B)
    aq_rows = jnp.einsum(
        "rkij,rkjl->rkil",
        a_blocks.reshape(rows, KA, B, B),
        picked,
        preferred_element_type=jnp.float32,
    ).astype(jnp.bfloat16)
    terms = jnp.einsum("rji,rkjl->rkil", qmats, aq_rows, preferred_element_type=jnp.float32)
    partial_value = select_sum(part_of.reshape(-1), NP, terms.reshape(rows * KA, width))
    target = part_dest[:, 0]
    onehot = (target[:, None] == jnp.arange(n_inner, dtype=jnp.int32)[None, :]).astype(jnp.int32)
    before = jnp.cumsum(onehot, axis=0) - onehot
    ranks = jnp.sum(before * onehot, axis=1)
    slots = target * capacity + ranks
    buffer = select_sum(slots, n_inner * capacity, partial_value).reshape(n_inner, capacity, width)
    slot_table = (
        jnp.arange(n_inner * capacity, dtype=jnp.int32)[:, None] == slots[None, :]
    ).astype(jnp.int32)
    where = jnp.sum(slot_table * (part_pos - cells)[None, :], axis=1) + cells
    where = where.reshape(n_inner, capacity)
    received, spots = (
        lax.all_to_all(buffer, "gy", split_axis=0, concat_axis=0, tiled=True),
        lax.all_to_all(where, "gy", split_axis=0, concat_axis=0, tiled=True),
    )
    coarse = select_sum(spots.reshape(-1), cells, received.reshape(-1, width))
    gmats = g_level.reshape(3, B, B)
    merged = coarse
    for level_bit in range(2):
        partner = partner_2(merged, "gy", level_bit)
        merged = project(merged + partner, gmats[level_bit])
    merged = lax.psum(merged, "gx")
    merged = project(merged, gmats[2])
    return (coarse.reshape(RC, SC, width), merged.reshape(RC, SC, width))


def solution(mesh):
    placed = (
        P(("gx", "gy"), None, None),
        P(("gx", "gy"), None),
        P(("gx", "gy"), None),
        P(("gx", "gy"), None),
        P(("gx", "gy"), None),
        P(("gx", "gy")),
        P(),
    )
    return jax.shard_map(
        local,
        mesh=mesh,
        in_specs=placed,
        out_specs=(P(("gx", "gy"), None, None), P(("gx", "gy"), None, None)),
        check_vma=False,
    )
```

profile of v0, /device:TPU:1, one launch (start us, length us, event | category | flops | bytes accessed | tf_op | source)
XLA Modules:
  0.0 318.0 jit_solution(4454564428661975025)
XLA Ops:
  10.4 9.4 %all-to-all-start = ((s32[32,1,4]{2,1,0:T(1,128)}), s32[32,1,4]{2,1,0:T(1,128)S(1)}, u32[]{:S(2)}, u32[]{:S(2)}) async-start(s32[32,1,4]{2,1,0:T(1,128)} %bitcast.1), calls=%async_computation | async-start | bytes 32768 | tf_op jit(solution)/shard_map/all_to_all | solution.py:58
  20.8 2.6 reshape.128
  23.4 8.7 %gather_fusion = bf16[512,9216]{1,0:T(8,128)(2,1)} fusion(bf16[64,9216]{1,0:T(8,128)(2,1)S(1)} %copy-done, s32[1024]{0:T(1024)S(1)} %pad_clamp_fusion), kind=kCustom, calls=%fused_computation | custom fusion | bytes 18876416 | tf_op jit(solution)/shard_map/gather | solution.py:36
  32.1 18.7 %reshape.107 = bf16[64,8,96,96]{3,2,1,0:T(8,128)(2,1)} reshape(bf16[512,9216]{1,0:T(8,128)(2,1)} %gather_fusion) | data formatting | bytes 18874368 | tf_op jit(solution)/shard_map/reshape | solution.py:36
  50.7 18.6 %reshape.108 = bf16[64,8,96,96]{3,2,1,0:T(8,128)(2,1)} reshape(bf16[64,8,9216]{2,1,0:T(8,128)(2,1)} %param.7) | data formatting | bytes 18874368 | tf_op jit(solution)/shard_map/reshape | solution.py:39
  69.4 22.4 %fusion.5 = f32[64,8,96,96]{2,3,1,0:T(8,128)} fusion(bf16[64,8,96,96]{3,2,1,0:T(8,128)(2,1)} %reshape.107, bf16[64,8,96,96]{3,2,1,0:T(8,128)(2,1)} %reshape.108, bf16[64,96,96,1]{2,1,0,3:T(8,128)(2,1)S(1)} %reshape.128), kind=kOutput, calls=%fused_computation.5 | convolution fusion | flops 1816657920 | bytes 38928384 | tf_op jit(solution)/shard_map/rji,rkjl->rkil/dot_general | solution.py:43
  91.8 24.7 %copy.29 = f32[64,8,96,96]{3,2,1,0:T(8,128)} copy(f32[64,8,96,96]{2,3,1,0:T(8,128)} %fusion.5) | data formatting | bytes 37748736 | tf_op jit(solution)/shard_map/rji,rkjl->rkil/transpose | solution.py:43
  116.5 24.4 %reshape.110 = f32[512,9216]{1,0:T(8,128)} reshape(f32[64,8,96,96]{3,2,1,0:T(8,128)} %copy.29) | data formatting | bytes 37748736 | tf_op jit(solution)/shard_map/reshape | solution.py:44
  141.0 11.5 %fusion.9 = f32[64,9216]{1,0:T(8,128)S(1)} fusion(f32[512,9216]{1,0:T(8,128)} %reshape.110, s32[512]{0:T(512)S(1)} %eq.74), kind=kOutput, calls=%fused_computation.11 | convolution fusion | flops 3623911424 | bytes 21235712 | tf_op jit(solution)/shard_map/dot_general | solution.py:26
  152.5 4.3 %fusion.12 = f32[128,9216]{1,0:T(8,128)} fusion(f32[64,9216]{1,0:T(8,128)S(1)} %fusion.9, s32[64]{0:T(128)S(1)} %get-tuple-element.5), kind=kOutput, calls=%fused_computation.21 | convolution fusion | flops 905977856 | bytes 7078144 | tf_op jit(solution)/shard_map/dot_general | solution.py:26
  156.8 5.6 %reshape.111 = f32[32,4,9216]{2,1,0:T(4,128)} reshape(f32[128,9216]{1,0:T(8,128)} %fusion.12) | data formatting | bytes 9437184 | tf_op jit(solution)/shard_map/reshape | solution.py:50
  162.4 7.4 %all-to-all-start.1 = ((f32[32,4,9216]{2,1,0:T(4,128)}), f32[32,4,9216]{2,1,0:T(4,128)}, u32[]{:S(2)}, u32[]{:S(2)}) async-start(f32[32,4,9216]{2,1,0:T(4,128)} %reshape.111), calls=%async_computation.1 | async-start | bytes 9437184 | tf_op jit(solution)/shard_map/all_to_all | solution.py:57
  171.2 56.9 %all-to-all-done.1 = f32[32,4,9216]{2,1,0:T(4,128)} async-done(((f32[32,4,9216]{2,1,0:T(4,128)}), f32[32,4,9216]{2,1,0:T(4,128)}, u32[]{:S(2)}, u32[]{:S(2)}) %all-to-all-start.1) | async-done | bytes 4718624 | tf_op jit(solution)/shard_map/all_to_all | solution.py:57
  228.1 5.7 %reshape.112 = f32[128,9216]{1,0:T(8,128)} reshape(f32[32,4,9216]{2,1,0:T(4,128)} %all-to-all-done.1) | data formatting | bytes 9437184 | tf_op jit(solution)/shard_map/reshape | solution.py:60
  233.8 4.0 %fusion.14 = f32[16,9216]{1,0:T(8,128)S(1)} fusion(f32[128,9216]{1,0:T(8,128)} %reshape.112, s32[128]{0:T(128)S(1)} %eq.70), kind=kOutput, calls=%fused_computation.25 | convolution fusion | flops 226494464 | bytes 5308928 | tf_op jit(solution)/shard_map/dot_general | solution.py:26
  239.1 1.3 collective-permute-done
  240.7 1.8 fusion.16
  244.0 4.7 %collective-permute-start.1 = (f32[16,9216]{1,0:T(8,128)S(1)}, f32[16,9216]{1,0:T(8,128)S(1)}, u32[]{:S(2)}, u32[]{:S(2)}) collective-permute-start(f32[16,9216]{1,0:T(8,128)S(1)} %reshape.115), channel_id=1, source_target_pairs={{0,2},{1,3},{2,0},{3,1},{4,6},{5,7},{6,4},{7,5},{8,10},{9,11},{10,... | collective-permute-start | bytes 1769480 | tf_op jit(solution)/shard_map/ppermute | solution.py:14
  248.7 13.3 %collective-permute-done.1 = f32[16,9216]{1,0:T(8,128)S(1)} collective-permute-done((f32[16,9216]{1,0:T(8,128)S(1)}, f32[16,9216]{1,0:T(8,128)S(1)}, u32[]{:S(2)}, u32[]{:S(2)}) %collective-permute-start.1) | collective-permute-done | bytes 589856 | tf_op jit(solution)/shard_map/ppermute | solution.py:14
  262.4 1.8 fusion.17
  264.2 1.7 convolution_bitcast_fusion.1
  266.0 41.0 %all-reduce.2.cloned.1.call-done = f32[16,96,96]{1,2,0:T(8,128)} async-done(((f32[16,96,96]{1,2,0:T(8,128)}), f32[16,96,96]{1,2,0:T(8,128)}) %all-reduce.2.cloned.1.call-update) | async-done | bytes 589840 | tf_op jit(solution)/shard_map/psum | solution.py:66
  307.0 2.0 fusion.18
  310.0 1.2 reshape_reshape.3
  (41 shorter events, 10.2 us)
Async XLA Ops:
  7.2 16.2 %copy-start = (bf16[64,9216]{1,0:T(8,128)(2,1)S(1)}, bf16[64,9216]{1,0:T(8,128)(2,1)}, u32[]{:S(2)}) copy-start(bf16[64,9216]{1,0:T(8,128)(2,1)} %param.9) | copy-start | bytes 3538948
  10.4 151.9 %all-to-all-start = ((s32[32,1,4]{2,1,0:T(1,128)}), s32[32,1,4]{2,1,0:T(1,128)S(1)}, u32[]{:S(2)}, u32[]{:S(2)}) async-start(s32[32,1,4]{2,1,0:T(1,128)} %bitcast.1), calls=%async_computation | async-start | bytes 32768 | tf_op jit(solution)/shard_map/all_to_all | solution.py:58
  116.5 24.4 %copy-start.3 = (s32[64,8]{0,1:T(8,128)S(1)}, s32[64,8]{0,1:T(8,128)}, u32[]{:S(2)}) copy-start(s32[64,8]{0,1:T(8,128)} %param.10) | copy-start | bytes 6148
  162.4 65.7 %all-to-all-start.1 = ((f32[32,4,9216]{2,1,0:T(4,128)}), f32[32,4,9216]{2,1,0:T(4,128)}, u32[]{:S(2)}, u32[]{:S(2)}) async-start(f32[32,4,9216]{2,1,0:T(4,128)} %reshape.111), calls=%async_computation.1 | async-start | bytes 9437184 | tf_op jit(solution)/shard_map/all_to_all | solution.py:57
  169.8 68.9 %copy-start.2 = (f32[3,9216]{1,0:T(4,128)S(1)}, f32[3,9216]{1,0:T(4,128)}, u32[]{:S(2)}) copy-start(f32[3,9216]{1,0:T(4,128)} %param.13) | copy-start | bytes 331780
  169.8 137.1 %all-reduce.2.cloned.1.call-start = ((), (), s32[]{:S(2)}) async-start(), calls=%async_computation.2 | async-start | bytes 1572864 | tf_op jit(solution)/shard_map/psum | solution.py:66
  237.8 71.9 %copy-start.1 = (f32[16,9216]{1,0:T(8,128)}, f32[16,9216]{1,0:T(8,128)S(1)}, u32[]{:S(2)}) copy-start(f32[16,9216]{1,0:T(8,128)S(1)} %fusion.14) | copy-start | bytes 1769476
  237.8 2.5 collective-permute-start
  244.0 18.0 %collective-permute-start.1 = (f32[16,9216]{1,0:T(8,128)S(1)}, f32[16,9216]{1,0:T(8,128)S(1)}, u32[]{:S(2)}, u32[]{:S(2)}) collective-permute-start(f32[16,9216]{1,0:T(8,128)S(1)} %reshape.115), channel_id=1, source_target_pairs={{0,2},{1,3},{2,0},{3,1},{4,6},{5,7},{6,4},{7,5},{8,10},{9,11},{10,... | collective-permute-start | bytes 1769480 | tf_op jit(solution)/shard_map/ppermute | solution.py:14
Sparse Core Ops, SparseCore 0:
  266.0 40.8 all-reduce.1
where the time goes:
time: 321 us; the launch traced here: 318 us
  local copies, waits for them, and re-layouts  115 us (36%)
  waiting for transfers between devices  112 us (35%)
  matrix products  51 us (16%)
  starting transfers between devices  22.4 us (7%)
  between operations  14.2 us (4%)
  other arithmetic  3.37 us (1%)
    all_to_all x1, waiting for transfers between devices, local(): lax.all_to_all(buffer, 'gy', split_axis=0, concat_axis=0, tiled=True)  56.9 us
    psum x1, waiting for transfers between devices, local(): merged = lax.psum(merged, 'gx')  41 us
    transpose x1, local copies, waits for them, and re-layouts, local(): jnp.einsum('rji,rkjl->rkil', qmats, aq_rows, preferred_element_type=jnp.f...  24.7 us
    reshape x1, local copies, waits for them, and re-layouts, local(): terms.reshape(rows * KA, width)  24.4 us
    dot_general x1, matrix products, local(): jnp.einsum('rji,rkjl->rkil', qmats, aq_rows, preferred_element_type=jnp.f...  22.4 us
    dot_general x3, matrix products, select_sum(): return jnp.dot(table, values, precision=lax.Precision.HIGHEST)  19.7 us
    reshape x2, local copies, waits for them, and re-layouts, local(): picked = q_blocks[a_cols.reshape(-1)].reshape(rows, KA, B, B)  18.8 us
    reshape x1, local copies, waits for them, and re-layouts, local(): a_blocks.reshape(rows, KA, B, B)  18.6 us
  transfers between devices with their start and end apart: 5, of which 4 were waited for; matrix products, arithmetic and copies ran while one was open for 45% of the time, Pallas kernels for 0%

commit v1 on v0

v1 whole, which is shorter than its diff:
```python
import functools
import jax
import jax.numpy as jnp
from jax import lax
from jax.experimental import pallas as pl
from jax.experimental.pallas import tpu as pltpu
from jax.sharding import PartitionSpec as P

B = 96
L = 128
R = 64
KA = 8
RC = 2
SC = 8
NP = 64
CELLS = RC * SC
WIDTH = B * B
GY = 32
GX = 4
PER = B // GY
TILES = 18
ROWS_STEP = 4


def lane_iota(rows):
    return lax.broadcasted_iota(jnp.int32, (rows, L), 1)


def unpack_rows(t0, t1, t2):
    lane = lane_iota(t0.shape[0])
    r1 = jnp.where(lane < 32, pltpu.roll(t0, 32, 1), pltpu.roll(t1, 32, 1))
    r2 = jnp.where(lane < 64, pltpu.roll(t1, 64, 1), pltpu.roll(t2, 64, 1))
    return t0, r1, r2, pltpu.roll(t2, 96, 1)


def pack_rows(v0, v1, v2, v3):
    lane = lane_iota(v0.shape[0])
    s1 = pltpu.roll(v1, 96, 1)
    s2 = pltpu.roll(v2, 64, 1)
    s3 = pltpu.roll(v3, 32, 1)
    return jnp.where(lane < 96, v0, s1), jnp.where(lane < 64, s1, s2), jnp.where(lane < 32, s2, s3)


def fine_kernel(cols, part, dest, pos, me, a_ref, q_ref, x_ref, s_ref, q_mat, q_tr, acc):
    step = pl.program_id(0)

    @pl.when(step == 0)
    def _():
        acc[...] = jnp.zeros_like(acc)
        q_mat[...] = jnp.zeros_like(q_mat)
        low = lane_iota(B) < B
        for g in range(R // 16):
            for j in range(B // 4):
                at = [q_ref[16 * g:16 * g + 16, 384 * j + L * u:384 * j + L * (u + 1)].astype(jnp.float32) for u in range(3)]
                for h in range(2):
                    rows = unpack_rows(*[piece[8 * h:8 * h + 8] for piece in at])
                    for v in range(4):
                        s_ref[h, pl.ds(4 * j + v, 8, stride=B), :] = rows[v]

            def one(k, carry):
                mat = jnp.where(low, s_ref[k // 8, pl.ds(pl.multiple_of((k % 8) * B, 8), B), :], 0.0)
                q_mat[16 * g + k, 0:B, :] = mat.astype(jnp.bfloat16)
                q_tr[16 * g + k] = mat.T[0:B].astype(jnp.bfloat16)
                return carry

            lax.fori_loop(0, 16, one, 0)

    def relayout(ii, slot):
        for j in range(B // 4):
            at = [a_ref[ii, :, 384 * j + L * u:384 * j + L * (u + 1)].astype(jnp.float32) for u in range(3)]
            rows = unpack_rows(*at)
            for v in range(4):
                s_ref[slot, pl.ds(4 * j + v, 8, stride=B), :] = rows[v]

    def multiply(ii, slot):
        i = step * ROWS_STEP + ii
        left = q_tr[i]
        for k in range(0, KA, 2):
            aq = []
            for kk in (k, k + 1):
                mat = s_ref[slot, kk * B:(kk + 1) * B, :].astype(jnp.bfloat16)
                aq.append(jnp.dot(mat, q_mat[cols[i, kk]], preferred_element_type=jnp.float32).astype(jnp.bfloat16))
            term = jnp.dot(left, jnp.concatenate(aq, axis=1), preferred_element_type=jnp.float32)
            for n, kk in enumerate((k, k + 1)):
                p = part[i, kk]
                at = pl.ds(pl.multiple_of(p * B, 8), B)
                acc[at, :] = acc[at, :] + term[:, L * n:L * (n + 1)]

    relayout(0, 0)
    for ii in range(ROWS_STEP):
        if ii + 1 < ROWS_STEP:
            relayout(ii + 1, (ii + 1) % 2)
        multiply(ii, ii % 2)

    @pl.when(step == pl.num_programs(0) - 1)
    def _():
        row = lax.broadcasted_iota(jnp.int32, (8, L), 0)
        lane = lane_iota(8)
        base = (me[0] % 8) * 16
        codes = jnp.zeros((8, L), jnp.float32)
        for p in range(NP):
            code = (dest[p, 0] * CELLS + pos[p]).astype(jnp.float32)
            codes = jnp.where((row == p % 4) & (lane == base + p // 4), code, codes)

        def one(w, carry):
            for a in range(PER):
                rows = [acc[pl.ds(v * B + w * PER + a, 16, stride=4 * B), :] for v in range(4)]
                for u, piece in enumerate(pack_rows(*rows)):
                    for h in range(2):
                        x_ref[w, (2 * a + h) * 3 + u] = piece[8 * h:8 * h + 8]
            x_ref[w, TILES] = codes
            return carry

        lax.fori_loop(0, GY, one, 0)


def fine(a_blocks, a_cols, q_blocks, part_of, part_dest, part_pos, me):
    return pl.pallas_call(
        fine_kernel,
        out_shape=jax.ShapeDtypeStruct((GY, TILES + 1, 8, L), jnp.float32),
        grid_spec=pltpu.PrefetchScalarGridSpec(
            num_scalar_prefetch=5,
            grid=(R // ROWS_STEP,),
            in_specs=[
                pl.BlockSpec((ROWS_STEP, KA, WIDTH), lambda g, *_: (g, 0, 0)),
                pl.BlockSpec((R, WIDTH), lambda g, *_: (0, 0)),
            ],
            out_specs=pl.BlockSpec((GY, TILES + 1, 8, L), lambda g, *_: (0, 0, 0, 0)),
            scratch_shapes=[
                pltpu.VMEM((2, KA * B, L), jnp.float32),
                pltpu.VMEM((R, L, L), jnp.bfloat16),
                pltpu.VMEM((R, B, B), jnp.bfloat16),
                pltpu.VMEM((NP * B, L), jnp.float32),
            ],
        ),
        name="fine",
    )(a_cols, part_of, part_dest, part_pos, me, a_blocks, q_blocks)


def split2(x):
    hi = x.astype(jnp.bfloat16)
    return hi, (x - hi.astype(jnp.float32)).astype(jnp.bfloat16)


def cells_kernel(y_ref, z_ref, t_ref, hi_ref, lo_ref):
    def one(s, carry):
        for a in range(PER):
            halves = [unpack_rows(*[y_ref[s, (2 * a + h) * 3 + u] for u in range(3)]) for h in range(2)]
            for v in range(4):
                hi, lo = split2(jnp.concatenate([halves[0][v], halves[1][v]], axis=0))
                at = pl.ds(pl.multiple_of(v * 512 + s * 16, 16), 16)
                hi_ref[at, L * a:L * (a + 1)] = hi
                lo_ref[at, L * a:L * (a + 1)] = lo
        return carry

    lax.fori_loop(0, GY, one, 0)
    tiles = [functools.reduce(jnp.add, [y_ref[8 * o + s, TILES] for s in range(8)]) for o in range(4)]
    codes = jnp.concatenate([tiles[o][v:v + 1] for v in range(4) for o in range(4)], axis=1)

    def chunk(c, carry):
        want = (lax.broadcasted_iota(jnp.int32, (L, 1), 0) + c * L).astype(jnp.float32)
        table = jnp.where(want == codes, 1.0, 0.0).astype(jnp.bfloat16)
        sums = jnp.dot(table, hi_ref[...], preferred_element_type=jnp.float32)
        sums = sums + jnp.dot(table, lo_ref[...], preferred_element_type=jnp.float32)
        for a in range(PER):
            at = sums[:, L * a:L * (a + 1)].reshape(8, 2, 8, L)
            z_ref[pl.ds(c * 8, 8), 2 * a:2 * a + 2] = at
            t_ref[pl.ds(c * 2, 2), 2 * a:2 * a + 2] = at.reshape(2, 4, 2, 8, L).sum(1)
        return carry

    lax.fori_loop(0, 4, chunk, 0)


def cells_of(received):
    return pl.pallas_call(
        cells_kernel,
        out_shape=(
            jax.ShapeDtypeStruct((GY, 2 * PER, 8, L), jnp.float32),
            jax.ShapeDtypeStruct((GY // 4, 2 * PER, 8, L), jnp.float32),
        ),
        scratch_shapes=[pltpu.VMEM((4 * 512, PER * L), jnp.bfloat16)] * 2,
        name="cells",
    )(received)


def close_kernel(w_ref, h_ref, ht_ref, first_ref, last_ref, r_ref, o_ref):
    def rows_of(tile):
        for j in range(B // 4):
            for half in range(RC):
                yield j, half, [tile(4 * j + v, half) for v in range(4)]

    for j, half, rows in rows_of(lambda r, half: w_ref[r // PER, 2 * (r % PER) + half]):
        for u, piece in enumerate(pack_rows(*rows)):
            first_ref[half, :, 384 * j + L * u:384 * j + L * (u + 1)] = piece
    total = w_ref[:, 2 * PER:4 * PER].reshape(B * CELLS, L)
    r_ref[...] = jnp.dot(total, h_ref[...], precision=lax.Precision.HIGHEST, preferred_element_type=jnp.float32)
    for c in range(0, CELLS, 2):
        pair = jnp.concatenate([r_ref[pl.ds(c + n, B, stride=CELLS), :] for n in range(2)], axis=1)
        out = jnp.dot(ht_ref[...], pair, precision=lax.Precision.HIGHEST, preferred_element_type=jnp.float32)
        for n in range(2):
            o_ref[pl.ds(c + n, B, stride=CELLS), :] = out[:, L * n:L * (n + 1)]
    for j, half, rows in rows_of(lambda r, half: o_ref[r * CELLS + 8 * half:r * CELLS + 8 * half + 8, :]):
        for u, piece in enumerate(pack_rows(*rows)):
            last_ref[half, :, 384 * j + L * u:384 * j + L * (u + 1)] = piece


def close(received, h, ht):
    out = jax.ShapeDtypeStruct((RC, SC, WIDTH), jnp.float32)
    return pl.pallas_call(
        close_kernel,
        out_shape=(out, out),
        scratch_shapes=[pltpu.VMEM((B * CELLS, L), jnp.float32)] * 2,
        name="close",
    )(received, h, ht)


def local(a_blocks, a_cols, q_blocks, part_of, part_dest, part_pos, g_level):
    me = lax.axis_index("gy").astype(jnp.int32).reshape(1)
    g = g_level.reshape(3, B, B)
    mm = functools.partial(jnp.dot, precision=lax.Precision.HIGHEST)
    h = mm(mm(g[0], g[1]), g[2])
    slices = fine(a_blocks, a_cols, q_blocks, part_of, part_dest, part_pos, me)
    gathered = lax.all_to_all(slices, "gy", split_axis=0, concat_axis=0, tiled=True)
    mine, group = cells_of(gathered)
    others = [lax.ppermute(group, "gx", [(i, (i + d) % GX) for i in range(GX)]) for d in range(1, GX)]
    total = group + others[0] + others[1] + others[2]
    total = jnp.broadcast_to(total[:, None], (GY // 4, 4) + total.shape[1:]).reshape(mine.shape)
    back = lax.all_to_all(jnp.concatenate([mine, total], axis=1), "gy", split_axis=0, concat_axis=0, tiled=True)
    return close(back, jnp.pad(h, ((0, L - B), (0, L - B))), h.T)


def solution(mesh):
    placed = (
        P(("gx", "gy"), None, None),
        P(("gx", "gy"), None),
        P(("gx", "gy"), None),
        P(("gx", "gy"), None),
        P(("gx", "gy"), None),
        P(("gx", "gy")),
        P(),
    )
    return jax.shard_map(
        local,
        mesh=mesh,
        in_specs=placed,
        out_specs=(P(("gx", "gy"), None, None), P(("gx", "gy"), None, None)),
        check_vma=False,
    )
```

time: 321 us -> 173 us (0.54)
  local copies, waits for them, and re-layouts: 115 us -> 7.17 us
  waiting for transfers between devices: 112 us -> 29 us
  Pallas kernels: 0 us -> 81.2 us
  matrix products: 51 us -> 0.37 us
  blocking collectives: 0 us -> 42.3 us
  between operations: 14.2 us -> 0.7 us
  starting transfers between devices: 22.4 us -> 9.53 us
    pallas_call x0 -> x3, Pallas kernels: none -> 81.2 us  [the longest x1 67.2 us: fine(): pl.pallas_call(fine_kernel, out_shape=jax.ShapeDtypeStruct((GY, TILES + 1...]
    reshape x10 -> x0, local copies, waits for them, and re-layouts: 76.7 us -> none  [the longest x1 24.4 us: local(): terms.reshape(rows * KA, width)]
    dot_general x10 -> x2, matrix products: 51 us -> 0.37 us  [local(): h = mm(mm(g[0], g[1]), g[2])]
    all_to_all x0 -> x1, blocking collectives: none -> 42.3 us  [local(): lax.all_to_all(slices, 'gy', split_axis=0, concat_axis=0, tiled=True)]
    psum x1 -> x0, waiting for transfers between devices: 41 us -> none  [local(): merged = lax.psum(merged, 'gx')]
    all_to_all x2 -> x1, waiting for transfers between devices: 56.9 us -> 20.5 us  [local(): lax.all_to_all(jnp.concatenate([mine, total], axis=1), 'gy', split_axis=0...]
    transpose x3 -> x0, local copies, waits for them, and re-layouts: 25.2 us -> none  [the longest x1 24.7 us: local(): jnp.einsum('rji,rkjl->rkil', qmats, aq_rows, preferred_element_type=jnp.f...]
    all_to_all x2 -> x1, starting transfers between devices: 16.8 us -> 4.54 us  [local(): lax.all_to_all(jnp.concatenate([mine, total], axis=1), 'gy', split_axis=0...]
  transfers between devices with their start and end apart: 5 -> 4, of which waited for: 4 -> 3; matrix products, arithmetic and copies ran while one was open for 45% -> 1% of each run, Pallas kernels for 0% -> 0%
where the time goes in v1:
time: 173 us
  Pallas kernels  81.2 us (47%)
  blocking collectives  42.3 us (24%)
  waiting for transfers between devices  29 us (17%)
  starting transfers between devices  9.53 us (6%)
  local copies, waits for them, and re-layouts  7.17 us (4%)
  other arithmetic  2.32 us (1%)
    pallas_call x1, Pallas kernels, fine(): pl.pallas_call(fine_kernel, out_shape=jax.ShapeDtypeStruct((GY, TILES + 1...  67.2 us
    all_to_all x1, blocking collectives, local(): lax.all_to_all(slices, 'gy', split_axis=0, concat_axis=0, tiled=True)  42.3 us
    all_to_all x1, waiting for transfers between devices, local(): lax.all_to_all(jnp.concatenate([mine, total], axis=1), 'gy', split_axis=0...  20.5 us
    pallas_call x1, Pallas kernels, cells_of(): pl.pallas_call(cells_kernel, out_shape=(jax.ShapeDtypeStruct((GY, 2 * PER...  8.82 us
    ppermute x3, waiting for transfers between devices, local(): lax.ppermute(group, 'gx', [(i, (i + d) % GX) for i in range(GX)])  8.43 us
    unnamed x9, local copies, waits for them, and re-layouts  5.28 us
    pallas_call x1, Pallas kernels, close(): pl.pallas_call(close_kernel, out_shape=(out, out), scratch_shapes=[pltpu....  5.18 us
    ppermute x3, starting transfers between devices, local(): lax.ppermute(group, 'gx', [(i, (i + d) % GX) for i in range(GX)])  4.99 us
  transfers between devices with their start and end apart: 4, of which 3 were waited for; matrix products, arithmetic and copies ran while one was open for 1% of the time, Pallas kernels for 0%

profile of v1, /device:TPU:1, one launch (start us, length us, event | category | flops | bytes accessed | tf_op | source)
XLA Modules:
  0.0 172.5 jit_solution(17735108852252220478)
XLA Ops:
  0.6 1.4 copy.10.part
  2.0 1.4 copy.11.dest
  3.4 1.4 copy.9.cols
  4.8 67.2 %fine.1 = f32[32,19,8,128]{3,2,1,0:T(8,128)} custom-call(s32[64,8]{1,0:T(8,128)} %copy.9.cols, s32[64,8]{1,0:T(8,128)} %copy.10.part, s32[64,1]{1,0:T(8,128)} %copy.11.dest, s32[64]{0:T(128)} %pos.1, s32[1]{0:T(128)} %bitcast.me, bf16[64,8,9216]{2,1,0:T(8,128)(2,1)} %a_ref.1, bf16[64,9216]{1,0:T(8,128)(2,1)} %q_ref.1), custom_call_target="tpu_custom_call" | custom-call | tf_op jit(solution)/shard_map/fine/pallas_call | solution.py:118
  72.0 42.3 %all_to_all.10.y_ref = f32[32,19,8,128]{3,2,1,0:T(8,128)} all-to-all(f32[32,19,8,128]{3,2,1,0:T(8,128)} %fine.1), channel_id=1, replica_groups=mesh['gx'=4,'gy'=32] {'gy'}, dimensions={0} | all-to-all | bytes 4980736 | tf_op jit(solution)/shard_map/all_to_all | solution.py:223
  114.2 8.8 %cells.1 = (f32[32,6,8,128]{3,2,1,0:T(8,128)}, f32[8,6,8,128]{3,2,1,0:T(8,128)}) custom-call(f32[32,19,8,128]{3,2,1,0:T(8,128)} %all_to_all.10.y_ref), custom_call_target="tpu_custom_call" | custom-call | tf_op jit(solution)/shard_map/cells/pallas_call | solution.py:175
  123.0 1.3 collective-permute-start
  124.3 2.6 %collective-permute-start.1 = (f32[8,6,8,128]{3,2,1,0:T(8,128)}, f32[8,6,8,128]{3,2,1,0:T(8,128)S(1)}, u32[]{:S(2)}, u32[]{:S(2)}) collective-permute-start(f32[8,6,8,128]{3,2,1,0:T(8,128)} %get-tuple-element.5), channel_id=1, source_target_pairs={{0,64},{32,96},{64,0},{96,32},{1,65},{33,97},{65,1},{97,33},{2,66}... | collective-permute-start | bytes 589832 | tf_op jit(solution)/shard_map/ppermute | solution.py:225
  127.0 1.1 collective-permute-start.2
  128.0 3.1 %collective-permute-done = f32[8,6,8,128]{3,2,1,0:T(8,128)S(1)} collective-permute-done((f32[8,6,8,128]{3,2,1,0:T(8,128)}, f32[8,6,8,128]{3,2,1,0:T(8,128)S(1)}, u32[]{:S(2)}, u32[]{:S(2)}) %collective-permute-start) | collective-permute-done | bytes 196640 | tf_op jit(solution)/shard_map/ppermute | solution.py:225
  131.1 5.3 %collective-permute-done.1 = f32[8,6,8,128]{3,2,1,0:T(8,128)S(1)} collective-permute-done((f32[8,6,8,128]{3,2,1,0:T(8,128)}, f32[8,6,8,128]{3,2,1,0:T(8,128)S(1)}, u32[]{:S(2)}, u32[]{:S(2)}) %collective-permute-start.1) | collective-permute-done | bytes 196640 | tf_op jit(solution)/shard_map/ppermute | solution.py:225
  136.5 1.0 add_add_fusion
  137.5 1.3 pad_maximum_fusion
  138.9 4.5 %all-to-all-start.1 = ((f32[32,12,8,128]{3,2,1,0:T(8,128)}), f32[32,12,8,128]{3,2,1,0:T(8,128)S(1)}, u32[]{:S(2)}, u32[]{:S(2)}) async-start(f32[32,12,8,128]{3,2,1,0:T(8,128)} %pad_maximum_fusion), calls=%async_computation.1 | async-start | bytes 3145728 | tf_op jit(solution)/shard_map/all_to_all | solution.py:228
  143.4 0.3 slice_reduce_fusion
  143.7 0.1 squeeze.10
  143.9 0.1 squeeze.11
  143.9 0.2 fusion
  144.1 0.2 fusion.1
  144.3 0.7 copy.12
  145.0 0.6 pad.4.h_ref
  145.6 20.5 %all-to-all-done.1.w_ref = f32[32,12,8,128]{3,2,1,0:T(8,128)S(1)} async-done(((f32[32,12,8,128]{3,2,1,0:T(8,128)}), f32[32,12,8,128]{3,2,1,0:T(8,128)S(1)}, u32[]{:S(2)}, u32[]{:S(2)}) %all-to-all-start.1) | async-done | bytes 1572896 | tf_op jit(solution)/shard_map/all_to_all | solution.py:228
  166.2 1.2 copy-done
  167.3 5.2 %close.1 = (f32[2,8,9216]{2,1,0:T(8,128)}, f32[2,8,9216]{2,1,0:T(8,128)}) custom-call(f32[32,12,8,128]{3,2,1,0:T(8,128)} %copy-done, f32[128,128]{1,0:T(8,128)} %pad.4.h_ref, f32[96,96]{1,0:T(8,128)} %bitcast.8), custom_call_target="tpu_custom_call" | custom-call | tf_op jit(solution)/shard_map/close/pallas_call | solution.py:209
  (8 shorter events, 0.1 us)
Async XLA Ops:
  123.0 14.5 %copy-start.1 = (f32[32,6,8,128]{3,2,1,0:T(8,128)S(1)}, f32[32,6,8,128]{3,2,1,0:T(8,128)}, u32[]{:S(2)}) copy-start(f32[32,6,8,128]{3,2,1,0:T(8,128)} %get-tuple-element.4) | copy-start | bytes 2359300
  123.0 8.1 %collective-permute-start = (f32[8,6,8,128]{3,2,1,0:T(8,128)}, f32[8,6,8,128]{3,2,1,0:T(8,128)S(1)}, u32[]{:S(2)}, u32[]{:S(2)}) collective-permute-start(f32[8,6,8,128]{3,2,1,0:T(8,128)} %get-tuple-element.5), channel_id=1, source_target_pairs={{0,32},{32,64},{64,96},{96,0},{1,33},{33,65},{65,97},{97,1},{2,34}... | collective-permute-start | bytes 589832 | tf_op jit(solution)/shard_map/ppermute | solution.py:225
  124.3 12.1 %collective-permute-start.1 = (f32[8,6,8,128]{3,2,1,0:T(8,128)}, f32[8,6,8,128]{3,2,1,0:T(8,128)S(1)}, u32[]{:S(2)}, u32[]{:S(2)}) collective-permute-start(f32[8,6,8,128]{3,2,1,0:T(8,128)} %get-tuple-element.5), channel_id=1, source_target_pairs={{0,64},{32,96},{64,0},{96,32},{1,65},{33,97},{65,1},{97,33},{2,66}... | collective-permute-start | bytes 589832 | tf_op jit(solution)/shard_map/ppermute | solution.py:225
  127.0 9.5 %collective-permute-start.2 = (f32[8,6,8,128]{3,2,1,0:T(8,128)}, f32[8,6,8,128]{3,2,1,0:T(8,128)S(1)}, u32[]{:S(2)}, u32[]{:S(2)}) collective-permute-start(f32[8,6,8,128]{3,2,1,0:T(8,128)} %get-tuple-element.5), channel_id=1, source_target_pairs={{0,96},{32,0},{64,32},{96,64},{1,97},{33,1},{65,33},{97,65},{2,98}... | collective-permute-start | bytes 589832 | tf_op jit(solution)/shard_map/ppermute | solution.py:225
  138.9 4.6 %copy-start.2 = (f32[3,9216]{1,0:T(4,128)S(1)}, f32[3,9216]{1,0:T(4,128)}, u32[]{:S(2)}) copy-start(f32[3,9216]{1,0:T(4,128)} %param.13) | copy-start | bytes 331780
  138.9 27.3 %all-to-all-start.1 = ((f32[32,12,8,128]{3,2,1,0:T(8,128)}), f32[32,12,8,128]{3,2,1,0:T(8,128)S(1)}, u32[]{:S(2)}, u32[]{:S(2)}) async-start(f32[32,12,8,128]{3,2,1,0:T(8,128)} %pad_maximum_fusion), calls=%async_computation.1 | async-start | bytes 3145728 | tf_op jit(solution)/shard_map/all_to_all | solution.py:228
  166.2 1.2 copy-start

commit v2 on v1

--- a/solution.py
+++ b/solution.py
@@ -19,7 +19,10 @@
 GX = 4
 PER = B // GY
 TILES = 18
-ROWS_STEP = 4
+ROWS_STEP = 8
+SKEW = 4
+STRIDE = 100
+APART = 104
 
 
 def lane_iota(rows):
@@ -41,56 +44,66 @@
     return jnp.where(lane < 96, v0, s1), jnp.where(lane < 64, s1, s2), jnp.where(lane < 32, s2, s3)
 
 
-def fine_kernel(cols, part, dest, pos, me, a_ref, q_ref, x_ref, s_ref, q_mat, q_tr, acc):
+def fine_kernel(pairs, code, me, a_ref, q_ref, x_ref, s_ref, q_mat, q_tr, acc):
     step = pl.program_id(0)
+
+    def relayout(load, slot, triples):
+        for j in triples:
+            rows = unpack_rows(*[load(slice(384 * j + L * u, 384 * j + L * (u + 1))).astype(jnp.float32) for u in range(3)])
+            for v in range(4):
+                s_ref[slot, pl.ds(4 * j + v, 8, stride=STRIDE), :] = rows[v]
 
     @pl.when(step == 0)
     def _():
         acc[...] = jnp.zeros_like(acc)
-        q_mat[...] = jnp.zeros_like(q_mat)
         low = lane_iota(B) < B
-        for g in range(R // 16):
-            for j in range(B // 4):
-                at = [q_ref[16 * g:16 * g + 16, 384 * j + L * u:384 * j + L * (u + 1)].astype(jnp.float32) for u in range(3)]
-                for h in range(2):
-                    rows = unpack_rows(*[piece[8 * h:8 * h + 8] for piece in at])
-                    for v in range(4):
-                        s_ref[h, pl.ds(4 * j + v, 8, stride=B), :] = rows[v]
-
-            def one(k, carry):
-                mat = jnp.where(low, s_ref[k // 8, pl.ds(pl.multiple_of((k % 8) * B, 8), B), :], 0.0)
-                q_mat[16 * g + k, 0:B, :] = mat.astype(jnp.bfloat16)
-                q_tr[16 * g + k] = mat.T[0:B].astype(jnp.bfloat16)
-                return carry
-
-            lax.fori_loop(0, 16, one, 0)
-
-    def relayout(ii, slot):
-        for j in range(B // 4):
-            at = [a_ref[ii, :, 384 * j + L * u:384 * j + L * (u + 1)].astype(jnp.float32) for u in range(3)]
-            rows = unpack_rows(*at)
-            for v in range(4):
-                s_ref[slot, pl.ds(4 * j + v, 8, stride=B), :] = rows[v]
-
-    def multiply(ii, slot):
+        unit = (lane_iota(B) == lax.broadcasted_iota(jnp.int32, (B, L), 0)).astype(jnp.bfloat16)
+
+        def group(g, carry):
+            both = pl.ds(pl.multiple_of(16 * g, 16), 16)
+            for h in range(2):
+                relayout(lambda lanes: q_ref[both, lanes][8 * h:8 * h + 8], h, range(B // 4))
+            for k in range(16):
+                at = (k % 8) * STRIDE
+                mat = jnp.where(low, s_ref[k // 8, at:at + B, :], 0.0).astype(jnp.bfloat16)
+                q_mat[16 * g + k, 0:B, :] = mat
+                q_mat[16 * g + k, B:L, :] = jnp.zeros((L - B, L), jnp.bfloat16)
+                turned = lax.dot_general(unit, mat, (((1,), (1,)), ((), ())), preferred_element_type=jnp.float32)
+                q_tr[16 * g + k] = turned.astype(jnp.bfloat16)
+            return carry
+
+        lax.fori_loop(0, R // 16, group, 0)
+
+    def first(n):
+        ii, k = n // 4, 2 * (n % 4)
+        aq = []
+        for kk in (k, k + 1):
+            mat = s_ref[ii % 2, kk * STRIDE:kk * STRIDE + B, :].astype(jnp.bfloat16)
+            at = pairs[step * ROWS_STEP + ii, kk] % R
+            aq.append(jnp.dot(mat, q_mat[at], preferred_element_type=jnp.float32).astype(jnp.bfloat16))
+        return jnp.concatenate(aq, axis=1)
+
+    def second(n, aq):
+        ii, k = n // 4, 2 * (n % 4)
         i = step * ROWS_STEP + ii
-        left = q_tr[i]
-        for k in range(0, KA, 2):
-            aq = []
-            for kk in (k, k + 1):
-                mat = s_ref[slot, kk * B:(kk + 1) * B, :].astype(jnp.bfloat16)
-                aq.append(jnp.dot(mat, q_mat[cols[i, kk]], preferred_element_type=jnp.float32).astype(jnp.bfloat16))
-            term = jnp.dot(left, jnp.concatenate(aq, axis=1), preferred_element_type=jnp.float32)
-            for n, kk in enumerate((k, k + 1)):
-                p = part[i, kk]
-                at = pl.ds(pl.multiple_of(p * B, 8), B)
-                acc[at, :] = acc[at, :] + term[:, L * n:L * (n + 1)]
-
-    relayout(0, 0)
-    for ii in range(ROWS_STEP):
-        if ii + 1 < ROWS_STEP:
-            relayout(ii + 1, (ii + 1) % 2)
-        multiply(ii, ii % 2)
+        term = jnp.dot(q_tr[i], aq, preferred_element_type=jnp.float32)
+        for m in range(2):
+            p = pairs[i, k + m] // R
+            at = pl.ds(pl.multiple_of(p * APART, 8), B)
+            acc[at, :] = acc[at, :] + term[:, L * m:L * (m + 1)]
+
+    def prepare(ii, triples):
+        relayout(lambda lanes: a_ref[ii, :, lanes], ii % 2, triples)
+
+    prepare(0, range(B // 4))
+    held = []
+    for n in range(4 * ROWS_STEP + SKEW):
+        if n < 4 * ROWS_STEP:
+            held.append(first(n))
+            if n // 4 + 1 < ROWS_STEP:
+                prepare(n // 4 + 1, range(6 * (n % 4), 6 * (n % 4) + 6))
+        if n >= SKEW:
+            second(n - SKEW, held[n - SKEW])
 
     @pl.when(step == pl.num_programs(0) - 1)
     def _():
@@ -99,12 +112,11 @@
         base = (me[0] % 8) * 16
         codes = jnp.zeros((8, L), jnp.float32)
         for p in range(NP):
-            code = (dest[p, 0] * CELLS + pos[p]).astype(jnp.float32)
-            codes = jnp.where((row == p % 4) & (lane == base + p // 4), code, codes)
+            codes = jnp.where((row == p // 16) & (lane == base + p % 16), code[p].astype(jnp.float32), codes)
 
         def one(w, carry):
             for a in range(PER):
-                rows = [acc[pl.ds(v * B + w * PER + a, 16, stride=4 * B), :] for v in range(4)]
+                rows = [acc[pl.ds(v * 16 * APART + w * PER + a, 16, stride=APART), :] for v in range(4)]
                 for u, piece in enumerate(pack_rows(*rows)):
                     for h in range(2):
                         x_ref[w, (2 * a + h) * 3 + u] = piece[8 * h:8 * h + 8]
@@ -115,11 +127,13 @@
 
 
 def fine(a_blocks, a_cols, q_blocks, part_of, part_dest, part_pos, me):
+    pairs = a_cols + R * part_of
+    code = part_dest[:, 0] * CELLS + part_pos
     return pl.pallas_call(
         fine_kernel,
         out_shape=jax.ShapeDtypeStruct((GY, TILES + 1, 8, L), jnp.float32),
         grid_spec=pltpu.PrefetchScalarGridSpec(
-            num_scalar_prefetch=5,
+            num_scalar_prefetch=3,
             grid=(R // ROWS_STEP,),
             in_specs=[
                 pl.BlockSpec((ROWS_STEP, KA, WIDTH), lambda g, *_: (g, 0, 0)),
@@ -127,14 +141,14 @@
             ],
             out_specs=pl.BlockSpec((GY, TILES + 1, 8, L), lambda g, *_: (0, 0, 0, 0)),
             scratch_shapes=[
-                pltpu.VMEM((2, KA * B, L), jnp.float32),
+                pltpu.VMEM((2, KA * STRIDE, L), jnp.float32),
                 pltpu.VMEM((R, L, L), jnp.bfloat16),
                 pltpu.VMEM((R, B, B), jnp.bfloat16),
-                pltpu.VMEM((NP * B, L), jnp.float32),
+                pltpu.VMEM((NP * APART, L), jnp.float32),
             ],
         ),
         name="fine",
-    )(a_cols, part_of, part_dest, part_pos, me, a_blocks, q_blocks)
+    )(pairs, code, me, a_blocks, q_blocks)
 
 
 def split2(x):

time: 173 us -> 126 us (0.73)
  Pallas kernels: 81.2 us -> 35.3 us
  local copies, waits for them, and re-layouts: 7.17 us -> 3.75 us
  other arithmetic: 2.32 us -> 4.21 us
    pallas_call x1, Pallas kernels: 67.2 us -> 21.4 us  [fine(): pl.pallas_call(fine_kernel, out_shape=jax.ShapeDtypeStruct((GY, TILES + 1...]
    unnamed x9 -> x6, local copies, waits for them, and re-layouts: 5.28 us -> 1.17 us
    add x0 -> x2, other arithmetic: none -> 1.89 us  [the longest x1 1.18 us: fine(): code = part_dest[:, 0] * CELLS + part_pos]
  transfers between devices with their start and end apart: 4 -> 4, of which waited for: 3 -> 3; matrix products, arithmetic and copies ran while one was open for 1% -> 2% of each run, Pallas kernels for 0% -> 0%
where the time goes in v2:
time: 126 us; the launch traced here: 125 us
  blocking collectives  42.3 us (34%)
  Pallas kernels  35.3 us (28%)
  waiting for transfers between devices  28.9 us (23%)
  starting transfers between devices  9.53 us (8%)
  other arithmetic  4.21 us (3%)
  local copies, waits for them, and re-layouts  3.75 us (3%)
    all_to_all x1, blocking collectives, local(): lax.all_to_all(slices, 'gy', split_axis=0, concat_axis=0, tiled=True)  42.3 us
    pallas_call x1, Pallas kernels, fine(): pl.pallas_call(fine_kernel, out_shape=jax.ShapeDtypeStruct((GY, TILES + 1...  21.4 us
    all_to_all x1, waiting for transfers between devices, local(): lax.all_to_all(jnp.concatenate([mine, total], axis=1), 'gy', split_axis=0...  20.5 us
    pallas_call x1, Pallas kernels, cells_of(): pl.pallas_call(cells_kernel, out_shape=(jax.ShapeDtypeStruct((GY, 2 * PER...  8.82 us
    ppermute x3, waiting for transfers between devices, local(): lax.ppermute(group, 'gx', [(i, (i + d) % GX) for i in range(GX)])  8.41 us
    pallas_call x1, Pallas kernels, close(): pl.pallas_call(close_kernel, out_shape=(out, out), scratch_shapes=[pltpu....  5.18 us
    ppermute x3, starting transfers between devices, local(): lax.ppermute(group, 'gx', [(i, (i + d) % GX) for i in range(GX)])  4.99 us
    all_to_all x1, starting transfers between devices, local(): lax.all_to_all(jnp.concatenate([mine, total], axis=1), 'gy', split_axis=0...  4.54 us
  transfers between devices with their start and end apart: 4, of which 3 were waited for; matrix products, arithmetic and copies ran while one was open for 2% of the time, Pallas kernels for 0%

profile of v2, /device:TPU:1, one launch (start us, length us, event | category | flops | bytes accessed | tf_op | source)
XLA Modules:
  0.0 125.1 jit_solution(14107162207321180536)
XLA Ops:
  0.6 0.7 multiply_add_fusion
  1.3 0.7 copy.13.pairs
  2.0 1.2 bitcast_add_fusion.code
  3.2 21.4 %fine.1 = f32[32,19,8,128]{3,2,1,0:T(8,128)} custom-call(s32[64,8]{1,0:T(8,128)} %copy.13.pairs, s32[64]{0:T(128)} %bitcast_add_fusion.code, s32[1]{0:T(128)} %bitcast.1.me, bf16[64,8,9216]{2,1,0:T(8,128)(2,1)} %a_ref.1, bf16[64,9216]{1,0:T(8,128)(2,1)} %q_ref.1), custom_call_target="tpu_custom_call" | custom-call | tf_op jit(solution)/shard_map/fine/pallas_call | solution.py:132
  24.6 42.3 %all_to_all.10.y_ref = f32[32,19,8,128]{3,2,1,0:T(8,128)} all-to-all(f32[32,19,8,128]{3,2,1,0:T(8,128)} %fine.1), channel_id=1, replica_groups=mesh['gx'=4,'gy'=32] {'gy'}, dimensions={0} | all-to-all | bytes 4980736 | tf_op jit(solution)/shard_map/all_to_all | solution.py:237
  66.9 8.8 %cells.1 = (f32[32,6,8,128]{3,2,1,0:T(8,128)}, f32[8,6,8,128]{3,2,1,0:T(8,128)}) custom-call(f32[32,19,8,128]{3,2,1,0:T(8,128)} %all_to_all.10.y_ref), custom_call_target="tpu_custom_call" | custom-call | tf_op jit(solution)/shard_map/cells/pallas_call | solution.py:189
  75.7 1.3 %collective-permute-start = (f32[8,6,8,128]{3,2,1,0:T(8,128)}, f32[8,6,8,128]{3,2,1,0:T(8,128)S(1)}, u32[]{:S(2)}, u32[]{:S(2)}) collective-permute-start(f32[8,6,8,128]{3,2,1,0:T(8,128)} %get-tuple-element.5), channel_id=1, source_target_pairs={{0,32},{32,64},{64,96},{96,0},{1,33},{33,65},{65,97},{97,1},{2,34}... | collective-permute-start | bytes 589832 | tf_op jit(solution)/shard_map/ppermute | solution.py:239
  77.0 2.6 %collective-permute-start.1 = (f32[8,6,8,128]{3,2,1,0:T(8,128)}, f32[8,6,8,128]{3,2,1,0:T(8,128)S(1)}, u32[]{:S(2)}, u32[]{:S(2)}) collective-permute-start(f32[8,6,8,128]{3,2,1,0:T(8,128)} %get-tuple-element.5), channel_id=1, source_target_pairs={{0,64},{32,96},{64,0},{96,32},{1,65},{33,97},{65,1},{97,33},{2,66}... | collective-permute-start | bytes 589832 | tf_op jit(solution)/shard_map/ppermute | solution.py:239
  79.6 1.1 collective-permute-start.2
  80.7 3.1 %collective-permute-done = f32[8,6,8,128]{3,2,1,0:T(8,128)S(1)} collective-permute-done((f32[8,6,8,128]{3,2,1,0:T(8,128)}, f32[8,6,8,128]{3,2,1,0:T(8,128)S(1)}, u32[]{:S(2)}, u32[]{:S(2)}) %collective-permute-start) | collective-permute-done | bytes 196640 | tf_op jit(solution)/shard_map/ppermute | solution.py:239
  83.7 5.3 %collective-permute-done.1 = f32[8,6,8,128]{3,2,1,0:T(8,128)S(1)} collective-permute-done((f32[8,6,8,128]{3,2,1,0:T(8,128)}, f32[8,6,8,128]{3,2,1,0:T(8,128)S(1)}, u32[]{:S(2)}, u32[]{:S(2)}) %collective-permute-start.1) | collective-permute-done | bytes 196640 | tf_op jit(solution)/shard_map/ppermute | solution.py:239
  89.1 1.0 add_add_fusion
  90.1 1.3 %pad_maximum_fusion = f32[32,12,8,128]{3,2,1,0:T(8,128)} fusion(f32[32,6,8,128]{3,2,1,0:T(8,128)S(1)} %bitcast.9, f32[32,6,8,128]{3,2,1,0:T(8,128)S(1)} %copy-done.1), kind=kLoop, calls=%fused_computation | loop fusion | flops 393216 | bytes 3145728 | tf_op jit(solution)/shard_map/concatenate | solution.py:242
  91.5 4.5 %all-to-all-start.1 = ((f32[32,12,8,128]{3,2,1,0:T(8,128)}), f32[32,12,8,128]{3,2,1,0:T(8,128)S(1)}, u32[]{:S(2)}, u32[]{:S(2)}) async-start(f32[32,12,8,128]{3,2,1,0:T(8,128)} %pad_maximum_fusion), calls=%async_computation.1 | async-start | bytes 3145728 | tf_op jit(solution)/shard_map/all_to_all | solution.py:242
  96.0 0.3 slice_reduce_fusion
  96.3 0.1 squeeze.10
  96.5 0.1 squeeze.12
  96.5 0.2 fusion
  96.7 0.2 fusion.1
  96.9 0.7 copy.14
  97.6 0.6 pad.4.h_ref
  98.3 20.5 %all-to-all-done.1.w_ref = f32[32,12,8,128]{3,2,1,0:T(8,128)S(1)} async-done(((f32[32,12,8,128]{3,2,1,0:T(8,128)}), f32[32,12,8,128]{3,2,1,0:T(8,128)S(1)}, u32[]{:S(2)}, u32[]{:S(2)}) %all-to-all-start.1) | async-done | bytes 1572896 | tf_op jit(solution)/shard_map/all_to_all | solution.py:242
  118.8 1.2 copy-done
  119.9 5.2 %close.1 = (f32[2,8,9216]{2,1,0:T(8,128)}, f32[2,8,9216]{2,1,0:T(8,128)}) custom-call(f32[32,12,8,128]{3,2,1,0:T(8,128)} %copy-done, f32[128,128]{1,0:T(8,128)} %pad.4.h_ref, f32[96,96]{1,0:T(8,128)} %bitcast.10), custom_call_target="tpu_custom_call" | custom-call | tf_op jit(solution)/shard_map/close/pallas_call | solution.py:223
  (8 shorter events, 0.1 us)
Async XLA Ops:
  75.7 14.4 %copy-start.1 = (f32[32,6,8,128]{3,2,1,0:T(8,128)S(1)}, f32[32,6,8,128]{3,2,1,0:T(8,128)}, u32[]{:S(2)}) copy-start(f32[32,6,8,128]{3,2,1,0:T(8,128)} %get-tuple-element.4) | copy-start | bytes 2359300
  75.7 8.0 %collective-permute-start = (f32[8,6,8,128]{3,2,1,0:T(8,128)}, f32[8,6,8,128]{3,2,1,0:T(8,128)S(1)}, u32[]{:S(2)}, u32[]{:S(2)}) collective-permute-start(f32[8,6,8,128]{3,2,1,0:T(8,128)} %get-tuple-element.5), channel_id=1, source_target_pairs={{0,32},{32,64},{64,96},{96,0},{1,33},{33,65},{65,97},{97,1},{2,34}... | collective-permute-start | bytes 589832 | tf_op jit(solution)/shard_map/ppermute | solution.py:239
  77.0 12.1 %collective-permute-start.1 = (f32[8,6,8,128]{3,2,1,0:T(8,128)}, f32[8,6,8,128]{3,2,1,0:T(8,128)S(1)}, u32[]{:S(2)}, u32[]{:S(2)}) collective-permute-start(f32[8,6,8,128]{3,2,1,0:T(8,128)} %get-tuple-element.5), channel_id=1, source_target_pairs={{0,64},{32,96},{64,0},{96,32},{1,65},{33,97},{65,1},{97,33},{2,66}... | collective-permute-start | bytes 589832 | tf_op jit(solution)/shard_map/ppermute | solution.py:239
  79.6 9.5 %collective-permute-start.2 = (f32[8,6,8,128]{3,2,1,0:T(8,128)}, f32[8,6,8,128]{3,2,1,0:T(8,128)S(1)}, u32[]{:S(2)}, u32[]{:S(2)}) collective-permute-start(f32[8,6,8,128]{3,2,1,0:T(8,128)} %get-tuple-element.5), channel_id=1, source_target_pairs={{0,96},{32,0},{64,32},{96,64},{1,97},{33,1},{65,33},{97,65},{2,98}... | collective-permute-start | bytes 589832 | tf_op jit(solution)/shard_map/ppermute | solution.py:239
  91.5 4.6 %copy-start.2 = (f32[3,9216]{1,0:T(4,128)S(1)}, f32[3,9216]{1,0:T(4,128)}, u32[]{:S(2)}) copy-start(f32[3,9216]{1,0:T(4,128)} %param.13) | copy-start | bytes 331780
  91.5 27.3 %all-to-all-start.1 = ((f32[32,12,8,128]{3,2,1,0:T(8,128)}), f32[32,12,8,128]{3,2,1,0:T(8,128)S(1)}, u32[]{:S(2)}, u32[]{:S(2)}) async-start(f32[32,12,8,128]{3,2,1,0:T(8,128)} %pad_maximum_fusion), calls=%async_computation.1 | async-start | bytes 3145728 | tf_op jit(solution)/shard_map/all_to_all | solution.py:242
  118.8 1.2 copy-start

commit v3 on v2

--- a/solution.py
+++ b/solution.py
@@ -20,8 +20,10 @@
 PER = B // GY
 TILES = 18
 ROWS_STEP = 8
-SKEW = 4
+SKEW = 8
 STRIDE = 100
+GAP = 20
+M_ROWS = 512
 APART = 104
 
 
@@ -55,24 +57,24 @@
 
     @pl.when(step == 0)
     def _():
-        acc[...] = jnp.zeros_like(acc)
         low = lane_iota(B) < B
         unit = (lane_iota(B) == lax.broadcasted_iota(jnp.int32, (B, L), 0)).astype(jnp.bfloat16)
-
-        def group(g, carry):
-            both = pl.ds(pl.multiple_of(16 * g, 16), 16)
-            for h in range(2):
-                relayout(lambda lanes: q_ref[both, lanes][8 * h:8 * h + 8], h, range(B // 4))
-            for k in range(16):
-                at = (k % 8) * STRIDE
-                mat = jnp.where(low, s_ref[k // 8, at:at + B, :], 0.0).astype(jnp.bfloat16)
-                q_mat[16 * g + k, 0:B, :] = mat
-                q_mat[16 * g + k, B:L, :] = jnp.zeros((L - B, L), jnp.bfloat16)
-                turned = lax.dot_general(unit, mat, (((1,), (1,)), ((), ())), preferred_element_type=jnp.float32)
-                q_tr[16 * g + k] = turned.astype(jnp.bfloat16)
-            return carry
-
-        lax.fori_loop(0, R // 16, group, 0)
+        part_rows = NP * APART // R
+
+        def spread(g, triples):
+            both = slice(16 * (g // 2), 16 * (g // 2) + 16)
+            relayout(lambda lanes: q_ref[both, lanes][8 * (g % 2):8 * (g % 2) + 8], g % 2, triples)
+
+        spread(0, range(B // 4))
+        for c in range(R):
+            g, k = divmod(c, 8)
+            if c + 8 < R:
+                spread(g + 1, range(3 * k, 3 * k + 3))
+            acc[c * part_rows:(c + 1) * part_rows, :] = jnp.zeros((part_rows, L), jnp.float32)
+            mat = jnp.where(low, s_ref[g % 2, k * STRIDE:k * STRIDE + B, :], 0.0).astype(jnp.bfloat16)
+            q_mat[c] = mat
+            turned = lax.dot_general(unit, mat, (((1,), (1,)), ((), ())), preferred_element_type=jnp.float32)
+            q_tr[c] = turned.astype(jnp.bfloat16)
 
     def first(n):
         ii, k = n // 4, 2 * (n % 4)
@@ -80,7 +82,7 @@
         for kk in (k, k + 1):
             mat = s_ref[ii % 2, kk * STRIDE:kk * STRIDE + B, :].astype(jnp.bfloat16)
             at = pairs[step * ROWS_STEP + ii, kk] % R
-            aq.append(jnp.dot(mat, q_mat[at], preferred_element_type=jnp.float32).astype(jnp.bfloat16))
+            aq.append(jnp.dot(mat[:, :B], q_mat[at], preferred_element_type=jnp.float32).astype(jnp.bfloat16))
         return jnp.concatenate(aq, axis=1)
 
     def second(n, aq):
@@ -123,7 +125,7 @@
             x_ref[w, TILES] = codes
             return carry
 
-        lax.fori_loop(0, GY, one, 0)
+        lax.fori_loop(0, GY, one, 0, unroll=4)
 
 
 def fine(a_blocks, a_cols, q_blocks, part_of, part_dest, part_pos, me):
@@ -142,11 +144,12 @@
             out_specs=pl.BlockSpec((GY, TILES + 1, 8, L), lambda g, *_: (0, 0, 0, 0)),
             scratch_shapes=[
                 pltpu.VMEM((2, KA * STRIDE, L), jnp.float32),
-                pltpu.VMEM((R, L, L), jnp.bfloat16),
+                pltpu.VMEM((R, B, L), jnp.bfloat16),
                 pltpu.VMEM((R, B, B), jnp.bfloat16),
                 pltpu.VMEM((NP * APART, L), jnp.float32),
             ],
         ),
+        compiler_params=pltpu.CompilerParams(vmem_limit_bytes=58 << 20),
         name="fine",
     )(pairs, code, me, a_blocks, q_blocks)
 
@@ -156,66 +159,141 @@
     return hi, (x - hi.astype(jnp.float32)).astype(jnp.bfloat16)
 
 
-def cells_kernel(y_ref, z_ref, t_ref, hi_ref, lo_ref):
+def cells_kernel(y_ref, z_ref, t_ref, x_ref, m_ref, g_ref):
+    wide = 2 * PER * L
+
     def one(s, carry):
         for a in range(PER):
             halves = [unpack_rows(*[y_ref[s, (2 * a + h) * 3 + u] for u in range(3)]) for h in range(2)]
             for v in range(4):
                 hi, lo = split2(jnp.concatenate([halves[0][v], halves[1][v]], axis=0))
                 at = pl.ds(pl.multiple_of(v * 512 + s * 16, 16), 16)
-                hi_ref[at, L * a:L * (a + 1)] = hi
-                lo_ref[at, L * a:L * (a + 1)] = lo
-        return carry
-
-    lax.fori_loop(0, GY, one, 0)
+                x_ref[at, L * a:L * (a + 1)] = hi
+                x_ref[at, L * (PER + a):L * (PER + a + 1)] = lo
+        return carry
+
+    lax.fori_loop(0, GY, one, 0, unroll=4)
     tiles = [functools.reduce(jnp.add, [y_ref[8 * o + s, TILES] for s in range(8)]) for o in range(4)]
-    codes = jnp.concatenate([tiles[o][v:v + 1] for v in range(4) for o in range(4)], axis=1)
-
-    def chunk(c, carry):
-        want = (lax.broadcasted_iota(jnp.int32, (L, 1), 0) + c * L).astype(jnp.float32)
-        table = jnp.where(want == codes, 1.0, 0.0).astype(jnp.bfloat16)
-        sums = jnp.dot(table, hi_ref[...], preferred_element_type=jnp.float32)
-        sums = sums + jnp.dot(table, lo_ref[...], preferred_element_type=jnp.float32)
+    codes = jnp.concatenate([tiles[o][v:v + 1] for v in range(4) for o in range(4)], axis=1) - 256.0
+    names = codes.astype(jnp.bfloat16)
+    row = lax.broadcasted_iota(jnp.int32, (4 * L, 1), 0)
+    want = ((row % L) // 4) * CELLS + 4 * (row // L) + row % 4
+    want = (want.astype(jnp.float32) - 256.0).astype(jnp.bfloat16)
+    one_bf, zero_bf = jnp.ones((), jnp.bfloat16), jnp.zeros((), jnp.bfloat16)
+    for c in range(0, 4 * L, M_ROWS):
+        table = jnp.where(want[c:c + M_ROWS] == names, one_bf, zero_bf)
+        sums = jnp.dot(table, x_ref[...], preferred_element_type=jnp.float32)
+        m_ref[c:c + M_ROWS, :] = sums[:, :wide // 2] + sums[:, wide // 2:]
+
+    def fold(g, carry):
         for a in range(PER):
-            at = sums[:, L * a:L * (a + 1)].reshape(8, 2, 8, L)
-            z_ref[pl.ds(c * 8, 8), 2 * a:2 * a + 2] = at
-            t_ref[pl.ds(c * 2, 2), 2 * a:2 * a + 2] = at.reshape(2, 4, 2, 8, L).sum(1)
-        return carry
-
-    lax.fori_loop(0, 4, chunk, 0)
+            for v in range(4):
+                at = pl.multiple_of(L * v + 16 * g, 16)
+                both = m_ref[pl.ds(at, 8), L * a:L * (a + 1)] + m_ref[pl.ds(at + 8, 8), L * a:L * (a + 1)]
+                both = both + pltpu.roll(both, 4, 0)
+                g_ref[a, v, pl.ds(pl.multiple_of(4 * g, 4), 4), :] = both[0:4]
+        return carry
+
+    lax.fori_loop(0, GY // 4, fold, 0, unroll=2)
+    for a in range(PER):
+        for u, piece in enumerate(pack_rows(*[g_ref[a, v] for v in range(4)])):
+            t_ref[3 * a + u] = piece
+
+    def pack(n, carry):
+        for a in range(PER):
+            rows = [m_ref[pl.ds(pl.multiple_of(L * v + 16 * n, 16), 16), L * a:L * (a + 1)] for v in range(4)]
+            for u, piece in enumerate(pack_rows(*rows)):
+                z_ref[3 * a + u, pl.ds(pl.multiple_of(16 * n, 16), 16), :] = piece
+        return carry
+
+    lax.fori_loop(0, L // 16, pack, 0, unroll=2)
 
 
 def cells_of(received):
     return pl.pallas_call(
         cells_kernel,
         out_shape=(
-            jax.ShapeDtypeStruct((GY, 2 * PER, 8, L), jnp.float32),
-            jax.ShapeDtypeStruct((GY // 4, 2 * PER, 8, L), jnp.float32),
+            jax.ShapeDtypeStruct((3 * PER, L + 8, L), jnp.float32),
+            jax.ShapeDtypeStruct((3 * PER, L // 4, L), jnp.float32),
         ),
-        scratch_shapes=[pltpu.VMEM((4 * 512, PER * L), jnp.bfloat16)] * 2,
+        scratch_shapes=[
+            pltpu.VMEM((4 * 512, 2 * PER * L), jnp.bfloat16),
+            pltpu.VMEM((4 * L, PER * L), jnp.float32),
+            pltpu.VMEM((PER, 4, L // 4, L), jnp.float32),
+        ],
+        compiler_params=pltpu.CompilerParams(vmem_limit_bytes=24 << 20),
         name="cells",
     )(received)
 
 
-def close_kernel(w_ref, h_ref, ht_ref, first_ref, last_ref, r_ref, o_ref):
-    def rows_of(tile):
-        for j in range(B // 4):
-            for half in range(RC):
-                yield j, half, [tile(4 * j + v, half) for v in range(4)]
-
-    for j, half, rows in rows_of(lambda r, half: w_ref[r // PER, 2 * (r % PER) + half]):
-        for u, piece in enumerate(pack_rows(*rows)):
-            first_ref[half, :, 384 * j + L * u:384 * j + L * (u + 1)] = piece
-    total = w_ref[:, 2 * PER:4 * PER].reshape(B * CELLS, L)
-    r_ref[...] = jnp.dot(total, h_ref[...], precision=lax.Precision.HIGHEST, preferred_element_type=jnp.float32)
+def merge_kernel(z_ref, t0, t1, t2, t3, out_ref, s_ref):
+    upper = lax.broadcasted_iota(jnp.int32, (8, L), 0) < 4
+    for n in range(3 * PER):
+        s_ref[n, 4:L // 4 + 4, :] = (t0[n] + t1[n]) + (t2[n] + t3[n])
+    for d in range(GY):
+        g = d // 4
+        for n in range(3 * PER):
+            out_ref[d, n] = jnp.where(upper, z_ref[n, 4 * d:4 * d + 8, :], s_ref[n, 4 * g:4 * g + 8, :])
+
+
+def merge(mine, parts):
+    return pl.pallas_call(
+        merge_kernel,
+        out_shape=jax.ShapeDtypeStruct((GY, 3 * PER, 8, L), jnp.float32),
+        scratch_shapes=[pltpu.VMEM((3 * PER, L // 4 + 8, L), jnp.float32)],
+        compiler_params=pltpu.CompilerParams(vmem_limit_bytes=8 << 20),
+        name="merge",
+    )(mine, *parts)
+
+
+def close_kernel(w_ref, h_ref, ht_ref, first_ref, last_ref, f_ref, hi_ref, lo_ref, r_ref, o_ref):
+    upper = lax.broadcasted_iota(jnp.int32, (8, L), 0) < 4
+
+    def spread(w, carry):
+        for a in range(PER):
+            rows = unpack_rows(*[w_ref[w, 3 * a + u] for u in range(3)])
+            for v in range(4):
+                f_ref[v, pl.ds(pl.multiple_of((w * PER + a) * 8 + 8, 8), 8), :] = rows[v]
+        return carry
+
+    lax.fori_loop(0, GY, spread, 0, unroll=4)
+
+    def outputs(j, carry):
+        lanes = [pl.ds(pl.multiple_of(384 * j + L * u, L), L) for u in range(3)]
+        base = pl.multiple_of(32 * j + 8, 8)
+        for half in range(RC):
+            rows = [jnp.where(upper, f_ref[2 * half, pl.ds(base + 8 * v, 8), :], f_ref[2 * half + 1, pl.ds(base + 8 * v - 4, 8), :]) for v in range(4)]
+            for u, piece in enumerate(pack_rows(*rows)):
+                first_ref[half, :, lanes[u]] = piece
+        for v in range(4):
+            both = [jnp.where(upper, f_ref[2 * half, pl.ds(base + 8 * v + 4, 8), :], f_ref[2 * half + 1, pl.ds(base + 8 * v, 8), :]) for half in range(RC)]
+            hi, lo = split2(jnp.concatenate(both, axis=0))
+            at = pl.ds(pl.multiple_of(64 * j + 16 * v, 16), 16)
+            hi_ref[at, :] = hi
+            lo_ref[at, :] = lo
+        return carry
+
+    lax.fori_loop(0, B // 4, outputs, 0, unroll=2)
+    h_hi, h_lo = split2(h_ref[...])
+    t_hi, t_lo = split2(ht_ref[...])
+    dot = functools.partial(jnp.dot, preferred_element_type=jnp.float32)
+    for c in range(0, B, 16):
+        at = slice(c * CELLS, (c + 16) * CELLS)
+        hi, lo = hi_ref[at, :], lo_ref[at, :]
+        right = dot(hi, h_hi) + (dot(lo, h_hi) + dot(hi, h_lo))
+        for r in range(16):
+            r_ref[(c + r) * GAP:(c + r) * GAP + CELLS, :] = right[r * CELLS:(r + 1) * CELLS]
     for c in range(0, CELLS, 2):
-        pair = jnp.concatenate([r_ref[pl.ds(c + n, B, stride=CELLS), :] for n in range(2)], axis=1)
-        out = jnp.dot(ht_ref[...], pair, precision=lax.Precision.HIGHEST, preferred_element_type=jnp.float32)
+        pair = jnp.concatenate([r_ref[pl.ds(c + n, B, stride=GAP), :] for n in range(2)], axis=1)
+        hi, lo = split2(pair)
+        out = dot(t_hi, hi) + (dot(t_hi, lo) + dot(t_lo, hi))
         for n in range(2):
-            o_ref[pl.ds(c + n, B, stride=CELLS), :] = out[:, L * n:L * (n + 1)]
-    for j, half, rows in rows_of(lambda r, half: o_ref[r * CELLS + 8 * half:r * CELLS + 8 * half + 8, :]):
-        for u, piece in enumerate(pack_rows(*rows)):
-            last_ref[half, :, 384 * j + L * u:384 * j + L * (u + 1)] = piece
+            o_ref[pl.ds(c + n, B, stride=GAP), :] = out[:, L * n:L * (n + 1)]
+    for j in range(B // 4):
+        for half in range(RC):
+            rows = [o_ref[(4 * j + v) * GAP + 8 * half:(4 * j + v) * GAP + 8 * half + 8, :] for v in range(4)]
+            for u, piece in enumerate(pack_rows(*rows)):
+                last_ref[half, :, 384 * j + L * u:384 * j + L * (u + 1)] = piece
 
 
 def close(received, h, ht):
@@ -223,7 +301,14 @@
     return pl.pallas_call(
         close_kernel,
         out_shape=(out, out),
-        scratch_shapes=[pltpu.VMEM((B * CELLS, L), jnp.float32)] * 2,
+        scratch_shapes=[
+            pltpu.VMEM((4, B * 8 + 16, L), jnp.float32),
+            pltpu.VMEM((B * CELLS, L), jnp.bfloat16),
+            pltpu.VMEM((B * CELLS, L), jnp.bfloat16),
+            pltpu.VMEM((B * GAP, L), jnp.float32),
+            pltpu.VMEM((B * GAP, L), jnp.float32),
+        ],
+        compiler_params=pltpu.CompilerParams(vmem_limit_bytes=16 << 20),
         name="close",
     )(received, h, ht)
 
@@ -237,9 +322,8 @@
     gathered = lax.all_to_all(slices, "gy", split_axis=0, concat_axis=0, tiled=True)
     mine, group = cells_of(gathered)
     others = [lax.ppermute(group, "gx", [(i, (i + d) % GX) for i in range(GX)]) for d in range(1, GX)]
-    total = group + others[0] + others[1] + others[2]
-    total = jnp.broadcast_to(total[:, None], (GY // 4, 4) + total.shape[1:]).reshape(mine.shape)
-    back = lax.all_to_all(jnp.concatenate([mine, total], axis=1), "gy", split_axis=0, concat_axis=0, tiled=True)
+    outgoing = merge(mine, [group] + others)
+    back = lax.all_to_all(outgoing, "gy", split_axis=0, concat_axis=0, tiled=True)
     return close(back, jnp.pad(h, ((0, L - B), (0, L - B))), h.T)
 
 

time: 126 us -> 107 us (0.85)
  Pallas kernels: 35.3 us -> 27 us
  waiting for transfers between devices: 28.9 us -> 23.6 us
  local copies, waits for them, and re-layouts: 3.75 us -> 1.3 us
  other arithmetic: 4.21 us -> 1.89 us
    pallas_call x1 -> x2, Pallas kernels: 8.82 us -> 5.13 us  [the longest x1 4 us: cells_of(): pl.pallas_call(cells_kernel, out_shape=(jax.ShapeDtypeStruct((3 * PER, L...]
    pallas_call x1, Pallas kernels: 21.4 us -> 17.9 us  [fine(): pl.pallas_call(fine_kernel, out_shape=jax.ShapeDtypeStruct((GY, TILES + 1...]
    all_to_all x1, waiting for transfers between devices: 20.5 us -> 17.4 us  [local(): lax.all_to_all(outgoing, 'gy', split_axis=0, concat_axis=0, tiled=True)]
    ppermute x3, waiting for transfers between devices: 8.41 us -> 6.13 us  [local(): lax.ppermute(group, 'gx', [(i, (i + d) % GX) for i in range(GX)])]
    concatenate x1 -> x0, other arithmetic: 1.34 us -> none  [local(): jnp.concatenate([mine, total], axis=1)]
  transfers between devices with their start and end apart: 4 -> 4, of which waited for: 3 -> 3; matrix products, arithmetic and copies ran while one was open for 2% -> 1% of each run, Pallas kernels for 0% -> 0%
where the time goes in v3:
time: 107 us; the launch traced here: 106 us
  blocking collectives  42.1 us (39%)
  Pallas kernels  27 us (25%)
  waiting for transfers between devices  23.6 us (22%)
  starting transfers between devices  9.48 us (9%)
  other arithmetic  1.89 us (2%)
  local copies, waits for them, and re-layouts  1.3 us (1%)
    all_to_all x1, blocking collectives, local(): lax.all_to_all(slices, 'gy', split_axis=0, concat_axis=0, tiled=True)  42.1 us
    pallas_call x1, Pallas kernels, fine(): pl.pallas_call(fine_kernel, out_shape=jax.ShapeDtypeStruct((GY, TILES + 1...  17.9 us
    all_to_all x1, waiting for transfers between devices, local(): lax.all_to_all(outgoing, 'gy', split_axis=0, concat_axis=0, tiled=True)  17.4 us
    ppermute x3, waiting for transfers between devices, local(): lax.ppermute(group, 'gx', [(i, (i + d) % GX) for i in range(GX)])  6.13 us
    ppermute x3, starting transfers between devices, local(): lax.ppermute(group, 'gx', [(i, (i + d) % GX) for i in range(GX)])  5.1 us
    all_to_all x1, starting transfers between devices, local(): lax.all_to_all(outgoing, 'gy', split_axis=0, concat_axis=0, tiled=True)  4.37 us
    pallas_call x1, Pallas kernels, close(): pl.pallas_call(close_kernel, out_shape=(out, out), scratch_shapes=[pltpu....  4.01 us
    pallas_call x1, Pallas kernels, cells_of(): pl.pallas_call(cells_kernel, out_shape=(jax.ShapeDtypeStruct((3 * PER, L...  4 us
  transfers between devices with their start and end apart: 4, of which 3 were waited for; matrix products, arithmetic and copies ran while one was open for 1% of the time, Pallas kernels for 0%

profile of v3, /device:TPU:1, one launch (start us, length us, event | category | flops | bytes accessed | tf_op | source)
XLA Modules:
  0.0 106.5 jit_solution(17852159074706070540)
XLA Ops:
  0.6 0.7 multiply_add_fusion
  1.3 0.7 copy.13.pairs
  2.0 1.2 %bitcast_add_fusion.code = s32[64]{0:T(128)} fusion(s32[64]{0:T(128)} %param.12, s32[64,1]{0,1:T(1,128)} %param.11), kind=kLoop, calls=%fused_computation.4 | loop fusion | flops 128 | bytes 768 | tf_op jit(solution)/shard_map/add | solution.py:133
  3.2 17.9 %fine.1 = f32[32,19,8,128]{3,2,1,0:T(8,128)} custom-call(s32[64,8]{1,0:T(8,128)} %copy.13.pairs, s32[64]{0:T(128)} %bitcast_add_fusion.code, s32[1]{0:T(128)} %bitcast.1.me, bf16[64,8,9216]{2,1,0:T(8,128)(2,1)} %a_ref.1, bf16[64,9216]{1,0:T(8,128)(2,1)} %q_ref.1), custom_call_target="tpu_custom_call" | custom-call | tf_op jit(solution)/shard_map/fine/pallas_call | solution.py:134
  21.1 42.1 %all_to_all.10.y_ref = f32[32,19,8,128]{3,2,1,0:T(8,128)S(1)} all-to-all(f32[32,19,8,128]{3,2,1,0:T(8,128)} %fine.1), channel_id=1, replica_groups=mesh['gx'=4,'gy'=32] {'gy'}, dimensions={0} | all-to-all | bytes 4980736 | tf_op jit(solution)/shard_map/all_to_all | solution.py:322
  63.2 4.0 %cells.1 = (f32[9,136,128]{2,1,0:T(8,128)S(1)}, f32[9,32,128]{2,1,0:T(8,128)S(1)}) custom-call(f32[32,19,8,128]{3,2,1,0:T(8,128)S(1)} %all_to_all.10.y_ref), custom_call_target="tpu_custom_call" | custom-call | tf_op jit(solution)/shard_map/cells/pallas_call | solution.py:213
  67.2 0.0 copy-start
  67.3 1.4 %collective-permute-start = (f32[9,32,128]{2,1,0:T(8,128)S(1)}, f32[9,32,128]{2,1,0:T(8,128)S(1)}, u32[]{:S(2)}, u32[]{:S(2)}) collective-permute-start(f32[9,32,128]{2,1,0:T(8,128)S(1)} %get-tuple-element.5.t0), channel_id=1, source_target_pairs={{0,32},{32,64},{64,96},{96,0},{1,33},{33,65},{65,97},{97,1},{2,34}... | collective-permute-start | bytes 442376 | tf_op jit(solution)/shard_map/ppermute | solution.py:324
  68.6 2.7 %collective-permute-start.1 = (f32[9,32,128]{2,1,0:T(8,128)S(1)}, f32[9,32,128]{2,1,0:T(8,128)S(1)}, u32[]{:S(2)}, u32[]{:S(2)}) collective-permute-start(f32[9,32,128]{2,1,0:T(8,128)S(1)} %get-tuple-element.5.t0), channel_id=1, source_target_pairs={{0,64},{32,96},{64,0},{96,32},{1,65},{33,97},{65,1},{97,33},{2,66}... | collective-permute-start | bytes 442376 | tf_op jit(solution)/shard_map/ppermute | solution.py:324
  71.3 1.0 collective-permute-start.2
  72.4 1.9 %collective-permute-done.t1 = f32[9,32,128]{2,1,0:T(8,128)S(1)} collective-permute-done((f32[9,32,128]{2,1,0:T(8,128)S(1)}, f32[9,32,128]{2,1,0:T(8,128)S(1)}, u32[]{:S(2)}, u32[]{:S(2)}) %collective-permute-start) | collective-permute-done | bytes 147488 | tf_op jit(solution)/shard_map/ppermute | solution.py:324
  74.3 4.2 %collective-permute-done.1.t2 = f32[9,32,128]{2,1,0:T(8,128)S(1)} collective-permute-done((f32[9,32,128]{2,1,0:T(8,128)S(1)}, f32[9,32,128]{2,1,0:T(8,128)S(1)}, u32[]{:S(2)}, u32[]{:S(2)}) %collective-permute-start.1) | collective-permute-done | bytes 147488 | tf_op jit(solution)/shard_map/ppermute | solution.py:324
  78.5 0.0 collective-permute-done.2.t3
  78.5 1.1 %merge.1 = f32[32,9,8,128]{3,2,1,0:T(8,128)} custom-call(f32[9,136,128]{2,1,0:T(8,128)S(1)} %get-tuple-element.4.z_ref, f32[9,32,128]{2,1,0:T(8,128)S(1)} %get-tuple-element.5.t0, f32[9,32,128]{2,1,0:T(8,128)S(1)} %collective-permute-done.t1, f32[9,32,128]{2,1,0:T(8,128)S(1)} %collective-permute-done.1.t2, f32[9,32,128]{2,1,0:T(8,128)S(1)} %collective-permute-done.2.t3), custom_call_target="tpu_custom_call" | custom-call | tf_op jit(solution)/shard_map/merge/pallas_call | solution.py:240
  79.6 4.4 %all-to-all-start.1 = ((f32[32,9,8,128]{3,2,1,0:T(8,128)}), f32[32,9,8,128]{3,2,1,0:T(8,128)S(1)}, u32[]{:S(2)}, u32[]{:S(2)}) async-start(f32[32,9,8,128]{3,2,1,0:T(8,128)} %merge.1), calls=%async_computation.1 | async-start | bytes 2359296 | tf_op jit(solution)/shard_map/all_to_all | solution.py:326
  84.0 0.3 slice_reduce_fusion
  84.3 0.1 squeeze.10
  84.4 0.1 squeeze.11
  84.5 0.1 squeeze.12
  84.5 0.2 fusion
  84.7 0.2 fusion.1
  84.9 0.1 copy.14
  85.0 17.4 %all-to-all-done.1.w_ref = f32[32,9,8,128]{3,2,1,0:T(8,128)S(1)} async-done(((f32[32,9,8,128]{3,2,1,0:T(8,128)}), f32[32,9,8,128]{3,2,1,0:T(8,128)S(1)}, u32[]{:S(2)}, u32[]{:S(2)}) %all-to-all-start.1) | async-done | bytes 1179680 | tf_op jit(solution)/shard_map/all_to_all | solution.py:326
  102.5 4.0 %close.1 = (f32[2,8,9216]{2,1,0:T(8,128)}, f32[2,8,9216]{2,1,0:T(8,128)}) custom-call(f32[32,9,8,128]{3,2,1,0:T(8,128)S(1)} %all-to-all-done.1.w_ref, f32[128,128]{1,0:T(8,128)S(1)} %pad.4.h_ref, f32[96,96]{1,0:T(8,128)S(1)} %bitcast.8), custom_call_target="tpu_custom_call" | custom-call | tf_op jit(solution)/shard_map/close/pallas_call | solution.py:301
  (2 shorter events, 0.0 us)
Async XLA Ops:
  67.2 16.8 %copy-start = (f32[3,9216]{1,0:T(4,128)S(1)}, f32[3,9216]{1,0:T(4,128)}, u32[]{:S(2)}) copy-start(f32[3,9216]{1,0:T(4,128)} %param.13) | copy-start | bytes 331780
  67.3 7.0 %collective-permute-start = (f32[9,32,128]{2,1,0:T(8,128)S(1)}, f32[9,32,128]{2,1,0:T(8,128)S(1)}, u32[]{:S(2)}, u32[]{:S(2)}) collective-permute-start(f32[9,32,128]{2,1,0:T(8,128)S(1)} %get-tuple-element.5.t0), channel_id=1, source_target_pairs={{0,32},{32,64},{64,96},{96,0},{1,33},{33,65},{65,97},{97,1},{2,34}... | collective-permute-start | bytes 442376 | tf_op jit(solution)/shard_map/ppermute | solution.py:324
  68.6 9.8 %collective-permute-start.1 = (f32[9,32,128]{2,1,0:T(8,128)S(1)}, f32[9,32,128]{2,1,0:T(8,128)S(1)}, u32[]{:S(2)}, u32[]{:S(2)}) collective-permute-start(f32[9,32,128]{2,1,0:T(8,128)S(1)} %get-tuple-element.5.t0), channel_id=1, source_target_pairs={{0,64},{32,96},{64,0},{96,32},{1,65},{33,97},{65,1},{97,33},{2,66}... | collective-permute-start | bytes 442376 | tf_op jit(solution)/shard_map/ppermute | solution.py:324
  71.3 7.2 %collective-permute-start.2 = (f32[9,32,128]{2,1,0:T(8,128)S(1)}, f32[9,32,128]{2,1,0:T(8,128)S(1)}, u32[]{:S(2)}, u32[]{:S(2)}) collective-permute-start(f32[9,32,128]{2,1,0:T(8,128)S(1)} %get-tuple-element.5.t0), channel_id=1, source_target_pairs={{0,96},{32,0},{64,32},{96,64},{1,97},{33,1},{65,33},{97,65},{2,98}... | collective-permute-start | bytes 442376 | tf_op jit(solution)/shard_map/ppermute | solution.py:324
  79.6 22.8 %all-to-all-start.1 = ((f32[32,9,8,128]{3,2,1,0:T(8,128)}), f32[32,9,8,128]{3,2,1,0:T(8,128)S(1)}, u32[]{:S(2)}, u32[]{:S(2)}) async-start(f32[32,9,8,128]{3,2,1,0:T(8,128)} %merge.1), calls=%async_computation.1 | async-start | bytes 2359296 | tf_op jit(solution)/shard_map/all_to_all | solution.py:326

commit v4 on v3

--- a/solution.py
+++ b/solution.py
@@ -19,8 +19,7 @@
 GX = 4
 PER = B // GY
 TILES = 18
-ROWS_STEP = 8
-SKEW = 8
+ROWS_STEP = 16
 STRIDE = 100
 GAP = 20
 M_ROWS = 512
@@ -46,7 +45,7 @@
     return jnp.where(lane < 96, v0, s1), jnp.where(lane < 64, s1, s2), jnp.where(lane < 32, s2, s3)
 
 
-def fine_kernel(pairs, code, me, a_ref, q_ref, x_ref, s_ref, q_mat, q_tr, acc):
+def fine_kernel(cols, part, dest, pos, me, a_ref, q_ref, x_ref, s_ref, q_mat, q_tr, acc, aq_ref):
     step = pl.program_id(0)
 
     def relayout(load, slot, triples):
@@ -65,6 +64,8 @@
             both = slice(16 * (g // 2), 16 * (g // 2) + 16)
             relayout(lambda lanes: q_ref[both, lanes][8 * (g % 2):8 * (g % 2) + 8], g % 2, triples)
 
+        s_ref[1] = jnp.zeros((KA * STRIDE, L), jnp.float32)
+        aq_ref[...] = jnp.zeros_like(aq_ref)
         spread(0, range(B // 4))
         for c in range(R):
             g, k = divmod(c, 8)
@@ -76,45 +77,48 @@
             turned = lax.dot_general(unit, mat, (((1,), (1,)), ((), ())), preferred_element_type=jnp.float32)
             q_tr[c] = turned.astype(jnp.bfloat16)
 
-    def first(n):
-        ii, k = n // 4, 2 * (n % 4)
-        aq = []
+    def first(r, slot, k):
+        row = jnp.maximum(r, 0)
         for kk in (k, k + 1):
-            mat = s_ref[ii % 2, kk * STRIDE:kk * STRIDE + B, :].astype(jnp.bfloat16)
-            at = pairs[step * ROWS_STEP + ii, kk] % R
-            aq.append(jnp.dot(mat[:, :B], q_mat[at], preferred_element_type=jnp.float32).astype(jnp.bfloat16))
-        return jnp.concatenate(aq, axis=1)
-
-    def second(n, aq):
-        ii, k = n // 4, 2 * (n % 4)
-        i = step * ROWS_STEP + ii
-        term = jnp.dot(q_tr[i], aq, preferred_element_type=jnp.float32)
+            mat = s_ref[slot, kk * STRIDE:kk * STRIDE + B, :].astype(jnp.bfloat16)
+            prod = jnp.dot(mat[:, :B], q_mat[cols[kk, row]], preferred_element_type=jnp.float32)
+            aq_ref[slot, k // 2, :, L * (kk - k):L * (kk - k + 1)] = prod.astype(jnp.bfloat16)
+
+    def second(r, slot, k):
+        row = jnp.maximum(r, 0)
+        term = jnp.dot(q_tr[row], aq_ref[slot, k // 2], preferred_element_type=jnp.float32)
         for m in range(2):
-            p = pairs[i, k + m] // R
+            p = jnp.where(r < 0, NP, part[k + m, row])
             at = pl.ds(pl.multiple_of(p * APART, 8), B)
             acc[at, :] = acc[at, :] + term[:, L * m:L * (m + 1)]
 
-    def prepare(ii, triples):
-        relayout(lambda lanes: a_ref[ii, :, lanes], ii % 2, triples)
-
-    prepare(0, range(B // 4))
-    held = []
-    for n in range(4 * ROWS_STEP + SKEW):
-        if n < 4 * ROWS_STEP:
-            held.append(first(n))
-            if n // 4 + 1 < ROWS_STEP:
-                prepare(n // 4 + 1, range(6 * (n % 4), 6 * (n % 4) + 6))
-        if n >= SKEW:
-            second(n - SKEW, held[n - SKEW])
-
-    @pl.when(step == pl.num_programs(0) - 1)
+    last = pl.num_programs(0) - 1
+
+    @pl.when(step < last)
+    def _():
+        for ii in range(ROWS_STEP):
+            r = step * ROWS_STEP + ii
+            for n in range(4):
+                first(r - 1, (ii + 1) % 2, 2 * n)
+                relayout(lambda lanes: a_ref[ii, :, lanes], ii % 2, range(6 * n, 6 * n + 6))
+                second(r - 2, ii % 2, 2 * n)
+
+    @pl.when(step == last)
+    def _():
+        for n in range(4):
+            first(R - 1, (R - 1) % 2, 2 * n)
+            second(R - 2, R % 2, 2 * n)
+        for n in range(4):
+            second(R - 1, (R - 1) % 2, 2 * n)
+
+    @pl.when(step == last)
     def _():
         row = lax.broadcasted_iota(jnp.int32, (8, L), 0)
         lane = lane_iota(8)
         base = (me[0] % 8) * 16
         codes = jnp.zeros((8, L), jnp.float32)
         for p in range(NP):
-            codes = jnp.where((row == p // 16) & (lane == base + p % 16), code[p].astype(jnp.float32), codes)
+            codes = jnp.where((row == p // 16) & (lane == base + p % 16), (dest[p] * CELLS + pos[p]).astype(jnp.float32), codes)
 
         def one(w, carry):
             for a in range(PER):
@@ -125,20 +129,18 @@
             x_ref[w, TILES] = codes
             return carry
 
-        lax.fori_loop(0, GY, one, 0, unroll=4)
+        lax.fori_loop(0, GY, one, 0, unroll=8)
 
 
 def fine(a_blocks, a_cols, q_blocks, part_of, part_dest, part_pos, me):
-    pairs = a_cols + R * part_of
-    code = part_dest[:, 0] * CELLS + part_pos
     return pl.pallas_call(
         fine_kernel,
         out_shape=jax.ShapeDtypeStruct((GY, TILES + 1, 8, L), jnp.float32),
         grid_spec=pltpu.PrefetchScalarGridSpec(
-            num_scalar_prefetch=3,
-            grid=(R // ROWS_STEP,),
+            num_scalar_prefetch=5,
+            grid=(R // ROWS_STEP + 1,),
             in_specs=[
-                pl.BlockSpec((ROWS_STEP, KA, WIDTH), lambda g, *_: (g, 0, 0)),
+                pl.BlockSpec((ROWS_STEP, KA, WIDTH), lambda g, *_: (jnp.minimum(g, R // ROWS_STEP - 1), 0, 0)),
                 pl.BlockSpec((R, WIDTH), lambda g, *_: (0, 0)),
             ],
             out_specs=pl.BlockSpec((GY, TILES + 1, 8, L), lambda g, *_: (0, 0, 0, 0)),
@@ -146,12 +148,13 @@
                 pltpu.VMEM((2, KA * STRIDE, L), jnp.float32),
                 pltpu.VMEM((R, B, L), jnp.bfloat16),
                 pltpu.VMEM((R, B, B), jnp.bfloat16),
-                pltpu.VMEM((NP * APART, L), jnp.float32),
+                pltpu.VMEM(((NP + 1) * APART, L), jnp.float32),
+                pltpu.VMEM((2, KA // 2, B, 2 * L), jnp.bfloat16),
             ],
         ),
         compiler_params=pltpu.CompilerParams(vmem_limit_bytes=58 << 20),
         name="fine",
-    )(pairs, code, me, a_blocks, q_blocks)
+    )(a_cols.T, part_of.T, part_dest.reshape(NP), part_pos, me, a_blocks, q_blocks)
 
 
 def split2(x):

time: 107 us -> 103 us (0.963)
  other arithmetic: 1.89 us -> 0 us
  Pallas kernels: 27 us -> 25.9 us
    add x2 -> x0, other arithmetic: 1.89 us -> none  [the longest x1 1.18 us: fine(): code = part_dest[:, 0] * CELLS + part_pos]
    pallas_call x1, Pallas kernels: 17.9 us -> 16.8 us  [fine(): pl.pallas_call(fine_kernel, out_shape=jax.ShapeDtypeStruct((GY, TILES + 1...]
where the time goes in v4:
time: 103 us
  blocking collectives  42.2 us (41%)
  Pallas kernels  25.9 us (25%)
  waiting for transfers between devices  23.6 us (23%)
  starting transfers between devices  9.41 us (9%)
    all_to_all x1, blocking collectives, local(): lax.all_to_all(slices, 'gy', split_axis=0, concat_axis=0, tiled=True)  42.2 us
    all_to_all x1, waiting for transfers between devices, local(): lax.all_to_all(outgoing, 'gy', split_axis=0, concat_axis=0, tiled=True)  17.4 us
    pallas_call x1, Pallas kernels, fine(): pl.pallas_call(fine_kernel, out_shape=jax.ShapeDtypeStruct((GY, TILES + 1...  16.8 us
    ppermute x3, waiting for transfers between devices, local(): lax.ppermute(group, 'gx', [(i, (i + d) % GX) for i in range(GX)])  6.13 us
    ppermute x3, starting transfers between devices, local(): lax.ppermute(group, 'gx', [(i, (i + d) % GX) for i in range(GX)])  5.03 us
    all_to_all x1, starting transfers between devices, local(): lax.all_to_all(outgoing, 'gy', split_axis=0, concat_axis=0, tiled=True)  4.38 us
    pallas_call x1, Pallas kernels, cells_of(): pl.pallas_call(cells_kernel, out_shape=(jax.ShapeDtypeStruct((3 * PER, L...  4.01 us
    pallas_call x1, Pallas kernels, close(): pl.pallas_call(close_kernel, out_shape=(out, out), scratch_shapes=[pltpu....  4 us
  transfers between devices with their start and end apart: 4, of which 3 were waited for; matrix products, arithmetic and copies ran while one was open for 1% of the time, Pallas kernels for 0%

profile of v4, /device:TPU:1, one launch (start us, length us, event | category | flops | bytes accessed | tf_op | source)
XLA Modules:
  0.0 102.8 jit_solution(17964346017302267215)
XLA Ops:
  0.6 16.8 %fine.1 = f32[32,19,8,128]{3,2,1,0:T(8,128)} custom-call(s32[8,64]{1,0:T(8,128)} %bitcast.10, s32[8,64]{1,0:T(8,128)} %bitcast.11, s32[64]{0:T(128)} %bitcast.12, s32[64]{0:T(128)} %pos.1, s32[1]{0:T(128)} %bitcast.3.me, bf16[64,8,9216]{2,1,0:T(8,128)(2,1)} %a_ref.1, bf16[64,9216]{1,0:T(8,128)(2,1)} %q_ref.1), custom_call_target="tpu_custom_call" | custom-call | tf_op jit(solution)/shard_map/fine/pallas_call | solution.py:136
  17.4 42.2 %all_to_all.10.y_ref = f32[32,19,8,128]{3,2,1,0:T(8,128)S(1)} all-to-all(f32[32,19,8,128]{3,2,1,0:T(8,128)} %fine.1), channel_id=1, replica_groups=mesh['gx'=4,'gy'=32] {'gy'}, dimensions={0} | all-to-all | bytes 4980736 | tf_op jit(solution)/shard_map/all_to_all | solution.py:325
  59.6 4.0 %cells.1 = (f32[9,136,128]{2,1,0:T(8,128)S(1)}, f32[9,32,128]{2,1,0:T(8,128)S(1)}) custom-call(f32[32,19,8,128]{3,2,1,0:T(8,128)S(1)} %all_to_all.10.y_ref), custom_call_target="tpu_custom_call" | custom-call | tf_op jit(solution)/shard_map/cells/pallas_call | solution.py:216
  63.6 0.0 copy-start
  63.6 1.3 %collective-permute-start = (f32[9,32,128]{2,1,0:T(8,128)S(1)}, f32[9,32,128]{2,1,0:T(8,128)S(1)}, u32[]{:S(2)}, u32[]{:S(2)}) collective-permute-start(f32[9,32,128]{2,1,0:T(8,128)S(1)} %get-tuple-element.5.t0), channel_id=1, source_target_pairs={{0,32},{32,64},{64,96},{96,0},{1,33},{33,65},{65,97},{97,1},{2,34}... | collective-permute-start | bytes 442376 | tf_op jit(solution)/shard_map/ppermute | solution.py:327
  65.0 2.6 %collective-permute-start.1 = (f32[9,32,128]{2,1,0:T(8,128)S(1)}, f32[9,32,128]{2,1,0:T(8,128)S(1)}, u32[]{:S(2)}, u32[]{:S(2)}) collective-permute-start(f32[9,32,128]{2,1,0:T(8,128)S(1)} %get-tuple-element.5.t0), channel_id=1, source_target_pairs={{0,64},{32,96},{64,0},{96,32},{1,65},{33,97},{65,1},{97,33},{2,66}... | collective-permute-start | bytes 442376 | tf_op jit(solution)/shard_map/ppermute | solution.py:327
  67.6 1.0 %collective-permute-start.2 = (f32[9,32,128]{2,1,0:T(8,128)S(1)}, f32[9,32,128]{2,1,0:T(8,128)S(1)}, u32[]{:S(2)}, u32[]{:S(2)}) collective-permute-start(f32[9,32,128]{2,1,0:T(8,128)S(1)} %get-tuple-element.5.t0), channel_id=1, source_target_pairs={{0,96},{32,0},{64,32},{96,64},{1,97},{33,1},{65,33},{97,65},{2,98}... | collective-permute-start | bytes 442376 | tf_op jit(solution)/shard_map/ppermute | solution.py:327
  68.7 1.9 %collective-permute-done.t1 = f32[9,32,128]{2,1,0:T(8,128)S(1)} collective-permute-done((f32[9,32,128]{2,1,0:T(8,128)S(1)}, f32[9,32,128]{2,1,0:T(8,128)S(1)}, u32[]{:S(2)}, u32[]{:S(2)}) %collective-permute-start) | collective-permute-done | bytes 147488 | tf_op jit(solution)/shard_map/ppermute | solution.py:327
  70.5 4.3 %collective-permute-done.1.t2 = f32[9,32,128]{2,1,0:T(8,128)S(1)} collective-permute-done((f32[9,32,128]{2,1,0:T(8,128)S(1)}, f32[9,32,128]{2,1,0:T(8,128)S(1)}, u32[]{:S(2)}, u32[]{:S(2)}) %collective-permute-start.1) | collective-permute-done | bytes 147488 | tf_op jit(solution)/shard_map/ppermute | solution.py:327
  74.8 0.0 collective-permute-done.2.t3
  74.8 1.1 %merge.1 = f32[32,9,8,128]{3,2,1,0:T(8,128)} custom-call(f32[9,136,128]{2,1,0:T(8,128)S(1)} %get-tuple-element.4.z_ref, f32[9,32,128]{2,1,0:T(8,128)S(1)} %get-tuple-element.5.t0, f32[9,32,128]{2,1,0:T(8,128)S(1)} %collective-permute-done.t1, f32[9,32,128]{2,1,0:T(8,128)S(1)} %collective-permute-done.1.t2, f32[9,32,128]{2,1,0:T(8,128)S(1)} %collective-permute-done.2.t3), custom_call_target="tpu_custom_call" | custom-call | tf_op jit(solution)/shard_map/merge/pallas_call | solution.py:243
  75.9 4.4 %all-to-all-start.1 = ((f32[32,9,8,128]{3,2,1,0:T(8,128)}), f32[32,9,8,128]{3,2,1,0:T(8,128)S(1)}, u32[]{:S(2)}, u32[]{:S(2)}) async-start(f32[32,9,8,128]{3,2,1,0:T(8,128)} %merge.1), calls=%async_computation.1 | async-start | bytes 2359296 | tf_op jit(solution)/shard_map/all_to_all | solution.py:329
  80.3 0.0 copy-done
  80.3 0.3 slice_reduce_fusion
  80.6 0.1 squeeze.10
  80.7 0.1 squeeze.9
  80.8 0.1 squeeze.11
  80.8 0.2 fusion
  81.0 0.2 fusion.1
  81.2 0.1 copy.9
  81.3 17.4 %all-to-all-done.1.w_ref = f32[32,9,8,128]{3,2,1,0:T(8,128)S(1)} async-done(((f32[32,9,8,128]{3,2,1,0:T(8,128)}), f32[32,9,8,128]{3,2,1,0:T(8,128)S(1)}, u32[]{:S(2)}, u32[]{:S(2)}) %all-to-all-start.1) | async-done | bytes 1179680 | tf_op jit(solution)/shard_map/all_to_all | solution.py:329
  98.8 4.0 %close.1 = (f32[2,8,9216]{2,1,0:T(8,128)}, f32[2,8,9216]{2,1,0:T(8,128)}) custom-call(f32[32,9,8,128]{3,2,1,0:T(8,128)S(1)} %all-to-all-done.1.w_ref, f32[128,128]{1,0:T(8,128)S(1)} %pad.4.h_ref, f32[96,96]{1,0:T(8,128)S(1)} %bitcast.9), custom_call_target="tpu_custom_call" | custom-call | tf_op jit(solution)/shard_map/close/pallas_call | solution.py:304
  (1 shorter events, 0.0 us)
Async XLA Ops:
  63.6 16.7 %copy-start = (f32[3,9216]{1,0:T(4,128)S(1)}, f32[3,9216]{1,0:T(4,128)}, u32[]{:S(2)}) copy-start(f32[3,9216]{1,0:T(4,128)} %param.13) | copy-start | bytes 331780
  63.6 6.9 %collective-permute-start = (f32[9,32,128]{2,1,0:T(8,128)S(1)}, f32[9,32,128]{2,1,0:T(8,128)S(1)}, u32[]{:S(2)}, u32[]{:S(2)}) collective-permute-start(f32[9,32,128]{2,1,0:T(8,128)S(1)} %get-tuple-element.5.t0), channel_id=1, source_target_pairs={{0,32},{32,64},{64,96},{96,0},{1,33},{33,65},{65,97},{97,1},{2,34}... | collective-permute-start | bytes 442376 | tf_op jit(solution)/shard_map/ppermute | solution.py:327
  65.0 9.8 %collective-permute-start.1 = (f32[9,32,128]{2,1,0:T(8,128)S(1)}, f32[9,32,128]{2,1,0:T(8,128)S(1)}, u32[]{:S(2)}, u32[]{:S(2)}) collective-permute-start(f32[9,32,128]{2,1,0:T(8,128)S(1)} %get-tuple-element.5.t0), channel_id=1, source_target_pairs={{0,64},{32,96},{64,0},{96,32},{1,65},{33,97},{65,1},{97,33},{2,66}... | collective-permute-start | bytes 442376 | tf_op jit(solution)/shard_map/ppermute | solution.py:327
  67.6 7.2 %collective-permute-start.2 = (f32[9,32,128]{2,1,0:T(8,128)S(1)}, f32[9,32,128]{2,1,0:T(8,128)S(1)}, u32[]{:S(2)}, u32[]{:S(2)}) collective-permute-start(f32[9,32,128]{2,1,0:T(8,128)S(1)} %get-tuple-element.5.t0), channel_id=1, source_target_pairs={{0,96},{32,0},{64,32},{96,64},{1,97},{33,1},{65,33},{97,65},{2,98}... | collective-permute-start | bytes 442376 | tf_op jit(solution)/shard_map/ppermute | solution.py:327
  75.9 22.8 %all-to-all-start.1 = ((f32[32,9,8,128]{3,2,1,0:T(8,128)}), f32[32,9,8,128]{3,2,1,0:T(8,128)S(1)}, u32[]{:S(2)}, u32[]{:S(2)}) async-start(f32[32,9,8,128]{3,2,1,0:T(8,128)} %merge.1), calls=%async_computation.1 | async-start | bytes 2359296 | tf_op jit(solution)/shard_map/all_to_all | solution.py:329

commit v5 on v4

--- a/solution.py
+++ b/solution.py
@@ -23,6 +23,7 @@
 STRIDE = 100
 GAP = 20
 M_ROWS = 512
+HALF = (3 * PER + 1) // 2
 APART = 104
 
 
@@ -162,7 +163,7 @@
     return hi, (x - hi.astype(jnp.float32)).astype(jnp.bfloat16)
 
 
-def cells_kernel(y_ref, z_ref, t_ref, x_ref, m_ref, g_ref):
+def cells_kernel(y_ref, z_ref, t_ref, x_ref, m_ref, g_ref, p_ref):
     wide = 2 * PER * L
 
     def one(s, carry):
@@ -206,77 +207,114 @@
         for a in range(PER):
             rows = [m_ref[pl.ds(pl.multiple_of(L * v + 16 * n, 16), 16), L * a:L * (a + 1)] for v in range(4)]
             for u, piece in enumerate(pack_rows(*rows)):
-                z_ref[3 * a + u, pl.ds(pl.multiple_of(16 * n, 16), 16), :] = piece
+                p_ref[3 * a + u, pl.ds(pl.multiple_of(16 * n + 8, 8), 16), :] = piece
         return carry
 
     lax.fori_loop(0, L // 16, pack, 0, unroll=2)
+    for d in range(GY):
+        for t in range(HALF):
+            z_ref[d, 8 * t:8 * t + 8, :] = two_halves(p_ref, t, 4 * d + 8)
+
+
+def two_halves(ref, t, at):
+    one = ref[2 * t, at:at + 8, :]
+    if 2 * t + 1 == 3 * PER:
+        return one
+    upper = lax.broadcasted_iota(jnp.int32, (8, L), 0) < 4
+    return jnp.where(upper, one, ref[2 * t + 1, at - 4:at + 4, :])
 
 
 def cells_of(received):
     return pl.pallas_call(
         cells_kernel,
         out_shape=(
-            jax.ShapeDtypeStruct((3 * PER, L + 8, L), jnp.float32),
+            jax.ShapeDtypeStruct((GY, 8 * HALF, L), jnp.float32),
             jax.ShapeDtypeStruct((3 * PER, L // 4, L), jnp.float32),
         ),
         scratch_shapes=[
             pltpu.VMEM((4 * 512, 2 * PER * L), jnp.bfloat16),
             pltpu.VMEM((4 * L, PER * L), jnp.float32),
             pltpu.VMEM((PER, 4, L // 4, L), jnp.float32),
+            pltpu.VMEM((3 * PER, L + 16, L), jnp.float32),
         ],
         compiler_params=pltpu.CompilerParams(vmem_limit_bytes=24 << 20),
         name="cells",
     )(received)
 
 
-def merge_kernel(z_ref, t0, t1, t2, t3, out_ref, s_ref):
-    upper = lax.broadcasted_iota(jnp.int32, (8, L), 0) < 4
+def merge_kernel(t0, t1, t2, t3, out_ref, s_ref):
     for n in range(3 * PER):
-        s_ref[n, 4:L // 4 + 4, :] = (t0[n] + t1[n]) + (t2[n] + t3[n])
-    for d in range(GY):
-        g = d // 4
-        for n in range(3 * PER):
-            out_ref[d, n] = jnp.where(upper, z_ref[n, 4 * d:4 * d + 8, :], s_ref[n, 4 * g:4 * g + 8, :])
-
-
-def merge(mine, parts):
+        s_ref[n, 8:L // 4 + 8, :] = (t0[n] + t1[n]) + (t2[n] + t3[n])
+    for g in range(GY // 4):
+        for t in range(HALF):
+            tile = two_halves(s_ref, t, 4 * g + 8)
+            for m in range(4):
+                out_ref[4 * g + m, 8 * t:8 * t + 8, :] = tile
+
+
+def merge(*parts):
     return pl.pallas_call(
         merge_kernel,
-        out_shape=jax.ShapeDtypeStruct((GY, 3 * PER, 8, L), jnp.float32),
-        scratch_shapes=[pltpu.VMEM((3 * PER, L // 4 + 8, L), jnp.float32)],
+        out_shape=jax.ShapeDtypeStruct((GY, 8 * HALF, L), jnp.float32),
+        scratch_shapes=[pltpu.VMEM((3 * PER, L // 4 + 16, L), jnp.float32)],
         compiler_params=pltpu.CompilerParams(vmem_limit_bytes=8 << 20),
+        cost_estimate=pl.CostEstimate(flops=1 << 20, bytes_accessed=2 << 20, transcendentals=0),
         name="merge",
-    )(mine, *parts)
-
-
-def close_kernel(w_ref, h_ref, ht_ref, first_ref, last_ref, f_ref, hi_ref, lo_ref, r_ref, o_ref):
+    )(*parts)
+
+
+def spread_cells(w_ref, f_ref):
     upper = lax.broadcasted_iota(jnp.int32, (8, L), 0) < 4
 
-    def spread(w, carry):
+    def pair(n, carry):
+        w = 2 * n
         for a in range(PER):
-            rows = unpack_rows(*[w_ref[w, 3 * a + u] for u in range(3)])
-            for v in range(4):
-                f_ref[v, pl.ds(pl.multiple_of((w * PER + a) * 8 + 8, 8), 8), :] = rows[v]
-        return carry
-
-    lax.fori_loop(0, GY, spread, 0, unroll=4)
-
-    def outputs(j, carry):
-        lanes = [pl.ds(pl.multiple_of(384 * j + L * u, L), L) for u in range(3)]
-        base = pl.multiple_of(32 * j + 8, 8)
-        for half in range(RC):
-            rows = [jnp.where(upper, f_ref[2 * half, pl.ds(base + 8 * v, 8), :], f_ref[2 * half + 1, pl.ds(base + 8 * v - 4, 8), :]) for v in range(4)]
-            for u, piece in enumerate(pack_rows(*rows)):
-                first_ref[half, :, lanes[u]] = piece
-        for v in range(4):
-            both = [jnp.where(upper, f_ref[2 * half, pl.ds(base + 8 * v + 4, 8), :], f_ref[2 * half + 1, pl.ds(base + 8 * v, 8), :]) for half in range(RC)]
-            hi, lo = split2(jnp.concatenate(both, axis=0))
-            at = pl.ds(pl.multiple_of(64 * j + 16 * v, 16), 16)
-            hi_ref[at, :] = hi
-            lo_ref[at, :] = lo
-        return carry
-
-    lax.fori_loop(0, B // 4, outputs, 0, unroll=2)
+            at = []
+            for u in range(3):
+                k = 4 * (3 * a + u)
+                other = w_ref[w + 1, k - 4:k + 4, :] if k else pltpu.roll(w_ref[w + 1, 0:8, :], 4, 0)
+                at.append(jnp.where(upper, w_ref[w, k:k + 8, :], other))
+            for v, rows in enumerate(unpack_rows(*at)):
+                f_ref[v, a, pl.ds(pl.multiple_of(8 * n + 8, 8), 8), :] = rows
+        return carry
+
+    lax.fori_loop(0, GY // 2, pair, 0, unroll=4)
+
+
+def cell_rows(f_ref, w, a, half):
+    upper = lax.broadcasted_iota(jnp.int32, (8, L), 0) < 4
+    return jnp.where(upper, f_ref[2 * half, a, pl.ds(4 * w + 8, 8), :], f_ref[2 * half + 1, a, pl.ds(4 * w + 4, 8), :])
+
+
+def first_kernel(w_ref, first_ref, f_ref):
+    spread_cells(w_ref, f_ref)
+
+    def outputs(n, carry):
+        for j in range(PER):
+            lanes = [pl.ds(pl.multiple_of(384 * (PER * n + j) + L * u, L), L) for u in range(3)]
+            for half in range(RC):
+                rows = [cell_rows(f_ref, 4 * n + (4 * j + v) // PER, (4 * j + v) % PER, half) for v in range(4)]
+                for u, piece in enumerate(pack_rows(*rows)):
+                    first_ref[half, :, lanes[u]] = piece
+        return carry
+
+    lax.fori_loop(0, GY // 4, outputs, 0)
+
+
+def close_kernel(w_ref, h_ref, ht_ref, last_ref, f_ref, hi_ref, lo_ref, r_ref, o_ref):
+    spread_cells(w_ref, f_ref)
+
+    def pieces(n, carry):
+        for i in range(2):
+            for a in range(PER):
+                w = 2 * n + i
+                hi, lo = split2(jnp.concatenate([cell_rows(f_ref, w, a, half) for half in range(RC)], axis=0))
+                at = pl.ds(pl.multiple_of(CELLS * (PER * w + a), CELLS), CELLS)
+                hi_ref[at, :] = hi
+                lo_ref[at, :] = lo
+        return carry
+
+    lax.fori_loop(0, GY // 2, pieces, 0)
     h_hi, h_lo = split2(h_ref[...])
     t_hi, t_lo = split2(ht_ref[...])
     dot = functools.partial(jnp.dot, preferred_element_type=jnp.float32)
@@ -299,21 +337,15 @@
                 last_ref[half, :, 384 * j + L * u:384 * j + L * (u + 1)] = piece
 
 
-def close(received, h, ht):
-    out = jax.ShapeDtypeStruct((RC, SC, WIDTH), jnp.float32)
+def finish(kernel, name, scratch, *operands):
     return pl.pallas_call(
-        close_kernel,
-        out_shape=(out, out),
-        scratch_shapes=[
-            pltpu.VMEM((4, B * 8 + 16, L), jnp.float32),
-            pltpu.VMEM((B * CELLS, L), jnp.bfloat16),
-            pltpu.VMEM((B * CELLS, L), jnp.bfloat16),
-            pltpu.VMEM((B * GAP, L), jnp.float32),
-            pltpu.VMEM((B * GAP, L), jnp.float32),
-        ],
+        kernel,
+        out_shape=jax.ShapeDtypeStruct((RC, SC, WIDTH), jnp.float32),
+        scratch_shapes=[pltpu.VMEM((4, PER, 4 * GY + 16, L), jnp.float32)] + scratch,
         compiler_params=pltpu.CompilerParams(vmem_limit_bytes=16 << 20),
-        name="close",
-    )(received, h, ht)
+        cost_estimate=pl.CostEstimate(flops=1 << 20, bytes_accessed=4 << 20, transcendentals=0),
+        name=name,
+    )(*operands)
 
 
 def local(a_blocks, a_cols, q_blocks, part_of, part_dest, part_pos, g_level):
@@ -325,9 +357,13 @@
     gathered = lax.all_to_all(slices, "gy", split_axis=0, concat_axis=0, tiled=True)
     mine, group = cells_of(gathered)
     others = [lax.ppermute(group, "gx", [(i, (i + d) % GX) for i in range(GX)]) for d in range(1, GX)]
-    outgoing = merge(mine, [group] + others)
-    back = lax.all_to_all(outgoing, "gy", split_axis=0, concat_axis=0, tiled=True)
-    return close(back, jnp.pad(h, ((0, L - B), (0, L - B))), h.T)
+    send = functools.partial(lax.all_to_all, axis_name="gy", split_axis=0, concat_axis=0, tiled=True)
+    first = send(mine)
+    total = send(merge(group, *others))
+    coarse = finish(first_kernel, "first", [], first)
+    scratch = [pltpu.VMEM((B * CELLS, L), jnp.bfloat16)] * 2 + [pltpu.VMEM((B * GAP, L), jnp.float32)] * 2
+    last = finish(close_kernel, "close", scratch, total, jnp.pad(h, ((0, L - B), (0, L - B))), h.T)
+    return coarse, last
 
 
 def solution(mesh):

time: 103 us -> 104 us (level)
  waiting for transfers between devices: 23.6 us -> 16.6 us
  starting transfers between devices: 9.41 us -> 15.9 us
  Pallas kernels: 25.9 us -> 27.3 us
    all_to_all x1 -> x2, waiting for transfers between devices: 17.4 us -> 10.7 us  [the longest x1 9.85 us: local(): total = send(merge(group, *others))]
    all_to_all x1 -> x2, starting transfers between devices: 4.38 us -> 10.8 us  [the longest x1 7 us: local(): total = send(merge(group, *others))]
    pallas_call x3 -> x4, Pallas kernels: 9.14 us -> 10.5 us  [the longest x1 4.91 us: cells_of(): pl.pallas_call(cells_kernel, out_shape=(jax.ShapeDtypeStruct((GY, 8 * HAL...]
  transfers between devices with their start and end apart: 4 -> 5, of which waited for: 3 -> 4; matrix products, arithmetic and copies ran while one was open for 1% -> 1% of each run, Pallas kernels for 0% -> 3%
where the time goes in v5:
time: 104 us
  blocking collectives  42.1 us (40%)
  Pallas kernels  27.3 us (26%)
  waiting for transfers between devices  16.6 us (16%)
  starting transfers between devices  15.9 us (15%)
    all_to_all x1, blocking collectives, local(): lax.all_to_all(slices, 'gy', split_axis=0, concat_axis=0, tiled=True)  42.1 us
    pallas_call x1, Pallas kernels, fine(): pl.pallas_call(fine_kernel, out_shape=jax.ShapeDtypeStruct((GY, TILES + 1...  16.8 us
    all_to_all x1, waiting for transfers between devices, local(): total = send(merge(group, *others))  9.85 us
    all_to_all x1, starting transfers between devices, local(): total = send(merge(group, *others))  7 us
    ppermute x3, waiting for transfers between devices, local(): lax.ppermute(group, 'gx', [(i, (i + d) % GX) for i in range(GX)])  5.9 us
    ppermute x3, starting transfers between devices, local(): lax.ppermute(group, 'gx', [(i, (i + d) % GX) for i in range(GX)])  5.09 us
    pallas_call x1, Pallas kernels, cells_of(): pl.pallas_call(cells_kernel, out_shape=(jax.ShapeDtypeStruct((GY, 8 * HAL...  4.91 us
    pallas_call x2, Pallas kernels, finish(): pl.pallas_call(kernel, out_shape=jax.ShapeDtypeStruct((RC, SC, WIDTH), jn...  4.71 us
  transfers between devices with their start and end apart: 5, of which 4 were waited for; matrix products, arithmetic and copies ran while one was open for 1% of the time, Pallas kernels for 3%

profile of v5, /device:TPU:1, one launch (start us, length us, event | category | flops | bytes accessed | tf_op | source)
XLA Modules:
  0.0 103.7 jit_solution(6603131779587512657)
XLA Ops:
  0.6 16.8 %fine.1 = f32[32,19,8,128]{3,2,1,0:T(8,128)} custom-call(s32[8,64]{1,0:T(8,128)} %bitcast.10, s32[8,64]{1,0:T(8,128)} %bitcast.11, s32[64]{0:T(128)} %bitcast.12, s32[64]{0:T(128)} %pos.1, s32[1]{0:T(128)} %bitcast.3.me, bf16[64,8,9216]{2,1,0:T(8,128)(2,1)} %a_ref.1, bf16[64,9216]{1,0:T(8,128)(2,1)} %q_ref.1), custom_call_target="tpu_custom_call" | custom-call | tf_op jit(solution)/shard_map/fine/pallas_call | solution.py:137
  17.4 42.1 %all_to_all.15.y_ref = f32[32,19,8,128]{3,2,1,0:T(8,128)S(1)} all-to-all(f32[32,19,8,128]{3,2,1,0:T(8,128)} %fine.1), channel_id=1, replica_groups=mesh['gx'=4,'gy'=32] {'gy'}, dimensions={0} | all-to-all | bytes 4980736 | tf_op jit(solution)/shard_map/all_to_all | solution.py:357
  59.6 4.9 %cells.1 = (f32[32,40,128]{2,1,0:T(8,128)}, f32[9,32,128]{2,1,0:T(8,128)S(1)}) custom-call(f32[32,19,8,128]{3,2,1,0:T(8,128)S(1)} %all_to_all.15.y_ref), custom_call_target="tpu_custom_call" | custom-call | tf_op jit(solution)/shard_map/cells/pallas_call | solution.py:228
  64.5 3.8 %all-to-all-start.1 = ((f32[32,40,128]{2,1,0:T(8,128)}), f32[32,40,128]{2,1,0:T(8,128)S(1)}, u32[]{:S(2)}, u32[]{:S(2)}) async-start(f32[32,40,128]{2,1,0:T(8,128)} %get-tuple-element.4), calls=%async_computation.1 | async-start | bytes 1310720 | tf_op jit(solution)/shard_map/all_to_all | solution.py:361
  68.3 1.4 %collective-permute-start = (f32[9,32,128]{2,1,0:T(8,128)S(1)}, f32[9,32,128]{2,1,0:T(8,128)S(1)}, u32[]{:S(2)}, u32[]{:S(2)}) collective-permute-start(f32[9,32,128]{2,1,0:T(8,128)S(1)} %get-tuple-element.5.t0), channel_id=1, source_target_pairs={{0,32},{32,64},{64,96},{96,0},{1,33},{33,65},{65,97},{97,1},{2,34}... | collective-permute-start | bytes 442376 | tf_op jit(solution)/shard_map/ppermute | solution.py:359
  69.7 2.6 %collective-permute-start.1 = (f32[9,32,128]{2,1,0:T(8,128)S(1)}, f32[9,32,128]{2,1,0:T(8,128)S(1)}, u32[]{:S(2)}, u32[]{:S(2)}) collective-permute-start(f32[9,32,128]{2,1,0:T(8,128)S(1)} %get-tuple-element.5.t0), channel_id=1, source_target_pairs={{0,64},{32,96},{64,0},{96,32},{1,65},{33,97},{65,1},{97,33},{2,66}... | collective-permute-start | bytes 442376 | tf_op jit(solution)/shard_map/ppermute | solution.py:359
  72.3 1.1 %collective-permute-start.2 = (f32[9,32,128]{2,1,0:T(8,128)S(1)}, f32[9,32,128]{2,1,0:T(8,128)S(1)}, u32[]{:S(2)}, u32[]{:S(2)}) collective-permute-start(f32[9,32,128]{2,1,0:T(8,128)S(1)} %get-tuple-element.5.t0), channel_id=1, source_target_pairs={{0,96},{32,0},{64,32},{96,64},{1,97},{33,1},{65,33},{97,65},{2,98}... | collective-permute-start | bytes 442376 | tf_op jit(solution)/shard_map/ppermute | solution.py:359
  73.4 1.7 %collective-permute-done.t1 = f32[9,32,128]{2,1,0:T(8,128)S(1)} collective-permute-done((f32[9,32,128]{2,1,0:T(8,128)S(1)}, f32[9,32,128]{2,1,0:T(8,128)S(1)}, u32[]{:S(2)}, u32[]{:S(2)}) %collective-permute-start) | collective-permute-done | bytes 147488 | tf_op jit(solution)/shard_map/ppermute | solution.py:359
  75.1 4.2 %collective-permute-done.1.t2 = f32[9,32,128]{2,1,0:T(8,128)S(1)} collective-permute-done((f32[9,32,128]{2,1,0:T(8,128)S(1)}, f32[9,32,128]{2,1,0:T(8,128)S(1)}, u32[]{:S(2)}, u32[]{:S(2)}) %collective-permute-start.1) | collective-permute-done | bytes 147488 | tf_op jit(solution)/shard_map/ppermute | solution.py:359
  79.3 0.0 collective-permute-done.2.t3
  79.3 0.9 merge.1
  80.2 0.9 all-to-all-done.1.w_ref
  81.1 7.0 %all-to-all-start.2 = ((f32[32,40,128]{2,1,0:T(8,128)}), f32[32,40,128]{2,1,0:T(8,128)S(1)}, u32[]{:S(2)}, u32[]{:S(2)}) async-start(f32[32,40,128]{2,1,0:T(8,128)} %merge.1), calls=%async_computation.2 | async-start | bytes 1310720 | tf_op jit(solution)/shard_map/all_to_all | solution.py:362
  88.1 0.0 copy-done
  88.1 0.3 slice_reduce_fusion
  88.4 0.1 squeeze.10
  88.5 0.1 squeeze.9
  88.6 0.1 squeeze.11
  88.6 0.2 fusion
  88.8 0.2 fusion.1
  89.0 0.1 copy.9
  89.1 2.0 %first.1 = f32[2,8,9216]{2,1,0:T(8,128)} custom-call(f32[32,40,128]{2,1,0:T(8,128)S(1)} %all-to-all-done.1.w_ref), custom_call_target="tpu_custom_call" | custom-call | flops 1048576 | bytes 4194304 | tf_op jit(solution)/shard_map/first/pallas_call | solution.py:341
  91.2 9.9 %all-to-all-done.2.w_ref = f32[32,40,128]{2,1,0:T(8,128)S(1)} async-done(((f32[32,40,128]{2,1,0:T(8,128)}), f32[32,40,128]{2,1,0:T(8,128)S(1)}, u32[]{:S(2)}, u32[]{:S(2)}) %all-to-all-start.2) | async-done | bytes 655392 | tf_op jit(solution)/shard_map/all_to_all | solution.py:362
  101.0 2.7 %close.1 = f32[2,8,9216]{2,1,0:T(8,128)} custom-call(f32[32,40,128]{2,1,0:T(8,128)S(1)} %all-to-all-done.2.w_ref, f32[128,128]{1,0:T(8,128)S(1)} %pad.4.h_ref, f32[96,96]{1,0:T(8,128)S(1)} %bitcast.9), custom_call_target="tpu_custom_call" | custom-call | flops 1048576 | bytes 4194304 | tf_op jit(solution)/shard_map/close/pallas_call | solution.py:341
  (2 shorter events, 0.0 us)
Async XLA Ops:
  64.5 23.6 %copy-start = (f32[3,9216]{1,0:T(4,128)S(1)}, f32[3,9216]{1,0:T(4,128)}, u32[]{:S(2)}) copy-start(f32[3,9216]{1,0:T(4,128)} %param.13) | copy-start | bytes 331780
  64.5 16.6 %all-to-all-start.1 = ((f32[32,40,128]{2,1,0:T(8,128)}), f32[32,40,128]{2,1,0:T(8,128)S(1)}, u32[]{:S(2)}, u32[]{:S(2)}) async-start(f32[32,40,128]{2,1,0:T(8,128)} %get-tuple-element.4), calls=%async_computation.1 | async-start | bytes 1310720 | tf_op jit(solution)/shard_map/all_to_all | solution.py:361
  68.3 6.8 %collective-permute-start = (f32[9,32,128]{2,1,0:T(8,128)S(1)}, f32[9,32,128]{2,1,0:T(8,128)S(1)}, u32[]{:S(2)}, u32[]{:S(2)}) collective-permute-start(f32[9,32,128]{2,1,0:T(8,128)S(1)} %get-tuple-element.5.t0), channel_id=1, source_target_pairs={{0,32},{32,64},{64,96},{96,0},{1,33},{33,65},{65,97},{97,1},{2,34}... | collective-permute-start | bytes 442376 | tf_op jit(solution)/shard_map/ppermute | solution.py:359
  69.7 9.6 %collective-permute-start.1 = (f32[9,32,128]{2,1,0:T(8,128)S(1)}, f32[9,32,128]{2,1,0:T(8,128)S(1)}, u32[]{:S(2)}, u32[]{:S(2)}) collective-permute-start(f32[9,32,128]{2,1,0:T(8,128)S(1)} %get-tuple-element.5.t0), channel_id=1, source_target_pairs={{0,64},{32,96},{64,0},{96,32},{1,65},{33,97},{65,1},{97,33},{2,66}... | collective-permute-start | bytes 442376 | tf_op jit(solution)/shard_map/ppermute | solution.py:359
  72.3 7.0 %collective-permute-start.2 = (f32[9,32,128]{2,1,0:T(8,128)S(1)}, f32[9,32,128]{2,1,0:T(8,128)S(1)}, u32[]{:S(2)}, u32[]{:S(2)}) collective-permute-start(f32[9,32,128]{2,1,0:T(8,128)S(1)} %get-tuple-element.5.t0), channel_id=1, source_target_pairs={{0,96},{32,0},{64,32},{96,64},{1,97},{33,1},{65,33},{97,65},{2,98}... | collective-permute-start | bytes 442376 | tf_op jit(solution)/shard_map/ppermute | solution.py:359
  81.1 19.9 %all-to-all-start.2 = ((f32[32,40,128]{2,1,0:T(8,128)}), f32[32,40,128]{2,1,0:T(8,128)S(1)}, u32[]{:S(2)}, u32[]{:S(2)}) async-start(f32[32,40,128]{2,1,0:T(8,128)} %merge.1), calls=%async_computation.2 | async-start | bytes 1310720 | tf_op jit(solution)/shard_map/all_to_all | solution.py:362

commit v6 on v5

--- a/solution.py
+++ b/solution.py
@@ -337,14 +337,13 @@
                 last_ref[half, :, 384 * j + L * u:384 * j + L * (u + 1)] = piece
 
 
-def finish(kernel, name, scratch, *operands):
+def finish(kernel, scratch, *operands):
     return pl.pallas_call(
         kernel,
         out_shape=jax.ShapeDtypeStruct((RC, SC, WIDTH), jnp.float32),
         scratch_shapes=[pltpu.VMEM((4, PER, 4 * GY + 16, L), jnp.float32)] + scratch,
         compiler_params=pltpu.CompilerParams(vmem_limit_bytes=16 << 20),
         cost_estimate=pl.CostEstimate(flops=1 << 20, bytes_accessed=4 << 20, transcendentals=0),
-        name=name,
     )(*operands)
 
 
@@ -353,16 +352,16 @@
     g = g_level.reshape(3, B, B)
     mm = functools.partial(jnp.dot, precision=lax.Precision.HIGHEST)
     h = mm(mm(g[0], g[1]), g[2])
-    slices = fine(a_blocks, a_cols, q_blocks, part_of, part_dest, part_pos, me)
-    gathered = lax.all_to_all(slices, "gy", split_axis=0, concat_axis=0, tiled=True)
-    mine, group = cells_of(gathered)
-    others = [lax.ppermute(group, "gx", [(i, (i + d) % GX) for i in range(GX)]) for d in range(1, GX)]
     send = functools.partial(lax.all_to_all, axis_name="gy", split_axis=0, concat_axis=0, tiled=True)
+    mine, group = cells_of(send(fine(a_blocks, a_cols, q_blocks, part_of, part_dest, part_pos, me)))
+    others = []
+    for d in range(1, GX):
+        others.append(lax.ppermute(group, "gx", [(i, (i + d) % GX) for i in range(GX)]))
     first = send(mine)
     total = send(merge(group, *others))
-    coarse = finish(first_kernel, "first", [], first)
+    coarse = finish(first_kernel, [], first)
     scratch = [pltpu.VMEM((B * CELLS, L), jnp.bfloat16)] * 2 + [pltpu.VMEM((B * GAP, L), jnp.float32)] * 2
-    last = finish(close_kernel, "close", scratch, total, jnp.pad(h, ((0, L - B), (0, L - B))), h.T)
+    last = finish(close_kernel, scratch, total, jnp.pad(h, ((0, L - B), (0, L - B))), h.T)
     return coarse, last
 
 

time: 104 us -> 104 us (level)
  no operation moved by 1% of the time
where the time goes in v6:
time: 104 us
  blocking collectives  42.2 us (41%)
  Pallas kernels  27.3 us (26%)
  waiting for transfers between devices  16.7 us (16%)
  starting transfers between devices  15.8 us (15%)
    all_to_all x1, blocking collectives, local(): send(fine(a_blocks, a_cols, q_blocks, part_of, part_dest, part_pos, me))  42.2 us
    pallas_call x1, Pallas kernels, fine(): pl.pallas_call(fine_kernel, out_shape=jax.ShapeDtypeStruct((GY, TILES + 1...  16.8 us
    all_to_all x1, waiting for transfers between devices, local(): total = send(merge(group, *others))  9.85 us
    all_to_all x1, starting transfers between devices, local(): total = send(merge(group, *others))  6.92 us
    ppermute x3, waiting for transfers between devices, local(): lax.ppermute(group, 'gx', [(i, (i + d) % GX) for i in range(GX)])  5.85 us
    ppermute x3, starting transfers between devices, local(): lax.ppermute(group, 'gx', [(i, (i + d) % GX) for i in range(GX)])  5.06 us
    pallas_call x1, Pallas kernels, cells_of(): pl.pallas_call(cells_kernel, out_shape=(jax.ShapeDtypeStruct((GY, 8 * HAL...  4.92 us
    pallas_call x2, Pallas kernels, finish(): pl.pallas_call(kernel, out_shape=jax.ShapeDtypeStruct((RC, SC, WIDTH), jn...  4.71 us
  transfers between devices with their start and end apart: 5, of which 4 were waited for; matrix products, arithmetic and copies ran while one was open for 1% of the time, Pallas kernels for 3%

profile of v6, /device:TPU:1, one launch (start us, length us, event | category | flops | bytes accessed | tf_op | source)
XLA Modules:
  0.0 103.6 jit_solution(6603131779587512657)
XLA Ops:
  0.6 16.8 %fine.1 = f32[32,19,8,128]{3,2,1,0:T(8,128)} custom-call(s32[8,64]{1,0:T(8,128)} %bitcast.10, s32[8,64]{1,0:T(8,128)} %bitcast.11, s32[64]{0:T(128)} %bitcast.12, s32[64]{0:T(128)} %pos.1, s32[1]{0:T(128)} %bitcast.3.me, bf16[64,8,9216]{2,1,0:T(8,128)(2,1)} %a_ref.1, bf16[64,9216]{1,0:T(8,128)(2,1)} %q_ref.1), custom_call_target="tpu_custom_call" | custom-call | tf_op jit(solution)/shard_map/fine/pallas_call | solution.py:137
  17.4 42.2 %all_to_all.15.y_ref = f32[32,19,8,128]{3,2,1,0:T(8,128)S(1)} all-to-all(f32[32,19,8,128]{3,2,1,0:T(8,128)} %fine.1), channel_id=1, replica_groups=mesh['gx'=4,'gy'=32] {'gy'}, dimensions={0} | all-to-all | bytes 4980736 | tf_op jit(solution)/shard_map/all_to_all | solution.py:356
  59.6 4.9 %cells.1 = (f32[32,40,128]{2,1,0:T(8,128)}, f32[9,32,128]{2,1,0:T(8,128)S(1)}) custom-call(f32[32,19,8,128]{3,2,1,0:T(8,128)S(1)} %all_to_all.15.y_ref), custom_call_target="tpu_custom_call" | custom-call | tf_op jit(solution)/shard_map/cells/pallas_call | solution.py:228
  64.5 3.8 %all-to-all-start.1 = ((f32[32,40,128]{2,1,0:T(8,128)}), f32[32,40,128]{2,1,0:T(8,128)S(1)}, u32[]{:S(2)}, u32[]{:S(2)}) async-start(f32[32,40,128]{2,1,0:T(8,128)} %get-tuple-element.4), calls=%async_computation.1 | async-start | bytes 1310720 | tf_op jit(solution)/shard_map/all_to_all | solution.py:360
  68.3 1.4 %collective-permute-start = (f32[9,32,128]{2,1,0:T(8,128)S(1)}, f32[9,32,128]{2,1,0:T(8,128)S(1)}, u32[]{:S(2)}, u32[]{:S(2)}) collective-permute-start(f32[9,32,128]{2,1,0:T(8,128)S(1)} %get-tuple-element.5.t0), channel_id=1, source_target_pairs={{0,32},{32,64},{64,96},{96,0},{1,33},{33,65},{65,97},{97,1},{2,34}... | collective-permute-start | bytes 442376 | tf_op jit(solution)/shard_map/ppermute | solution.py:359
  69.7 2.6 %collective-permute-start.1 = (f32[9,32,128]{2,1,0:T(8,128)S(1)}, f32[9,32,128]{2,1,0:T(8,128)S(1)}, u32[]{:S(2)}, u32[]{:S(2)}) collective-permute-start(f32[9,32,128]{2,1,0:T(8,128)S(1)} %get-tuple-element.5.t0), channel_id=1, source_target_pairs={{0,64},{32,96},{64,0},{96,32},{1,65},{33,97},{65,1},{97,33},{2,66}... | collective-permute-start | bytes 442376 | tf_op jit(solution)/shard_map/ppermute | solution.py:359
  72.3 1.1 %collective-permute-start.2 = (f32[9,32,128]{2,1,0:T(8,128)S(1)}, f32[9,32,128]{2,1,0:T(8,128)S(1)}, u32[]{:S(2)}, u32[]{:S(2)}) collective-permute-start(f32[9,32,128]{2,1,0:T(8,128)S(1)} %get-tuple-element.5.t0), channel_id=1, source_target_pairs={{0,96},{32,0},{64,32},{96,64},{1,97},{33,1},{65,33},{97,65},{2,98}... | collective-permute-start | bytes 442376 | tf_op jit(solution)/shard_map/ppermute | solution.py:359
  73.4 1.5 %collective-permute-done.t1 = f32[9,32,128]{2,1,0:T(8,128)S(1)} collective-permute-done((f32[9,32,128]{2,1,0:T(8,128)S(1)}, f32[9,32,128]{2,1,0:T(8,128)S(1)}, u32[]{:S(2)}, u32[]{:S(2)}) %collective-permute-start) | collective-permute-done | bytes 147488 | tf_op jit(solution)/shard_map/ppermute | solution.py:359
  74.9 4.3 %collective-permute-done.1.t2 = f32[9,32,128]{2,1,0:T(8,128)S(1)} collective-permute-done((f32[9,32,128]{2,1,0:T(8,128)S(1)}, f32[9,32,128]{2,1,0:T(8,128)S(1)}, u32[]{:S(2)}, u32[]{:S(2)}) %collective-permute-start.1) | collective-permute-done | bytes 147488 | tf_op jit(solution)/shard_map/ppermute | solution.py:359
  79.2 0.0 collective-permute-done.2.t3
  79.2 0.9 merge.1
  80.2 1.0 all-to-all-done.1.w_ref
  81.1 6.9 %all-to-all-start.2 = ((f32[32,40,128]{2,1,0:T(8,128)}), f32[32,40,128]{2,1,0:T(8,128)S(1)}, u32[]{:S(2)}, u32[]{:S(2)}) async-start(f32[32,40,128]{2,1,0:T(8,128)} %merge.1), calls=%async_computation.2 | async-start | bytes 1310720 | tf_op jit(solution)/shard_map/all_to_all | solution.py:361
  88.1 0.0 copy-done
  88.1 0.3 slice_reduce_fusion
  88.4 0.1 squeeze.10
  88.4 0.1 squeeze.9
  88.5 0.1 squeeze.11
  88.6 0.2 fusion
  88.8 0.2 fusion.1
  89.0 0.1 copy.9
  89.1 2.0 %shard_map.86 = f32[2,8,9216]{2,1,0:T(8,128)} custom-call(f32[32,40,128]{2,1,0:T(8,128)S(1)} %all-to-all-done.1.w_ref), custom_call_target="tpu_custom_call" | custom-call | flops 1048576 | bytes 4194304 | tf_op jit(solution)/shard_map/pallas_call | solution.py:341
  91.1 9.9 %all-to-all-done.2.w_ref = f32[32,40,128]{2,1,0:T(8,128)S(1)} async-done(((f32[32,40,128]{2,1,0:T(8,128)}), f32[32,40,128]{2,1,0:T(8,128)S(1)}, u32[]{:S(2)}, u32[]{:S(2)}) %all-to-all-start.2) | async-done | bytes 655392 | tf_op jit(solution)/shard_map/all_to_all | solution.py:361
  101.0 2.7 %shard_map.87 = f32[2,8,9216]{2,1,0:T(8,128)} custom-call(f32[32,40,128]{2,1,0:T(8,128)S(1)} %all-to-all-done.2.w_ref, f32[128,128]{1,0:T(8,128)S(1)} %pad.4.h_ref, f32[96,96]{1,0:T(8,128)S(1)} %bitcast.9), custom_call_target="tpu_custom_call" | custom-call | flops 1048576 | bytes 4194304 | tf_op jit(solution)/shard_map/pallas_call | solution.py:341
  (2 shorter events, 0.0 us)
Async XLA Ops:
  64.5 23.6 %copy-start = (f32[3,9216]{1,0:T(4,128)S(1)}, f32[3,9216]{1,0:T(4,128)}, u32[]{:S(2)}) copy-start(f32[3,9216]{1,0:T(4,128)} %param.13) | copy-start | bytes 331780
  64.5 16.6 %all-to-all-start.1 = ((f32[32,40,128]{2,1,0:T(8,128)}), f32[32,40,128]{2,1,0:T(8,128)S(1)}, u32[]{:S(2)}, u32[]{:S(2)}) async-start(f32[32,40,128]{2,1,0:T(8,128)} %get-tuple-element.4), calls=%async_computation.1 | async-start | bytes 1310720 | tf_op jit(solution)/shard_map/all_to_all | solution.py:360
  68.3 6.6 %collective-permute-start = (f32[9,32,128]{2,1,0:T(8,128)S(1)}, f32[9,32,128]{2,1,0:T(8,128)S(1)}, u32[]{:S(2)}, u32[]{:S(2)}) collective-permute-start(f32[9,32,128]{2,1,0:T(8,128)S(1)} %get-tuple-element.5.t0), channel_id=1, source_target_pairs={{0,32},{32,64},{64,96},{96,0},{1,33},{33,65},{65,97},{97,1},{2,34}... | collective-permute-start | bytes 442376 | tf_op jit(solution)/shard_map/ppermute | solution.py:359
  69.7 9.5 %collective-permute-start.1 = (f32[9,32,128]{2,1,0:T(8,128)S(1)}, f32[9,32,128]{2,1,0:T(8,128)S(1)}, u32[]{:S(2)}, u32[]{:S(2)}) collective-permute-start(f32[9,32,128]{2,1,0:T(8,128)S(1)} %get-tuple-element.5.t0), channel_id=1, source_target_pairs={{0,64},{32,96},{64,0},{96,32},{1,65},{33,97},{65,1},{97,33},{2,66}... | collective-permute-start | bytes 442376 | tf_op jit(solution)/shard_map/ppermute | solution.py:359
  72.3 7.0 %collective-permute-start.2 = (f32[9,32,128]{2,1,0:T(8,128)S(1)}, f32[9,32,128]{2,1,0:T(8,128)S(1)}, u32[]{:S(2)}, u32[]{:S(2)}) collective-permute-start(f32[9,32,128]{2,1,0:T(8,128)S(1)} %get-tuple-element.5.t0), channel_id=1, source_target_pairs={{0,96},{32,0},{64,32},{96,64},{1,97},{33,1},{65,33},{97,65},{2,98}... | collective-permute-start | bytes 442376 | tf_op jit(solution)/shard_map/ppermute | solution.py:359
  81.1 19.8 %all-to-all-start.2 = ((f32[32,40,128]{2,1,0:T(8,128)}), f32[32,40,128]{2,1,0:T(8,128)S(1)}, u32[]{:S(2)}, u32[]{:S(2)}) async-start(f32[32,40,128]{2,1,0:T(8,128)} %merge.1), calls=%async_computation.2 | async-start | bytes 1310720 | tf_op jit(solution)/shard_map/all_to_all | solution.py:361

commit v7 on v4

--- a/solution.py
+++ b/solution.py
@@ -45,8 +45,20 @@
     return jnp.where(lane < 96, v0, s1), jnp.where(lane < 64, s1, s2), jnp.where(lane < 32, s2, s3)
 
 
-def fine_kernel(cols, part, dest, pos, me, a_ref, q_ref, x_ref, s_ref, q_mat, q_tr, acc, aq_ref):
-    step = pl.program_id(0)
+def fine_kernel(cols, part, dest, pos, me, a_hbm, q_hbm, x_hbm, a_ref, q_ref, x_ref, s_ref, q_mat, q_tr, acc, aq_ref, a_sem, q_sem, x_sem):
+    steps = R // ROWS_STEP
+
+    def fetch(step):
+        at = pl.ds(pl.multiple_of(step * ROWS_STEP, ROWS_STEP), ROWS_STEP)
+        return pltpu.make_async_copy(a_hbm.at[at], a_ref.at[at], a_sem.at[step])
+
+    get_q = pltpu.make_async_copy(q_hbm, q_ref, q_sem)
+    get_q.start()
+    for step in range(steps):
+        fetch(step).start()
+    s_ref[1] = jnp.zeros((KA * STRIDE, L), jnp.float32)
+    aq_ref[...] = jnp.zeros_like(aq_ref)
+    acc[...] = jnp.zeros_like(acc)
 
     def relayout(load, slot, triples):
         for j in triples:
@@ -54,28 +66,23 @@
             for v in range(4):
                 s_ref[slot, pl.ds(4 * j + v, 8, stride=STRIDE), :] = rows[v]
 
-    @pl.when(step == 0)
-    def _():
-        low = lane_iota(B) < B
-        unit = (lane_iota(B) == lax.broadcasted_iota(jnp.int32, (B, L), 0)).astype(jnp.bfloat16)
-        part_rows = NP * APART // R
-
-        def spread(g, triples):
-            both = slice(16 * (g // 2), 16 * (g // 2) + 16)
-            relayout(lambda lanes: q_ref[both, lanes][8 * (g % 2):8 * (g % 2) + 8], g % 2, triples)
-
-        s_ref[1] = jnp.zeros((KA * STRIDE, L), jnp.float32)
-        aq_ref[...] = jnp.zeros_like(aq_ref)
-        spread(0, range(B // 4))
-        for c in range(R):
-            g, k = divmod(c, 8)
-            if c + 8 < R:
-                spread(g + 1, range(3 * k, 3 * k + 3))
-            acc[c * part_rows:(c + 1) * part_rows, :] = jnp.zeros((part_rows, L), jnp.float32)
-            mat = jnp.where(low, s_ref[g % 2, k * STRIDE:k * STRIDE + B, :], 0.0).astype(jnp.bfloat16)
-            q_mat[c] = mat
-            turned = lax.dot_general(unit, mat, (((1,), (1,)), ((), ())), preferred_element_type=jnp.float32)
-            q_tr[c] = turned.astype(jnp.bfloat16)
+    low = lane_iota(B) < B
+    unit = (lane_iota(B) == lax.broadcasted_iota(jnp.int32, (B, L), 0)).astype(jnp.bfloat16)
+
+    def spread(g, triples):
+        both = slice(16 * (g // 2), 16 * (g // 2) + 16)
+        relayout(lambda lanes: q_ref[both, lanes][8 * (g % 2):8 * (g % 2) + 8], g % 2, triples)
+
+    get_q.wait()
+    spread(0, range(B // 4))
+    for c in range(R):
+        g, k = divmod(c, 8)
+        if c + 8 < R:
+            spread(g + 1, range(3 * k, 3 * k + 3))
+        mat = jnp.where(low, s_ref[g % 2, k * STRIDE:k * STRIDE + B, :], 0.0).astype(jnp.bfloat16)
+        q_mat[c] = mat
+        turned = lax.dot_general(unit, mat, (((1,), (1,)), ((), ())), preferred_element_type=jnp.float32)
+        q_tr[c] = turned.astype(jnp.bfloat16)
 
     def first(r, slot, k):
         row = jnp.maximum(r, 0)
@@ -92,66 +99,75 @@
             at = pl.ds(pl.multiple_of(p * APART, 8), B)
             acc[at, :] = acc[at, :] + term[:, L * m:L * (m + 1)]
 
-    last = pl.num_programs(0) - 1
-
-    @pl.when(step < last)
-    def _():
+    def rows_of_step(step, carry):
+        fetch(step).wait()
         for ii in range(ROWS_STEP):
             r = step * ROWS_STEP + ii
             for n in range(4):
                 first(r - 1, (ii + 1) % 2, 2 * n)
-                relayout(lambda lanes: a_ref[ii, :, lanes], ii % 2, range(6 * n, 6 * n + 6))
+                relayout(lambda lanes: a_ref[r, :, lanes], ii % 2, range(6 * n, 6 * n + 6))
                 second(r - 2, ii % 2, 2 * n)
-
-    @pl.when(step == last)
-    def _():
-        for n in range(4):
-            first(R - 1, (R - 1) % 2, 2 * n)
-            second(R - 2, R % 2, 2 * n)
-        for n in range(4):
-            second(R - 1, (R - 1) % 2, 2 * n)
-
-    @pl.when(step == last)
-    def _():
-        row = lax.broadcasted_iota(jnp.int32, (8, L), 0)
-        lane = lane_iota(8)
-        base = (me[0] % 8) * 16
-        codes = jnp.zeros((8, L), jnp.float32)
-        for p in range(NP):
-            codes = jnp.where((row == p // 16) & (lane == base + p % 16), (dest[p] * CELLS + pos[p]).astype(jnp.float32), codes)
-
-        def one(w, carry):
+        return carry
+
+    lax.fori_loop(0, steps, rows_of_step, 0)
+    for n in range(4):
+        first(R - 1, (R - 1) % 2, 2 * n)
+        second(R - 2, R % 2, 2 * n)
+    for n in range(4):
+        second(R - 1, (R - 1) % 2, 2 * n)
+
+    row = lax.broadcasted_iota(jnp.int32, (8, L), 0)
+    lane = lane_iota(8)
+    base = (me[0] % 8) * 16
+    codes = jnp.zeros((8, L), jnp.float32)
+    for p in range(NP):
+        codes = jnp.where((row == p // 16) & (lane == base + p % 16), (dest[p] * CELLS + pos[p]).astype(jnp.float32), codes)
+
+    def leave(c):
+        at = pl.ds(pl.multiple_of(c * 8, 8), 8)
+        return pltpu.make_async_copy(x_ref.at[at], x_hbm.at[at], x_sem.at[c])
+
+    def eight(c, carry):
+        for n in range(8):
+            w = c * 8 + n
             for a in range(PER):
                 rows = [acc[pl.ds(v * 16 * APART + w * PER + a, 16, stride=APART), :] for v in range(4)]
                 for u, piece in enumerate(pack_rows(*rows)):
                     for h in range(2):
                         x_ref[w, (2 * a + h) * 3 + u] = piece[8 * h:8 * h + 8]
             x_ref[w, TILES] = codes
-            return carry
-
-        lax.fori_loop(0, GY, one, 0, unroll=8)
+
+        @pl.when(c > 0)
+        def _():
+            leave(c - 1).start()
+
+        return carry
+
+    lax.fori_loop(0, GY // 8, eight, 0)
+    leave(GY // 8 - 1).start()
+    for c in range(GY // 8):
+        leave(c).wait()
 
 
 def fine(a_blocks, a_cols, q_blocks, part_of, part_dest, part_pos, me):
     return pl.pallas_call(
         fine_kernel,
         out_shape=jax.ShapeDtypeStruct((GY, TILES + 1, 8, L), jnp.float32),
-        grid_spec=pltpu.PrefetchScalarGridSpec(
-            num_scalar_prefetch=5,
-            grid=(R // ROWS_STEP + 1,),
-            in_specs=[
-                pl.BlockSpec((ROWS_STEP, KA, WIDTH), lambda g, *_: (jnp.minimum(g, R // ROWS_STEP - 1), 0, 0)),
-                pl.BlockSpec((R, WIDTH), lambda g, *_: (0, 0)),
-            ],
-            out_specs=pl.BlockSpec((GY, TILES + 1, 8, L), lambda g, *_: (0, 0, 0, 0)),
-            scratch_shapes=[
-                pltpu.VMEM((2, KA * STRIDE, L), jnp.float32),
-                pltpu.VMEM((R, B, L), jnp.bfloat16),
-                pltpu.VMEM((R, B, B), jnp.bfloat16),
-                pltpu.VMEM(((NP + 1) * APART, L), jnp.float32),
-                pltpu.VMEM((2, KA // 2, B, 2 * L), jnp.bfloat16),
-            ],
-        ),
+        in_specs=[pl.BlockSpec(memory_space=pltpu.SMEM)] * 5 + [pl.BlockSpec(memory_space=pltpu.HBM)] * 2,
+        out_specs=pl.BlockSpec(memory_space=pltpu.HBM),
+        scratch_shapes=[
+            pltpu.VMEM((R, KA, WIDTH), jnp.bfloat16),
+            pltpu.VMEM((R, WIDTH), jnp.bfloat16),
+            pltpu.VMEM((GY, TILES + 1, 8, L), jnp.float32),
+            pltpu.VMEM((2, KA * STRIDE, L), jnp.float32),
+            pltpu.VMEM((R, B, L), jnp.bfloat16),
+            pltpu.VMEM((R, B, B), jnp.bfloat16),
+            pltpu.VMEM(((NP + 1) * APART, L), jnp.float32),
+            pltpu.VMEM((2, KA // 2, B, 2 * L), jnp.bfloat16),
+            pltpu.SemaphoreType.DMA((R // ROWS_STEP,)),
+            pltpu.SemaphoreType.DMA,
+            pltpu.SemaphoreType.DMA((GY // 8,)),
+        ],
         compiler_params=pltpu.CompilerParams(vmem_limit_bytes=58 << 20),
         name="fine",
     )(a_cols.T, part_of.T, part_dest.reshape(NP), part_pos, me, a_blocks, q_blocks)

time: 103 us -> 104 us (level)
  no operation moved by 1% of the time
where the time goes in v7:
time: 104 us; the launch traced here: 103 us
  blocking collectives  42.2 us (41%)
  Pallas kernels  26.6 us (26%)
  waiting for transfers between devices  23.5 us (23%)
  starting transfers between devices  9.42 us (9%)
    all_to_all x1, blocking collectives, local(): lax.all_to_all(slices, 'gy', split_axis=0, concat_axis=0, tiled=True)  42.2 us
    pallas_call x1, Pallas kernels, fine(): pl.pallas_call(fine_kernel, out_shape=jax.ShapeDtypeStruct((GY, TILES + 1...  17.4 us
    all_to_all x1, waiting for transfers between devices, local(): lax.all_to_all(outgoing, 'gy', split_axis=0, concat_axis=0, tiled=True)  17.4 us
    ppermute x3, waiting for transfers between devices, local(): lax.ppermute(group, 'gx', [(i, (i + d) % GX) for i in range(GX)])  6.09 us
    ppermute x3, starting transfers between devices, local(): lax.ppermute(group, 'gx', [(i, (i + d) % GX) for i in range(GX)])  5.05 us
    all_to_all x1, starting transfers between devices, local(): lax.all_to_all(outgoing, 'gy', split_axis=0, concat_axis=0, tiled=True)  4.37 us
    pallas_call x1, Pallas kernels, close(): pl.pallas_call(close_kernel, out_shape=(out, out), scratch_shapes=[pltpu....  4.01 us
    pallas_call x1, Pallas kernels, cells_of(): pl.pallas_call(cells_kernel, out_shape=(jax.ShapeDtypeStruct((3 * PER, L...  4 us
  transfers between devices with their start and end apart: 4, of which 3 were waited for; matrix products, arithmetic and copies ran while one was open for 1% of the time, Pallas kernels for 0%

profile of v7, /device:TPU:1, one launch (start us, length us, event | category | flops | bytes accessed | tf_op | source)
XLA Modules:
  0.0 103.4 jit_solution(648031551710585777)
XLA Ops:
  0.6 17.4 %fine.1 = f32[32,19,8,128]{3,2,1,0:T(8,128)} custom-call(s32[8,64]{1,0:T(8,128)} %bitcast.10, s32[8,64]{1,0:T(8,128)} %bitcast.11, s32[64]{0:T(128)} %bitcast.12, s32[64]{0:T(128)} %pos.1, s32[1]{0:T(128)} %bitcast.3.me, bf16[64,8,9216]{2,1,0:T(8,128)(2,1)} %a_hbm.1, bf16[64,9216]{1,0:T(8,128)(2,1)} %q_hbm.1), custom_call_target="tpu_custom_call" | custom-call | tf_op jit(solution)/shard_map/fine/pallas_call | solution.py:153
  18.1 42.2 %all_to_all.10.y_ref = f32[32,19,8,128]{3,2,1,0:T(8,128)S(1)} all-to-all(f32[32,19,8,128]{3,2,1,0:T(8,128)} %fine.1), channel_id=1, replica_groups=mesh['gx'=4,'gy'=32] {'gy'}, dimensions={0} | all-to-all | bytes 4980736 | tf_op jit(solution)/shard_map/all_to_all | solution.py:341
  60.3 4.0 %cells.1 = (f32[9,136,128]{2,1,0:T(8,128)S(1)}, f32[9,32,128]{2,1,0:T(8,128)S(1)}) custom-call(f32[32,19,8,128]{3,2,1,0:T(8,128)S(1)} %all_to_all.10.y_ref), custom_call_target="tpu_custom_call" | custom-call | tf_op jit(solution)/shard_map/cells/pallas_call | solution.py:232
  64.3 0.0 copy-start
  64.3 1.4 %collective-permute-start = (f32[9,32,128]{2,1,0:T(8,128)S(1)}, f32[9,32,128]{2,1,0:T(8,128)S(1)}, u32[]{:S(2)}, u32[]{:S(2)}) collective-permute-start(f32[9,32,128]{2,1,0:T(8,128)S(1)} %get-tuple-element.5.t0), channel_id=1, source_target_pairs={{0,32},{32,64},{64,96},{96,0},{1,33},{33,65},{65,97},{97,1},{2,34}... | collective-permute-start | bytes 442376 | tf_op jit(solution)/shard_map/ppermute | solution.py:343
  65.7 2.6 %collective-permute-start.1 = (f32[9,32,128]{2,1,0:T(8,128)S(1)}, f32[9,32,128]{2,1,0:T(8,128)S(1)}, u32[]{:S(2)}, u32[]{:S(2)}) collective-permute-start(f32[9,32,128]{2,1,0:T(8,128)S(1)} %get-tuple-element.5.t0), channel_id=1, source_target_pairs={{0,64},{32,96},{64,0},{96,32},{1,65},{33,97},{65,1},{97,33},{2,66}... | collective-permute-start | bytes 442376 | tf_op jit(solution)/shard_map/ppermute | solution.py:343
  68.3 1.1 %collective-permute-start.2 = (f32[9,32,128]{2,1,0:T(8,128)S(1)}, f32[9,32,128]{2,1,0:T(8,128)S(1)}, u32[]{:S(2)}, u32[]{:S(2)}) collective-permute-start(f32[9,32,128]{2,1,0:T(8,128)S(1)} %get-tuple-element.5.t0), channel_id=1, source_target_pairs={{0,96},{32,0},{64,32},{96,64},{1,97},{33,1},{65,33},{97,65},{2,98}... | collective-permute-start | bytes 442376 | tf_op jit(solution)/shard_map/ppermute | solution.py:343
  69.3 1.8 %collective-permute-done.t1 = f32[9,32,128]{2,1,0:T(8,128)S(1)} collective-permute-done((f32[9,32,128]{2,1,0:T(8,128)S(1)}, f32[9,32,128]{2,1,0:T(8,128)S(1)}, u32[]{:S(2)}, u32[]{:S(2)}) %collective-permute-start) | collective-permute-done | bytes 147488 | tf_op jit(solution)/shard_map/ppermute | solution.py:343
  71.1 4.3 %collective-permute-done.1.t2 = f32[9,32,128]{2,1,0:T(8,128)S(1)} collective-permute-done((f32[9,32,128]{2,1,0:T(8,128)S(1)}, f32[9,32,128]{2,1,0:T(8,128)S(1)}, u32[]{:S(2)}, u32[]{:S(2)}) %collective-permute-start.1) | collective-permute-done | bytes 147488 | tf_op jit(solution)/shard_map/ppermute | solution.py:343
  75.4 0.0 collective-permute-done.2.t3
  75.4 1.1 %merge.1 = f32[32,9,8,128]{3,2,1,0:T(8,128)} custom-call(f32[9,136,128]{2,1,0:T(8,128)S(1)} %get-tuple-element.4.z_ref, f32[9,32,128]{2,1,0:T(8,128)S(1)} %get-tuple-element.5.t0, f32[9,32,128]{2,1,0:T(8,128)S(1)} %collective-permute-done.t1, f32[9,32,128]{2,1,0:T(8,128)S(1)} %collective-permute-done.1.t2, f32[9,32,128]{2,1,0:T(8,128)S(1)} %collective-permute-done.2.t3), custom_call_target="tpu_custom_call" | custom-call | tf_op jit(solution)/shard_map/merge/pallas_call | solution.py:259
  76.6 4.4 %all-to-all-start.1 = ((f32[32,9,8,128]{3,2,1,0:T(8,128)}), f32[32,9,8,128]{3,2,1,0:T(8,128)S(1)}, u32[]{:S(2)}, u32[]{:S(2)}) async-start(f32[32,9,8,128]{3,2,1,0:T(8,128)} %merge.1), calls=%async_computation.1 | async-start | bytes 2359296 | tf_op jit(solution)/shard_map/all_to_all | solution.py:345
  80.9 0.0 copy-done
  81.0 0.3 slice_reduce_fusion
  81.2 0.1 squeeze.10
  81.3 0.1 squeeze.9
  81.4 0.1 squeeze.11
  81.5 0.2 fusion
  81.7 0.2 fusion.1
  81.9 0.1 copy.9
  82.0 17.4 %all-to-all-done.1.w_ref = f32[32,9,8,128]{3,2,1,0:T(8,128)S(1)} async-done(((f32[32,9,8,128]{3,2,1,0:T(8,128)}), f32[32,9,8,128]{3,2,1,0:T(8,128)S(1)}, u32[]{:S(2)}, u32[]{:S(2)}) %all-to-all-start.1) | async-done | bytes 1179680 | tf_op jit(solution)/shard_map/all_to_all | solution.py:345
  99.4 4.0 %close.1 = (f32[2,8,9216]{2,1,0:T(8,128)}, f32[2,8,9216]{2,1,0:T(8,128)}) custom-call(f32[32,9,8,128]{3,2,1,0:T(8,128)S(1)} %all-to-all-done.1.w_ref, f32[128,128]{1,0:T(8,128)S(1)} %pad.4.h_ref, f32[96,96]{1,0:T(8,128)S(1)} %bitcast.9), custom_call_target="tpu_custom_call" | custom-call | tf_op jit(solution)/shard_map/close/pallas_call | solution.py:320
  (1 shorter events, 0.0 us)
Async XLA Ops:
  64.3 16.7 %copy-start = (f32[3,9216]{1,0:T(4,128)S(1)}, f32[3,9216]{1,0:T(4,128)}, u32[]{:S(2)}) copy-start(f32[3,9216]{1,0:T(4,128)} %param.13) | copy-start | bytes 331780
  64.3 6.8 %collective-permute-start = (f32[9,32,128]{2,1,0:T(8,128)S(1)}, f32[9,32,128]{2,1,0:T(8,128)S(1)}, u32[]{:S(2)}, u32[]{:S(2)}) collective-permute-start(f32[9,32,128]{2,1,0:T(8,128)S(1)} %get-tuple-element.5.t0), channel_id=1, source_target_pairs={{0,32},{32,64},{64,96},{96,0},{1,33},{33,65},{65,97},{97,1},{2,34}... | collective-permute-start | bytes 442376 | tf_op jit(solution)/shard_map/ppermute | solution.py:343
  65.7 9.8 %collective-permute-start.1 = (f32[9,32,128]{2,1,0:T(8,128)S(1)}, f32[9,32,128]{2,1,0:T(8,128)S(1)}, u32[]{:S(2)}, u32[]{:S(2)}) collective-permute-start(f32[9,32,128]{2,1,0:T(8,128)S(1)} %get-tuple-element.5.t0), channel_id=1, source_target_pairs={{0,64},{32,96},{64,0},{96,32},{1,65},{33,97},{65,1},{97,33},{2,66}... | collective-permute-start | bytes 442376 | tf_op jit(solution)/shard_map/ppermute | solution.py:343
  68.3 7.2 %collective-permute-start.2 = (f32[9,32,128]{2,1,0:T(8,128)S(1)}, f32[9,32,128]{2,1,0:T(8,128)S(1)}, u32[]{:S(2)}, u32[]{:S(2)}) collective-permute-start(f32[9,32,128]{2,1,0:T(8,128)S(1)} %get-tuple-element.5.t0), channel_id=1, source_target_pairs={{0,96},{32,0},{64,32},{96,64},{1,97},{33,1},{65,33},{97,65},{2,98}... | collective-permute-start | bytes 442376 | tf_op jit(solution)/shard_map/ppermute | solution.py:343
  76.6 22.8 %all-to-all-start.1 = ((f32[32,9,8,128]{3,2,1,0:T(8,128)}), f32[32,9,8,128]{3,2,1,0:T(8,128)S(1)}, u32[]{:S(2)}, u32[]{:S(2)}) async-start(f32[32,9,8,128]{3,2,1,0:T(8,128)} %merge.1), calls=%async_computation.1 | async-start | bytes 2359296 | tf_op jit(solution)/shard_map/all_to_all | solution.py:345

commit v8 on v7

--- a/solution.py
+++ b/solution.py
@@ -54,8 +54,6 @@
 
     get_q = pltpu.make_async_copy(q_hbm, q_ref, q_sem)
     get_q.start()
-    for step in range(steps):
-        fetch(step).start()
     s_ref[1] = jnp.zeros((KA * STRIDE, L), jnp.float32)
     aq_ref[...] = jnp.zeros_like(aq_ref)
     acc[...] = jnp.zeros_like(acc)
@@ -74,6 +72,8 @@
         relayout(lambda lanes: q_ref[both, lanes][8 * (g % 2):8 * (g % 2) + 8], g % 2, triples)
 
     get_q.wait()
+    for step in range(steps):
+        fetch(step).start()
     spread(0, range(B // 4))
     for c in range(R):
         g, k = divmod(c, 8)
@@ -265,19 +265,17 @@
     )(mine, *parts)
 
 
-def close_kernel(w_ref, h_ref, ht_ref, first_ref, last_ref, f_ref, hi_ref, lo_ref, r_ref, o_ref):
+def close_kernel(w_ref, h_ref, ht_ref, first_hbm, last_ref, f_ref, hi_ref, lo_ref, r_ref, o_ref, first_ref, first_sem):
     upper = lax.broadcasted_iota(jnp.int32, (8, L), 0) < 4
 
-    def spread(w, carry):
-        for a in range(PER):
+    def spread(n):
+        for k in range(4 * PER):
+            w, a = 4 * n + k // PER, k % PER
             rows = unpack_rows(*[w_ref[w, 3 * a + u] for u in range(3)])
             for v in range(4):
                 f_ref[v, pl.ds(pl.multiple_of((w * PER + a) * 8 + 8, 8), 8), :] = rows[v]
-        return carry
-
-    lax.fori_loop(0, GY, spread, 0, unroll=4)
-
-    def outputs(j, carry):
+
+    def outputs(j):
         lanes = [pl.ds(pl.multiple_of(384 * j + L * u, L), L) for u in range(3)]
         base = pl.multiple_of(32 * j + 8, 8)
         for half in range(RC):
@@ -290,9 +288,19 @@
             at = pl.ds(pl.multiple_of(64 * j + 16 * v, 16), 16)
             hi_ref[at, :] = hi
             lo_ref[at, :] = lo
-        return carry
-
-    lax.fori_loop(0, B // 4, outputs, 0, unroll=2)
+
+    def block(n, carry):
+        for j in range(PER):
+            outputs(PER * (n - 1) + j)
+        spread(n)
+        return carry
+
+    spread(0)
+    lax.fori_loop(1, GY // 4, block, 0)
+    for j in range(B // 4 - PER, B // 4):
+        outputs(j)
+    leave = pltpu.make_async_copy(first_ref, first_hbm, first_sem)
+    leave.start()
     h_hi, h_lo = split2(h_ref[...])
     t_hi, t_lo = split2(ht_ref[...])
     dot = functools.partial(jnp.dot, preferred_element_type=jnp.float32)
@@ -313,6 +321,7 @@
             rows = [o_ref[(4 * j + v) * GAP + 8 * half:(4 * j + v) * GAP + 8 * half + 8, :] for v in range(4)]
             for u, piece in enumerate(pack_rows(*rows)):
                 last_ref[half, :, 384 * j + L * u:384 * j + L * (u + 1)] = piece
+    leave.wait()
 
 
 def close(received, h, ht):
@@ -320,12 +329,15 @@
     return pl.pallas_call(
         close_kernel,
         out_shape=(out, out),
+        out_specs=(pl.BlockSpec(memory_space=pltpu.HBM), pl.BlockSpec(memory_space=pltpu.VMEM)),
         scratch_shapes=[
             pltpu.VMEM((4, B * 8 + 16, L), jnp.float32),
             pltpu.VMEM((B * CELLS, L), jnp.bfloat16),
             pltpu.VMEM((B * CELLS, L), jnp.bfloat16),
             pltpu.VMEM((B * GAP, L), jnp.float32),
             pltpu.VMEM((B * GAP, L), jnp.float32),
+            pltpu.VMEM((RC, SC, WIDTH), jnp.float32),
+            pltpu.SemaphoreType.DMA,
         ],
         compiler_params=pltpu.CompilerParams(vmem_limit_bytes=16 << 20),
         name="close",

time: 104 us -> 102 us (0.981)
  Pallas kernels: 26.6 us -> 24.5 us
    pallas_call x1, Pallas kernels: 17.4 us -> 15.5 us  [fine(): pl.pallas_call(fine_kernel, out_shape=jax.ShapeDtypeStruct((GY, TILES + 1...]
where the time goes in v8:
time: 102 us; the launch traced here: 101 us
  blocking collectives  42.2 us (41%)
  Pallas kernels  24.5 us (24%)
  waiting for transfers between devices  23.6 us (23%)
  starting transfers between devices  9.42 us (9%)
    all_to_all x1, blocking collectives, local(): lax.all_to_all(slices, 'gy', split_axis=0, concat_axis=0, tiled=True)  42.2 us
    all_to_all x1, waiting for transfers between devices, local(): lax.all_to_all(outgoing, 'gy', split_axis=0, concat_axis=0, tiled=True)  17.4 us
    pallas_call x1, Pallas kernels, fine(): pl.pallas_call(fine_kernel, out_shape=jax.ShapeDtypeStruct((GY, TILES + 1...  15.5 us
    ppermute x3, waiting for transfers between devices, local(): lax.ppermute(group, 'gx', [(i, (i + d) % GX) for i in range(GX)])  6.16 us
    ppermute x3, starting transfers between devices, local(): lax.ppermute(group, 'gx', [(i, (i + d) % GX) for i in range(GX)])  5.05 us
    all_to_all x1, starting transfers between devices, local(): lax.all_to_all(outgoing, 'gy', split_axis=0, concat_axis=0, tiled=True)  4.38 us
    pallas_call x1, Pallas kernels, cells_of(): pl.pallas_call(cells_kernel, out_shape=(jax.ShapeDtypeStruct((3 * PER, L...  4 us
    pallas_call x1, Pallas kernels, close(): pl.pallas_call(close_kernel, out_shape=(out, out), out_specs=(pl.BlockSpe...  3.86 us
  transfers between devices with their start and end apart: 4, of which 3 were waited for; matrix products, arithmetic and copies ran while one was open for 1% of the time, Pallas kernels for 0%

profile of v8, /device:TPU:1, one launch (start us, length us, event | category | flops | bytes accessed | tf_op | source)
XLA Modules:
  0.0 101.4 jit_solution(863929865172956009)
XLA Ops:
  0.6 15.5 %fine.1 = f32[32,19,8,128]{3,2,1,0:T(8,128)} custom-call(s32[8,64]{1,0:T(8,128)} %bitcast.10, s32[8,64]{1,0:T(8,128)} %bitcast.11, s32[64]{0:T(128)} %bitcast.12, s32[64]{0:T(128)} %pos.1, s32[1]{0:T(128)} %bitcast.3.me, bf16[64,8,9216]{2,1,0:T(8,128)(2,1)} %a_hbm.1, bf16[64,9216]{1,0:T(8,128)(2,1)} %q_hbm.1), custom_call_target="tpu_custom_call" | custom-call | tf_op jit(solution)/shard_map/fine/pallas_call | solution.py:153
  16.2 42.2 %all_to_all.10.y_ref = f32[32,19,8,128]{3,2,1,0:T(8,128)S(1)} all-to-all(f32[32,19,8,128]{3,2,1,0:T(8,128)} %fine.1), channel_id=1, replica_groups=mesh['gx'=4,'gy'=32] {'gy'}, dimensions={0} | all-to-all | bytes 4980736 | tf_op jit(solution)/shard_map/all_to_all | solution.py:353
  58.3 4.0 %cells.1 = (f32[9,136,128]{2,1,0:T(8,128)S(1)}, f32[9,32,128]{2,1,0:T(8,128)S(1)}) custom-call(f32[32,19,8,128]{3,2,1,0:T(8,128)S(1)} %all_to_all.10.y_ref), custom_call_target="tpu_custom_call" | custom-call | tf_op jit(solution)/shard_map/cells/pallas_call | solution.py:232
  62.3 0.0 copy-start
  62.3 1.4 %collective-permute-start = (f32[9,32,128]{2,1,0:T(8,128)S(1)}, f32[9,32,128]{2,1,0:T(8,128)S(1)}, u32[]{:S(2)}, u32[]{:S(2)}) collective-permute-start(f32[9,32,128]{2,1,0:T(8,128)S(1)} %get-tuple-element.5.t0), channel_id=1, source_target_pairs={{0,32},{32,64},{64,96},{96,0},{1,33},{33,65},{65,97},{97,1},{2,34}... | collective-permute-start | bytes 442376 | tf_op jit(solution)/shard_map/ppermute | solution.py:355
  63.7 2.6 %collective-permute-start.1 = (f32[9,32,128]{2,1,0:T(8,128)S(1)}, f32[9,32,128]{2,1,0:T(8,128)S(1)}, u32[]{:S(2)}, u32[]{:S(2)}) collective-permute-start(f32[9,32,128]{2,1,0:T(8,128)S(1)} %get-tuple-element.5.t0), channel_id=1, source_target_pairs={{0,64},{32,96},{64,0},{96,32},{1,65},{33,97},{65,1},{97,33},{2,66}... | collective-permute-start | bytes 442376 | tf_op jit(solution)/shard_map/ppermute | solution.py:355
  66.4 1.0 collective-permute-start.2
  67.4 1.9 %collective-permute-done.t1 = f32[9,32,128]{2,1,0:T(8,128)S(1)} collective-permute-done((f32[9,32,128]{2,1,0:T(8,128)S(1)}, f32[9,32,128]{2,1,0:T(8,128)S(1)}, u32[]{:S(2)}, u32[]{:S(2)}) %collective-permute-start) | collective-permute-done | bytes 147488 | tf_op jit(solution)/shard_map/ppermute | solution.py:355
  69.3 4.2 %collective-permute-done.1.t2 = f32[9,32,128]{2,1,0:T(8,128)S(1)} collective-permute-done((f32[9,32,128]{2,1,0:T(8,128)S(1)}, f32[9,32,128]{2,1,0:T(8,128)S(1)}, u32[]{:S(2)}, u32[]{:S(2)}) %collective-permute-start.1) | collective-permute-done | bytes 147488 | tf_op jit(solution)/shard_map/ppermute | solution.py:355
  73.6 0.0 collective-permute-done.2.t3
  73.6 1.1 %merge.1 = f32[32,9,8,128]{3,2,1,0:T(8,128)} custom-call(f32[9,136,128]{2,1,0:T(8,128)S(1)} %get-tuple-element.4.z_ref, f32[9,32,128]{2,1,0:T(8,128)S(1)} %get-tuple-element.5.t0, f32[9,32,128]{2,1,0:T(8,128)S(1)} %collective-permute-done.t1, f32[9,32,128]{2,1,0:T(8,128)S(1)} %collective-permute-done.1.t2, f32[9,32,128]{2,1,0:T(8,128)S(1)} %collective-permute-done.2.t3), custom_call_target="tpu_custom_call" | custom-call | tf_op jit(solution)/shard_map/merge/pallas_call | solution.py:259
  74.7 4.4 %all-to-all-start.1 = ((f32[32,9,8,128]{3,2,1,0:T(8,128)}), f32[32,9,8,128]{3,2,1,0:T(8,128)S(1)}, u32[]{:S(2)}, u32[]{:S(2)}) async-start(f32[32,9,8,128]{3,2,1,0:T(8,128)} %merge.1), calls=%async_computation.1 | async-start | bytes 2359296 | tf_op jit(solution)/shard_map/all_to_all | solution.py:357
  79.1 0.0 copy-done
  79.1 0.3 slice_reduce_fusion
  79.4 0.1 squeeze.10
  79.4 0.1 squeeze.9
  79.5 0.1 squeeze.11
  79.6 0.2 fusion
  79.8 0.2 fusion.1
  80.0 0.1 copy.9
  80.1 17.4 %all-to-all-done.1.w_ref = f32[32,9,8,128]{3,2,1,0:T(8,128)S(1)} async-done(((f32[32,9,8,128]{3,2,1,0:T(8,128)}), f32[32,9,8,128]{3,2,1,0:T(8,128)S(1)}, u32[]{:S(2)}, u32[]{:S(2)}) %all-to-all-start.1) | async-done | bytes 1179680 | tf_op jit(solution)/shard_map/all_to_all | solution.py:357
  97.5 3.9 %close.1 = (f32[2,8,9216]{2,1,0:T(8,128)}, f32[2,8,9216]{2,1,0:T(8,128)}) custom-call(f32[32,9,8,128]{3,2,1,0:T(8,128)S(1)} %all-to-all-done.1.w_ref, f32[128,128]{1,0:T(8,128)S(1)} %pad.4.h_ref, f32[96,96]{1,0:T(8,128)S(1)} %bitcast.9), custom_call_target="tpu_custom_call" | custom-call | tf_op jit(solution)/shard_map/close/pallas_call | solution.py:329
  (1 shorter events, 0.0 us)
Async XLA Ops:
  62.3 16.7 %copy-start = (f32[3,9216]{1,0:T(4,128)S(1)}, f32[3,9216]{1,0:T(4,128)}, u32[]{:S(2)}) copy-start(f32[3,9216]{1,0:T(4,128)} %param.13) | copy-start | bytes 331780
  62.3 7.0 %collective-permute-start = (f32[9,32,128]{2,1,0:T(8,128)S(1)}, f32[9,32,128]{2,1,0:T(8,128)S(1)}, u32[]{:S(2)}, u32[]{:S(2)}) collective-permute-start(f32[9,32,128]{2,1,0:T(8,128)S(1)} %get-tuple-element.5.t0), channel_id=1, source_target_pairs={{0,32},{32,64},{64,96},{96,0},{1,33},{33,65},{65,97},{97,1},{2,34}... | collective-permute-start | bytes 442376 | tf_op jit(solution)/shard_map/ppermute | solution.py:355
  63.7 9.8 %collective-permute-start.1 = (f32[9,32,128]{2,1,0:T(8,128)S(1)}, f32[9,32,128]{2,1,0:T(8,128)S(1)}, u32[]{:S(2)}, u32[]{:S(2)}) collective-permute-start(f32[9,32,128]{2,1,0:T(8,128)S(1)} %get-tuple-element.5.t0), channel_id=1, source_target_pairs={{0,64},{32,96},{64,0},{96,32},{1,65},{33,97},{65,1},{97,33},{2,66}... | collective-permute-start | bytes 442376 | tf_op jit(solution)/shard_map/ppermute | solution.py:355
  66.4 7.2 %collective-permute-start.2 = (f32[9,32,128]{2,1,0:T(8,128)S(1)}, f32[9,32,128]{2,1,0:T(8,128)S(1)}, u32[]{:S(2)}, u32[]{:S(2)}) collective-permute-start(f32[9,32,128]{2,1,0:T(8,128)S(1)} %get-tuple-element.5.t0), channel_id=1, source_target_pairs={{0,96},{32,0},{64,32},{96,64},{1,97},{33,1},{65,33},{97,65},{2,98}... | collective-permute-start | bytes 442376 | tf_op jit(solution)/shard_map/ppermute | solution.py:355
  74.7 22.8 %all-to-all-start.1 = ((f32[32,9,8,128]{3,2,1,0:T(8,128)}), f32[32,9,8,128]{3,2,1,0:T(8,128)S(1)}, u32[]{:S(2)}, u32[]{:S(2)}) async-start(f32[32,9,8,128]{3,2,1,0:T(8,128)} %merge.1), calls=%async_computation.1 | async-start | bytes 2359296 | tf_op jit(solution)/shard_map/all_to_all | solution.py:357

commit v9 on v8

--- a/solution.py
+++ b/solution.py
@@ -22,7 +22,6 @@
 ROWS_STEP = 16
 STRIDE = 100
 GAP = 20
-M_ROWS = 512
 APART = 104
 
 
@@ -178,9 +177,23 @@
     return hi, (x - hi.astype(jnp.float32)).astype(jnp.bfloat16)
 
 
-def cells_kernel(y_ref, z_ref, t_ref, x_ref, m_ref, g_ref):
-    wide = 2 * PER * L
-
+def code_names(tiles, per_row):
+    codes = jnp.concatenate([tiles[o][v:v + 1] for v in range(4) for o in range(4)], axis=1)
+    if per_row == 4 * CELLS:
+        whole = codes.astype(jnp.int32)
+        codes = ((whole // per_row) * CELLS + whole % CELLS).astype(jnp.float32)
+    return (codes - 256.0).astype(jnp.bfloat16)
+
+
+def table_of(rows, names):
+    row = lax.broadcasted_iota(jnp.int32, (rows, 1), 0)
+    quarter = rows // 4
+    want = ((row % quarter) // 4) * CELLS + 4 * (row // quarter) + row % 4
+    want = (want.astype(jnp.float32) - 256.0).astype(jnp.bfloat16)
+    return jnp.where(want == names, jnp.ones((), jnp.bfloat16), jnp.zeros((), jnp.bfloat16))
+
+
+def groups_kernel(y_ref, x_ref, codes_ref, t_ref, m_ref):
     def one(s, carry):
         for a in range(PER):
             halves = [unpack_rows(*[y_ref[s, (2 * a + h) * 3 + u] for u in range(3)]) for h in range(2)]
@@ -193,30 +206,33 @@
 
     lax.fori_loop(0, GY, one, 0, unroll=4)
     tiles = [functools.reduce(jnp.add, [y_ref[8 * o + s, TILES] for s in range(8)]) for o in range(4)]
-    codes = jnp.concatenate([tiles[o][v:v + 1] for v in range(4) for o in range(4)], axis=1) - 256.0
-    names = codes.astype(jnp.bfloat16)
-    row = lax.broadcasted_iota(jnp.int32, (4 * L, 1), 0)
-    want = ((row % L) // 4) * CELLS + 4 * (row // L) + row % 4
-    want = (want.astype(jnp.float32) - 256.0).astype(jnp.bfloat16)
-    one_bf, zero_bf = jnp.ones((), jnp.bfloat16), jnp.zeros((), jnp.bfloat16)
-    for c in range(0, 4 * L, M_ROWS):
-        table = jnp.where(want[c:c + M_ROWS] == names, one_bf, zero_bf)
-        sums = jnp.dot(table, x_ref[...], preferred_element_type=jnp.float32)
-        m_ref[c:c + M_ROWS, :] = sums[:, :wide // 2] + sums[:, wide // 2:]
-
-    def fold(g, carry):
-        for a in range(PER):
-            for v in range(4):
-                at = pl.multiple_of(L * v + 16 * g, 16)
-                both = m_ref[pl.ds(at, 8), L * a:L * (a + 1)] + m_ref[pl.ds(at + 8, 8), L * a:L * (a + 1)]
-                both = both + pltpu.roll(both, 4, 0)
-                g_ref[a, v, pl.ds(pl.multiple_of(4 * g, 4), 4), :] = both[0:4]
-        return carry
-
-    lax.fori_loop(0, GY // 4, fold, 0, unroll=2)
+    for o in range(4):
+        codes_ref[o] = tiles[o]
+    sums = jnp.dot(table_of(L, code_names(tiles, 4 * CELLS)), x_ref[...], preferred_element_type=jnp.float32)
+    m_ref[...] = sums[:, :PER * L] + sums[:, PER * L:]
     for a in range(PER):
-        for u, piece in enumerate(pack_rows(*[g_ref[a, v] for v in range(4)])):
+        for u, piece in enumerate(pack_rows(*[m_ref[32 * v:32 * v + 32, L * a:L * (a + 1)] for v in range(4)])):
             t_ref[3 * a + u] = piece
+
+
+def groups_of(received):
+    return pl.pallas_call(
+        groups_kernel,
+        out_shape=(
+            jax.ShapeDtypeStruct((4 * 512, 2 * PER * L), jnp.bfloat16),
+            jax.ShapeDtypeStruct((4, 8, L), jnp.float32),
+            jax.ShapeDtypeStruct((3 * PER, L // 4, L), jnp.float32),
+        ),
+        scratch_shapes=[pltpu.VMEM((L, PER * L), jnp.float32)],
+        compiler_params=pltpu.CompilerParams(vmem_limit_bytes=24 << 20),
+        name="groups",
+    )(received)
+
+
+def cells_kernel(x_ref, codes_ref, z_ref, m_ref):
+    names = code_names([codes_ref[o] for o in range(4)], CELLS)
+    sums = jnp.dot(table_of(4 * L, names), x_ref[...], preferred_element_type=jnp.float32)
+    m_ref[...] = sums[:, :PER * L] + sums[:, PER * L:]
 
     def pack(n, carry):
         for a in range(PER):
@@ -228,21 +244,15 @@
     lax.fori_loop(0, L // 16, pack, 0, unroll=2)
 
 
-def cells_of(received):
+def cells_of(x, codes):
     return pl.pallas_call(
         cells_kernel,
-        out_shape=(
-            jax.ShapeDtypeStruct((3 * PER, L + 8, L), jnp.float32),
-            jax.ShapeDtypeStruct((3 * PER, L // 4, L), jnp.float32),
-        ),
-        scratch_shapes=[
-            pltpu.VMEM((4 * 512, 2 * PER * L), jnp.bfloat16),
-            pltpu.VMEM((4 * L, PER * L), jnp.float32),
-            pltpu.VMEM((PER, 4, L // 4, L), jnp.float32),
-        ],
+        out_shape=jax.ShapeDtypeStruct((3 * PER, L + 8, L), jnp.float32),
+        scratch_shapes=[pltpu.VMEM((4 * L, PER * L), jnp.float32)],
         compiler_params=pltpu.CompilerParams(vmem_limit_bytes=24 << 20),
+        cost_estimate=pl.CostEstimate(flops=2 * 512 * 2048 * 768, bytes_accessed=4 << 20, transcendentals=0),
         name="cells",
-    )(received)
+    )(x, codes)
 
 
 def merge_kernel(z_ref, t0, t1, t2, t3, out_ref, s_ref):
@@ -351,8 +361,9 @@
     h = mm(mm(g[0], g[1]), g[2])
     slices = fine(a_blocks, a_cols, q_blocks, part_of, part_dest, part_pos, me)
     gathered = lax.all_to_all(slices, "gy", split_axis=0, concat_axis=0, tiled=True)
-    mine, group = cells_of(gathered)
+    x, codes, group = groups_of(gathered)
     others = [lax.ppermute(group, "gx", [(i, (i + d) % GX) for i in range(GX)]) for d in range(1, GX)]
+    mine = cells_of(x, codes)
     outgoing = merge(mine, [group] + others)
     back = lax.all_to_all(outgoing, "gy", split_axis=0, concat_axis=0, tiled=True)
     return close(back, jnp.pad(h, ((0, L - B), (0, L - B))), h.T)

time: 102 us -> 100 us (0.980)
  waiting for transfers between devices: 23.6 us -> 21.3 us
    ppermute x3, waiting for transfers between devices: 6.16 us -> 3.85 us  [local(): lax.ppermute(group, 'gx', [(i, (i + d) % GX) for i in range(GX)])]
    pallas_call x1 -> x2, Pallas kernels: 4 us -> 4.51 us  [the longest x1 2.29 us: groups_of(): pl.pallas_call(groups_kernel, out_shape=(jax.ShapeDtypeStruct((4 * 512, 2...]
  transfers between devices with their start and end apart: 4 -> 4, of which waited for: 3 -> 2; matrix products, arithmetic and copies ran while one was open for 1% -> 1% of each run, Pallas kernels for 0% -> 2%
where the time goes in v9:
time: 100 us; the launch traced here: 99.6 us
  blocking collectives  42.2 us (42%)
  Pallas kernels  25 us (25%)
  waiting for transfers between devices  21.3 us (21%)
  starting transfers between devices  9.43 us (9%)
    all_to_all x1, blocking collectives, local(): lax.all_to_all(slices, 'gy', split_axis=0, concat_axis=0, tiled=True)  42.2 us
    all_to_all x1, waiting for transfers between devices, local(): lax.all_to_all(outgoing, 'gy', split_axis=0, concat_axis=0, tiled=True)  17.4 us
    pallas_call x1, Pallas kernels, fine(): pl.pallas_call(fine_kernel, out_shape=jax.ShapeDtypeStruct((GY, TILES + 1...  15.5 us
    ppermute x3, starting transfers between devices, local(): lax.ppermute(group, 'gx', [(i, (i + d) % GX) for i in range(GX)])  5.06 us
    all_to_all x1, starting transfers between devices, local(): lax.all_to_all(outgoing, 'gy', split_axis=0, concat_axis=0, tiled=True)  4.37 us
    ppermute x3, waiting for transfers between devices, local(): lax.ppermute(group, 'gx', [(i, (i + d) % GX) for i in range(GX)])  3.85 us
    pallas_call x1, Pallas kernels, close(): pl.pallas_call(close_kernel, out_shape=(out, out), out_specs=(pl.BlockSpe...  3.85 us
    pallas_call x1, Pallas kernels, groups_of(): pl.pallas_call(groups_kernel, out_shape=(jax.ShapeDtypeStruct((4 * 512, 2...  2.29 us
  transfers between devices with their start and end apart: 4, of which 2 were waited for; matrix products, arithmetic and copies ran while one was open for 1% of the time, Pallas kernels for 2%

profile of v9, /device:TPU:1, one launch (start us, length us, event | category | flops | bytes accessed | tf_op | source)
XLA Modules:
  0.0 99.6 jit_solution(6344898320981894917)
XLA Ops:
  0.6 15.5 %fine.1 = f32[32,19,8,128]{3,2,1,0:T(8,128)} custom-call(s32[8,64]{1,0:T(8,128)} %bitcast.10, s32[8,64]{1,0:T(8,128)} %bitcast.11, s32[64]{0:T(128)} %bitcast.12, s32[64]{0:T(128)} %pos.1, s32[1]{0:T(128)} %bitcast.3.me, bf16[64,8,9216]{2,1,0:T(8,128)(2,1)} %a_hbm.1, bf16[64,9216]{1,0:T(8,128)(2,1)} %q_hbm.1), custom_call_target="tpu_custom_call" | custom-call | tf_op jit(solution)/shard_map/fine/pallas_call | solution.py:152
  16.2 42.2 %all_to_all.10.y_ref = f32[32,19,8,128]{3,2,1,0:T(8,128)S(1)} all-to-all(f32[32,19,8,128]{3,2,1,0:T(8,128)} %fine.1), channel_id=1, replica_groups=mesh['gx'=4,'gy'=32] {'gy'}, dimensions={0} | all-to-all | bytes 4980736 | tf_op jit(solution)/shard_map/all_to_all | solution.py:363
  58.3 2.3 %groups.1 = (bf16[2048,768]{1,0:T(8,128)(2,1)S(1)}, f32[4,8,128]{2,1,0:T(8,128)S(1)}, f32[9,32,128]{2,1,0:T(8,128)S(1)}) custom-call(f32[32,19,8,128]{3,2,1,0:T(8,128)S(1)} %all_to_all.10.y_ref), custom_call_target="tpu_custom_call" | custom-call | tf_op jit(solution)/shard_map/groups/pallas_call | solution.py:219
  60.6 1.4 %collective-permute-start = (f32[9,32,128]{2,1,0:T(8,128)S(1)}, f32[9,32,128]{2,1,0:T(8,128)S(1)}, u32[]{:S(2)}, u32[]{:S(2)}) collective-permute-start(f32[9,32,128]{2,1,0:T(8,128)S(1)} %get-tuple-element.7.t0), channel_id=1, source_target_pairs={{0,32},{32,64},{64,96},{96,0},{1,33},{33,65},{65,97},{97,1},{2,34}... | collective-permute-start | bytes 442376 | tf_op jit(solution)/shard_map/ppermute | solution.py:365
  62.0 2.6 %collective-permute-start.1 = (f32[9,32,128]{2,1,0:T(8,128)S(1)}, f32[9,32,128]{2,1,0:T(8,128)S(1)}, u32[]{:S(2)}, u32[]{:S(2)}) collective-permute-start(f32[9,32,128]{2,1,0:T(8,128)S(1)} %get-tuple-element.7.t0), channel_id=1, source_target_pairs={{0,64},{32,96},{64,0},{96,32},{1,65},{33,97},{65,1},{97,33},{2,66}... | collective-permute-start | bytes 442376 | tf_op jit(solution)/shard_map/ppermute | solution.py:365
  64.6 1.1 %collective-permute-start.2 = (f32[9,32,128]{2,1,0:T(8,128)S(1)}, f32[9,32,128]{2,1,0:T(8,128)S(1)}, u32[]{:S(2)}, u32[]{:S(2)}) collective-permute-start(f32[9,32,128]{2,1,0:T(8,128)S(1)} %get-tuple-element.7.t0), channel_id=1, source_target_pairs={{0,96},{32,0},{64,32},{96,64},{1,97},{33,1},{65,33},{97,65},{2,98}... | collective-permute-start | bytes 442376 | tf_op jit(solution)/shard_map/ppermute | solution.py:365
  65.7 2.2 %cells.1.z_ref = f32[9,136,128]{2,1,0:T(8,128)S(1)} custom-call(bf16[2048,768]{1,0:T(8,128)(2,1)S(1)} %get-tuple-element.5.x_ref, f32[4,8,128]{2,1,0:T(8,128)S(1)} %get-tuple-element.6.codes_ref), custom_call_target="tpu_custom_call" | custom-call | flops 1610612736 | bytes 4194304 | tf_op jit(solution)/shard_map/cells/pallas_call | solution.py:248
  67.9 0.0 copy-start
  67.9 0.0 collective-permute-done.t1
  67.9 3.8 %collective-permute-done.1.t2 = f32[9,32,128]{2,1,0:T(8,128)S(1)} collective-permute-done((f32[9,32,128]{2,1,0:T(8,128)S(1)}, f32[9,32,128]{2,1,0:T(8,128)S(1)}, u32[]{:S(2)}, u32[]{:S(2)}) %collective-permute-start.1) | collective-permute-done | bytes 147488 | tf_op jit(solution)/shard_map/ppermute | solution.py:365
  71.8 0.0 collective-permute-done.2.t3
  71.8 1.1 %merge.1 = f32[32,9,8,128]{3,2,1,0:T(8,128)} custom-call(f32[9,136,128]{2,1,0:T(8,128)S(1)} %cells.1.z_ref, f32[9,32,128]{2,1,0:T(8,128)S(1)} %get-tuple-element.7.t0, f32[9,32,128]{2,1,0:T(8,128)S(1)} %collective-permute-done.t1, f32[9,32,128]{2,1,0:T(8,128)S(1)} %collective-permute-done.1.t2, f32[9,32,128]{2,1,0:T(8,128)S(1)} %collective-permute-done.2.t3), custom_call_target="tpu_custom_call" | custom-call | tf_op jit(solution)/shard_map/merge/pallas_call | solution.py:269
  72.9 4.4 %all-to-all-start.1 = ((f32[32,9,8,128]{3,2,1,0:T(8,128)}), f32[32,9,8,128]{3,2,1,0:T(8,128)S(1)}, u32[]{:S(2)}, u32[]{:S(2)}) async-start(f32[32,9,8,128]{3,2,1,0:T(8,128)} %merge.1), calls=%async_computation.1 | async-start | bytes 2359296 | tf_op jit(solution)/shard_map/all_to_all | solution.py:368
  77.3 0.0 copy-done
  77.3 0.3 slice_reduce_fusion
  77.6 0.1 squeeze.10
  77.7 0.1 squeeze.9
  77.8 0.1 squeeze.11
  77.8 0.2 fusion
  78.0 0.2 fusion.1
  78.2 0.1 copy.9
  78.3 17.4 %all-to-all-done.1.w_ref = f32[32,9,8,128]{3,2,1,0:T(8,128)S(1)} async-done(((f32[32,9,8,128]{3,2,1,0:T(8,128)}), f32[32,9,8,128]{3,2,1,0:T(8,128)S(1)}, u32[]{:S(2)}, u32[]{:S(2)}) %all-to-all-start.1) | async-done | bytes 1179680 | tf_op jit(solution)/shard_map/all_to_all | solution.py:368
  95.8 3.9 %close.1 = (f32[2,8,9216]{2,1,0:T(8,128)}, f32[2,8,9216]{2,1,0:T(8,128)}) custom-call(f32[32,9,8,128]{3,2,1,0:T(8,128)S(1)} %all-to-all-done.1.w_ref, f32[128,128]{1,0:T(8,128)S(1)} %pad.4.h_ref, f32[96,96]{1,0:T(8,128)S(1)} %bitcast.9), custom_call_target="tpu_custom_call" | custom-call | tf_op jit(solution)/shard_map/close/pallas_call | solution.py:339
  (1 shorter events, 0.0 us)
Async XLA Ops:
  60.6 7.3 %collective-permute-start = (f32[9,32,128]{2,1,0:T(8,128)S(1)}, f32[9,32,128]{2,1,0:T(8,128)S(1)}, u32[]{:S(2)}, u32[]{:S(2)}) collective-permute-start(f32[9,32,128]{2,1,0:T(8,128)S(1)} %get-tuple-element.7.t0), channel_id=1, source_target_pairs={{0,32},{32,64},{64,96},{96,0},{1,33},{33,65},{65,97},{97,1},{2,34}... | collective-permute-start | bytes 442376 | tf_op jit(solution)/shard_map/ppermute | solution.py:365
  62.0 9.8 %collective-permute-start.1 = (f32[9,32,128]{2,1,0:T(8,128)S(1)}, f32[9,32,128]{2,1,0:T(8,128)S(1)}, u32[]{:S(2)}, u32[]{:S(2)}) collective-permute-start(f32[9,32,128]{2,1,0:T(8,128)S(1)} %get-tuple-element.7.t0), channel_id=1, source_target_pairs={{0,64},{32,96},{64,0},{96,32},{1,65},{33,97},{65,1},{97,33},{2,66}... | collective-permute-start | bytes 442376 | tf_op jit(solution)/shard_map/ppermute | solution.py:365
  64.6 7.2 %collective-permute-start.2 = (f32[9,32,128]{2,1,0:T(8,128)S(1)}, f32[9,32,128]{2,1,0:T(8,128)S(1)}, u32[]{:S(2)}, u32[]{:S(2)}) collective-permute-start(f32[9,32,128]{2,1,0:T(8,128)S(1)} %get-tuple-element.7.t0), channel_id=1, source_target_pairs={{0,96},{32,0},{64,32},{96,64},{1,97},{33,1},{65,33},{97,65},{2,98}... | collective-permute-start | bytes 442376 | tf_op jit(solution)/shard_map/ppermute | solution.py:365
  67.9 9.4 %copy-start = (f32[3,9216]{1,0:T(4,128)S(1)}, f32[3,9216]{1,0:T(4,128)}, u32[]{:S(2)}) copy-start(f32[3,9216]{1,0:T(4,128)} %param.13) | copy-start | bytes 331780
  72.9 22.8 %all-to-all-start.1 = ((f32[32,9,8,128]{3,2,1,0:T(8,128)}), f32[32,9,8,128]{3,2,1,0:T(8,128)S(1)}, u32[]{:S(2)}, u32[]{:S(2)}) async-start(f32[32,9,8,128]{3,2,1,0:T(8,128)} %merge.1), calls=%async_computation.1 | async-start | bytes 2359296 | tf_op jit(solution)/shard_map/all_to_all | solution.py:368

commit v10 on v9

--- a/solution.py
+++ b/solution.py
@@ -51,8 +51,12 @@
         at = pl.ds(pl.multiple_of(step * ROWS_STEP, ROWS_STEP), ROWS_STEP)
         return pltpu.make_async_copy(a_hbm.at[at], a_ref.at[at], a_sem.at[step])
 
-    get_q = pltpu.make_async_copy(q_hbm, q_ref, q_sem)
-    get_q.start()
+    def get_q(part):
+        at = slice(16 * part, 16 * part + 16)
+        return pltpu.make_async_copy(q_hbm.at[at], q_ref.at[at], q_sem.at[part])
+
+    for quarter in range(R // 16):
+        get_q(quarter).start()
     s_ref[1] = jnp.zeros((KA * STRIDE, L), jnp.float32)
     aq_ref[...] = jnp.zeros_like(aq_ref)
     acc[...] = jnp.zeros_like(acc)
@@ -70,12 +74,15 @@
         both = slice(16 * (g // 2), 16 * (g // 2) + 16)
         relayout(lambda lanes: q_ref[both, lanes][8 * (g % 2):8 * (g % 2) + 8], g % 2, triples)
 
-    get_q.wait()
-    for step in range(steps):
-        fetch(step).start()
+    get_q(0).wait()
     spread(0, range(B // 4))
     for c in range(R):
         g, k = divmod(c, 8)
+        if c % 16 == 8 and c + 8 < R:
+            get_q(c // 16 + 1).wait()
+            if c + 24 >= R:
+                for step in range(steps):
+                    fetch(step).start()
         if c + 8 < R:
             spread(g + 1, range(3 * k, 3 * k + 3))
         mat = jnp.where(low, s_ref[g % 2, k * STRIDE:k * STRIDE + B, :], 0.0).astype(jnp.bfloat16)
@@ -164,7 +171,7 @@
             pltpu.VMEM(((NP + 1) * APART, L), jnp.float32),
             pltpu.VMEM((2, KA // 2, B, 2 * L), jnp.bfloat16),
             pltpu.SemaphoreType.DMA((R // ROWS_STEP,)),
-            pltpu.SemaphoreType.DMA,
+            pltpu.SemaphoreType.DMA((R // 16,)),
             pltpu.SemaphoreType.DMA((GY // 8,)),
         ],
         compiler_params=pltpu.CompilerParams(vmem_limit_bytes=58 << 20),

time: 100 us -> 101 us (1.010)
  no operation moved by 1% of the time
where the time goes in v10:
time: 101 us
  blocking collectives  42.2 us (42%)
  Pallas kernels  26 us (26%)
  waiting for transfers between devices  21.3 us (21%)
  starting transfers between devices  9.44 us (9%)
    all_to_all x1, blocking collectives, local(): lax.all_to_all(slices, 'gy', split_axis=0, concat_axis=0, tiled=True)  42.2 us
    all_to_all x1, waiting for transfers between devices, local(): lax.all_to_all(outgoing, 'gy', split_axis=0, concat_axis=0, tiled=True)  17.4 us
    pallas_call x1, Pallas kernels, fine(): pl.pallas_call(fine_kernel, out_shape=jax.ShapeDtypeStruct((GY, TILES + 1...  16.5 us
    ppermute x3, starting transfers between devices, local(): lax.ppermute(group, 'gx', [(i, (i + d) % GX) for i in range(GX)])  5.06 us
    all_to_all x1, starting transfers between devices, local(): lax.all_to_all(outgoing, 'gy', split_axis=0, concat_axis=0, tiled=True)  4.37 us
    ppermute x3, waiting for transfers between devices, local(): lax.ppermute(group, 'gx', [(i, (i + d) % GX) for i in range(GX)])  3.87 us
    pallas_call x1, Pallas kernels, close(): pl.pallas_call(close_kernel, out_shape=(out, out), out_specs=(pl.BlockSpe...  3.86 us
    pallas_call x1, Pallas kernels, groups_of(): pl.pallas_call(groups_kernel, out_shape=(jax.ShapeDtypeStruct((4 * 512, 2...  2.29 us
  transfers between devices with their start and end apart: 4, of which 2 were waited for; matrix products, arithmetic and copies ran while one was open for 1% of the time, Pallas kernels for 2%

profile of v10, /device:TPU:1, one launch (start us, length us, event | category | flops | bytes accessed | tf_op | source)
XLA Modules:
  0.0 100.6 jit_solution(17327295636194854013)
XLA Ops:
  0.6 16.5 %fine.1 = f32[32,19,8,128]{3,2,1,0:T(8,128)} custom-call(s32[8,64]{1,0:T(8,128)} %bitcast.10, s32[8,64]{1,0:T(8,128)} %bitcast.11, s32[64]{0:T(128)} %bitcast.12, s32[64]{0:T(128)} %pos.1, s32[1]{0:T(128)} %bitcast.3.me, bf16[64,8,9216]{2,1,0:T(8,128)(2,1)} %a_hbm.1, bf16[64,9216]{1,0:T(8,128)(2,1)} %q_hbm.1), custom_call_target="tpu_custom_call" | custom-call | tf_op jit(solution)/shard_map/fine/pallas_call | solution.py:159
  17.1 42.2 %all_to_all.10.y_ref = f32[32,19,8,128]{3,2,1,0:T(8,128)S(1)} all-to-all(f32[32,19,8,128]{3,2,1,0:T(8,128)} %fine.1), channel_id=1, replica_groups=mesh['gx'=4,'gy'=32] {'gy'}, dimensions={0} | all-to-all | bytes 4980736 | tf_op jit(solution)/shard_map/all_to_all | solution.py:370
  59.3 2.3 %groups.1 = (bf16[2048,768]{1,0:T(8,128)(2,1)S(1)}, f32[4,8,128]{2,1,0:T(8,128)S(1)}, f32[9,32,128]{2,1,0:T(8,128)S(1)}) custom-call(f32[32,19,8,128]{3,2,1,0:T(8,128)S(1)} %all_to_all.10.y_ref), custom_call_target="tpu_custom_call" | custom-call | tf_op jit(solution)/shard_map/groups/pallas_call | solution.py:226
  61.6 1.4 %collective-permute-start = (f32[9,32,128]{2,1,0:T(8,128)S(1)}, f32[9,32,128]{2,1,0:T(8,128)S(1)}, u32[]{:S(2)}, u32[]{:S(2)}) collective-permute-start(f32[9,32,128]{2,1,0:T(8,128)S(1)} %get-tuple-element.7.t0), channel_id=1, source_target_pairs={{0,32},{32,64},{64,96},{96,0},{1,33},{33,65},{65,97},{97,1},{2,34}... | collective-permute-start | bytes 442376 | tf_op jit(solution)/shard_map/ppermute | solution.py:372
  62.9 2.6 %collective-permute-start.1 = (f32[9,32,128]{2,1,0:T(8,128)S(1)}, f32[9,32,128]{2,1,0:T(8,128)S(1)}, u32[]{:S(2)}, u32[]{:S(2)}) collective-permute-start(f32[9,32,128]{2,1,0:T(8,128)S(1)} %get-tuple-element.7.t0), channel_id=1, source_target_pairs={{0,64},{32,96},{64,0},{96,32},{1,65},{33,97},{65,1},{97,33},{2,66}... | collective-permute-start | bytes 442376 | tf_op jit(solution)/shard_map/ppermute | solution.py:372
  65.6 1.0 %collective-permute-start.2 = (f32[9,32,128]{2,1,0:T(8,128)S(1)}, f32[9,32,128]{2,1,0:T(8,128)S(1)}, u32[]{:S(2)}, u32[]{:S(2)}) collective-permute-start(f32[9,32,128]{2,1,0:T(8,128)S(1)} %get-tuple-element.7.t0), channel_id=1, source_target_pairs={{0,96},{32,0},{64,32},{96,64},{1,97},{33,1},{65,33},{97,65},{2,98}... | collective-permute-start | bytes 442376 | tf_op jit(solution)/shard_map/ppermute | solution.py:372
  66.6 2.2 %cells.1.z_ref = f32[9,136,128]{2,1,0:T(8,128)S(1)} custom-call(bf16[2048,768]{1,0:T(8,128)(2,1)S(1)} %get-tuple-element.5.x_ref, f32[4,8,128]{2,1,0:T(8,128)S(1)} %get-tuple-element.6.codes_ref), custom_call_target="tpu_custom_call" | custom-call | flops 1610612736 | bytes 4194304 | tf_op jit(solution)/shard_map/cells/pallas_call | solution.py:255
  68.9 0.0 copy-start
  68.9 0.0 collective-permute-done.t1
  68.9 3.9 %collective-permute-done.1.t2 = f32[9,32,128]{2,1,0:T(8,128)S(1)} collective-permute-done((f32[9,32,128]{2,1,0:T(8,128)S(1)}, f32[9,32,128]{2,1,0:T(8,128)S(1)}, u32[]{:S(2)}, u32[]{:S(2)}) %collective-permute-start.1) | collective-permute-done | bytes 147488 | tf_op jit(solution)/shard_map/ppermute | solution.py:372
  72.8 0.0 collective-permute-done.2.t3
  72.8 1.1 %merge.1 = f32[32,9,8,128]{3,2,1,0:T(8,128)} custom-call(f32[9,136,128]{2,1,0:T(8,128)S(1)} %cells.1.z_ref, f32[9,32,128]{2,1,0:T(8,128)S(1)} %get-tuple-element.7.t0, f32[9,32,128]{2,1,0:T(8,128)S(1)} %collective-permute-done.t1, f32[9,32,128]{2,1,0:T(8,128)S(1)} %collective-permute-done.1.t2, f32[9,32,128]{2,1,0:T(8,128)S(1)} %collective-permute-done.2.t3), custom_call_target="tpu_custom_call" | custom-call | tf_op jit(solution)/shard_map/merge/pallas_call | solution.py:276
  73.9 4.4 %all-to-all-start.1 = ((f32[32,9,8,128]{3,2,1,0:T(8,128)}), f32[32,9,8,128]{3,2,1,0:T(8,128)S(1)}, u32[]{:S(2)}, u32[]{:S(2)}) async-start(f32[32,9,8,128]{3,2,1,0:T(8,128)} %merge.1), calls=%async_computation.1 | async-start | bytes 2359296 | tf_op jit(solution)/shard_map/all_to_all | solution.py:375
  78.3 0.0 copy-done
  78.3 0.3 slice_reduce_fusion
  78.6 0.1 squeeze.10
  78.6 0.1 squeeze.9
  78.7 0.1 squeeze.11
  78.8 0.2 fusion
  79.0 0.2 fusion.1
  79.2 0.1 copy.9
  79.3 17.4 %all-to-all-done.1.w_ref = f32[32,9,8,128]{3,2,1,0:T(8,128)S(1)} async-done(((f32[32,9,8,128]{3,2,1,0:T(8,128)}), f32[32,9,8,128]{3,2,1,0:T(8,128)S(1)}, u32[]{:S(2)}, u32[]{:S(2)}) %all-to-all-start.1) | async-done | bytes 1179680 | tf_op jit(solution)/shard_map/all_to_all | solution.py:375
  96.7 3.9 %close.1 = (f32[2,8,9216]{2,1,0:T(8,128)}, f32[2,8,9216]{2,1,0:T(8,128)}) custom-call(f32[32,9,8,128]{3,2,1,0:T(8,128)S(1)} %all-to-all-done.1.w_ref, f32[128,128]{1,0:T(8,128)S(1)} %pad.4.h_ref, f32[96,96]{1,0:T(8,128)S(1)} %bitcast.9), custom_call_target="tpu_custom_call" | custom-call | tf_op jit(solution)/shard_map/close/pallas_call | solution.py:346
  (1 shorter events, 0.0 us)
Async XLA Ops:
  61.6 7.3 %collective-permute-start = (f32[9,32,128]{2,1,0:T(8,128)S(1)}, f32[9,32,128]{2,1,0:T(8,128)S(1)}, u32[]{:S(2)}, u32[]{:S(2)}) collective-permute-start(f32[9,32,128]{2,1,0:T(8,128)S(1)} %get-tuple-element.7.t0), channel_id=1, source_target_pairs={{0,32},{32,64},{64,96},{96,0},{1,33},{33,65},{65,97},{97,1},{2,34}... | collective-permute-start | bytes 442376 | tf_op jit(solution)/shard_map/ppermute | solution.py:372
  62.9 9.8 %collective-permute-start.1 = (f32[9,32,128]{2,1,0:T(8,128)S(1)}, f32[9,32,128]{2,1,0:T(8,128)S(1)}, u32[]{:S(2)}, u32[]{:S(2)}) collective-permute-start(f32[9,32,128]{2,1,0:T(8,128)S(1)} %get-tuple-element.7.t0), channel_id=1, source_target_pairs={{0,64},{32,96},{64,0},{96,32},{1,65},{33,97},{65,1},{97,33},{2,66}... | collective-permute-start | bytes 442376 | tf_op jit(solution)/shard_map/ppermute | solution.py:372
  65.6 7.2 %collective-permute-start.2 = (f32[9,32,128]{2,1,0:T(8,128)S(1)}, f32[9,32,128]{2,1,0:T(8,128)S(1)}, u32[]{:S(2)}, u32[]{:S(2)}) collective-permute-start(f32[9,32,128]{2,1,0:T(8,128)S(1)} %get-tuple-element.7.t0), channel_id=1, source_target_pairs={{0,96},{32,0},{64,32},{96,64},{1,97},{33,1},{65,33},{97,65},{2,98}... | collective-permute-start | bytes 442376 | tf_op jit(solution)/shard_map/ppermute | solution.py:372
  68.9 9.4 %copy-start = (f32[3,9216]{1,0:T(4,128)S(1)}, f32[3,9216]{1,0:T(4,128)}, u32[]{:S(2)}) copy-start(f32[3,9216]{1,0:T(4,128)} %param.13) | copy-start | bytes 331780
  73.9 22.8 %all-to-all-start.1 = ((f32[32,9,8,128]{3,2,1,0:T(8,128)}), f32[32,9,8,128]{3,2,1,0:T(8,128)S(1)}, u32[]{:S(2)}, u32[]{:S(2)}) async-start(f32[32,9,8,128]{3,2,1,0:T(8,128)} %merge.1), calls=%async_computation.1 | async-start | bytes 2359296 | tf_op jit(solution)/shard_map/all_to_all | solution.py:375
